TPU v7x, 256 devices: a whole 4x4x8 slice. The times are simulated.
256 devices in a mesh: rep: 4 (over y_hi, core), ep: 64 (over y_lo, z, x).
Axes of the slice: x: 4, y: 4 (y_hi: 2, y_lo: 2; y = y_hi * 2 + y_lo), z: 8, core: 2. Of those that a mesh axis runs over, the one named last changes fastest.
Arguments:
- tokens: bfloat16 [196608, 2048], P(('rep', 'ep')), may hold values from -6 to 6
- route: int32 [2, 131072], P(None, ('rep', 'ep')), may hold values from 0 to 767, as said below
- cotangent: bfloat16 [2, 131072, 512], P(None, ('rep', 'ep')), may hold values from -6 to 6
- weight: float32 [2, 2048, 512], P(None, 'ep'), may hold values from -0.125 to 0.125
- first_q: int32 [2, 2048, 512], P(None, 'ep'), may hold values from -127 to 127
- first_scale: float32 [2, 2048, 4], P(None, 'ep'), may hold values from 3e-05 to 6e-05
- second_q: int32 [2, 2048, 512], P(None, 'ep'), may hold values from 32 to 127
- second_scale: float32 [2, 2048, 4], P(None, 'ep'), may hold values from 3e-09 to 8e-09
Outputs:
- token_grad: bfloat16 [196608, 2048], P(('rep', 'ep'))
- step_dir: float32 [2, 2048, 512], P(None, 'ep')
- new_weight: float32 [2, 2048, 512], P(None, 'ep')
- next_gate: bfloat16 [2, 131072, 512], P(None, ('rep', 'ep'))
Inputs may be any that keep to these rules, and one draw needn't show every extreme that they name: `route`: for each hot expert, the 512 entries of one device's rows (aligned blocks of 512 along the last dimension) are distinct.
All inputs are finite; a program needn't handle non-finite values.
Results may differ from a plain program's by a relative error of at most 0.006.
Values may be sent and summed in bfloat16 or wider, within the bound.
No kernel may reach another device: no remote copies, remote signals or barrier semaphores. Data moves between devices by JAX's collectives and lax.ppermute only.
A program may use at most 128 MiB of HBM per device.

v0:
```python
import jax
import jax.numpy as jnp
from jax import lax
from jax.sharding import PartitionSpec as P

QBLOCK = 128


BETA_ONE = 0.9
BETA_TWO = 0.95
CORR_ONE = 1.0 - 0.9**10
CORR_TWO = 1.0 - 0.95**10
EPSILON = 1e-08
RATE = 0.002


def dequant(quant, scale):
    shaped = quant.astype(jnp.float32).reshape(quant.shape[0], quant.shape[1], -1, QBLOCK)
    return (shaped * scale[..., None]).reshape(quant.shape)


def adam_update(weight, grad, first_q, first_scale, second_q, second_scale):
    first = BETA_ONE * dequant(first_q, first_scale) + (1.0 - BETA_ONE) * grad
    second = BETA_TWO * dequant(second_q, second_scale) + (1.0 - BETA_TWO) * grad * grad
    step = first / CORR_ONE / (jnp.sqrt(second / CORR_TWO) + EPSILON)
    return (step, weight - RATE * step)


def on_device(tokens, route, cotangent, weight, first_q, first_scale, second_q, second_scale):
    n_rep = lax.axis_size("rep")
    n_ep = lax.axis_size("ep")
    experts, rows_here = route.shape
    width = tokens.shape[1]
    feature = cotangent.shape[2]
    total_rows = rows_here * n_rep * n_ep
    chosen = tokens[route]
    whole = lax.all_gather(weight.astype(jnp.bfloat16), "ep", axis=1, tiled=True)
    gate = jnp.einsum("erd,edf->erf", chosen, whole, preferred_element_type=jnp.float32)
    sig = jax.nn.sigmoid(gate)
    dgate = (cotangent.astype(jnp.float32) * sig * (1.0 + gate * (1.0 - sig))).astype(jnp.bfloat16)
    dx = jnp.einsum("erf,edf->erd", dgate, whole, preferred_element_type=jnp.float32)
    token_grad = (
        jnp.zeros(tokens.shape, jnp.float32)
        .at[route.reshape(-1)]
        .add(dx.reshape(-1, width))
        .astype(jnp.bfloat16)
    )
    owned = weight.shape[1]
    columns = chosen
    partial_value = lax.psum_scatter(
        jnp.einsum("erd,erf->def", columns, dgate, preferred_element_type=jnp.float32).reshape(
            lax.axis_size("ep") * owned, experts * feature
        ),
        "ep",
        scatter_dimension=0,
        tiled=True,
    )
    summed = lax.psum(partial_value, "rep")
    grad = summed.reshape(owned, experts, feature).transpose(1, 0, 2) / total_rows
    step_dir, new_weight = adam_update(weight, grad, first_q, first_scale, second_q, second_scale)
    columns = chosen
    next_gate = jnp.einsum(
        "erd,edf->erf",
        columns,
        lax.all_gather(new_weight.astype(jnp.bfloat16), "ep", axis=1, tiled=True),
        preferred_element_type=jnp.float32,
    ).astype(jnp.bfloat16)
    return (token_grad, step_dir, new_weight, next_gate)


def solution(mesh):
    in_specs = (
        P(("rep", "ep"), None),
        P(None, ("rep", "ep")),
        P(None, ("rep", "ep"), None),
        P(None, "ep", None),
        P(None, "ep", None),
        P(None, "ep", None),
        P(None, "ep", None),
        P(None, "ep", None),
    )
    out_specs = (
        P(("rep", "ep"), None),
        P(None, "ep", None),
        P(None, "ep", None),
        P(None, ("rep", "ep"), None),
    )
    return jax.shard_map(
        on_device, mesh=mesh, in_specs=in_specs, out_specs=out_specs, check_vma=False
    )
```

profile of v0, /device:TPU:16, one launch (start us, length us, event | category | flops | bytes accessed | tf_op | source)
XLA Modules:
  0.0 1029.5 jit_solution(10997818630183672256)
XLA Ops:
  7.2 0.0 copy-start
  7.2 0.0 all-gather.3.cloned.1.call-start
  7.2 1.7 convert_element_type.25
  8.9 0.0 all-gather.3.cloned.1.call-update
  8.9 0.0 reduce-scatter.2.cloned.1.call-start
  9.0 0.7 fusion.13
  9.7 0.0 copy-done
  9.7 6.0 gather_fusion
  15.7 301.1 %all-gather.3.cloned.1.call-done = bf16[2,2048,512]{2,1,0:T(8,128)(2,1)} async-done(((bf16[2,32,512]{2,1,0:T(8,128)(2,1)}), bf16[2,2048,512]{2,1,0:T(8,128)(2,1)}) %all-gather.3.cloned.1.call-update) | async-done | bytes 4194320 | tf_op jit(solution)/shard_map/all_gather | solution.py:37
  316.8 0.0 copy-start.1
  316.8 0.0 copy-start.6
  316.8 5.9 fusion.18
  322.8 0.0 copy-done.1
  322.8 0.0 copy-done.6
  322.8 0.0 copy-start.7
  322.8 6.0 fusion.2
  328.8 0.0 copy-done.7
  328.8 9.2 copy.17
  338.0 0.0 copy-start.4
  338.0 0.0 copy-start.5
  338.0 0.0 copy-start.2
  338.0 0.0 copy-start.3
  338.0 0.0 reduce-scatter.2.cloned.1.call-update
  338.1 0.0 all-reduce.2.cloned.1.call-start
  338.1 330.2 %reduce-scatter.2.cloned.1.call-done = f32[32,1024]{1,0:T(8,128)} async-done(((f32[2048,1024]{1,0:T(8,128)}), f32[32,1024]{1,0:T(8,128)}) %reduce-scatter.2.cloned.1.call-update) | async-done | bytes 131088 | tf_op jit(solution)/shard_map/reduce_scatter | solution.py:50
  668.3 0.0 all-reduce.2.cloned.1.call-update
  668.4 0.2 all-gather.5.cloned.1.call-start
  668.6 0.0 copy-done.4
  668.6 0.1 copy.19
  668.7 0.1 mul.90
  668.8 0.1 mul.91
  668.9 0.0 copy-done.5
  668.9 0.1 copy.15
  669.0 0.8 mul.81
  669.8 1.0 mul.82
  670.7 37.0 %all-reduce.2.cloned.1.call-done = f32[32,1024]{1,0:T(8,128)} async-done(((f32[32,1024]{1,0:T(8,128)}), f32[32,1024]{1,0:T(8,128)}) %all-reduce.2.cloned.1.call-update) | async-done | bytes 131088 | tf_op jit(solution)/shard_map/psum | solution.py:58
  707.8 0.9 broadcast_multiply_fusion
  708.7 0.0 copy-done.2
  708.7 1.8 fusion.16
  710.5 0.0 all-gather.5.cloned.1.call-update
  710.5 0.0 copy-done.3
  710.6 9.1 fusion.3
  719.6 17.7 %scatter_custom_fusion = f32[768,2048]{1,0:T(8,128)} fusion(s32[1024]{0:T(1024)S(1)} %bitcast.74, f32[1024,2048]{1,0:T(8,128)} %bitcast.75, f32[]{:T(128)} %constant.13.clone.1), kind=kCustom, calls=%fused_computation.2 | custom fusion | flops 2097152 | bytes 6291968 | tf_op jit(solution)/shard_map/scatter-add | solution.py:45
  737.3 4.9 convert_element_type.27
  742.3 273.9 %all-gather.5.cloned.1.call-done = bf16[2,2048,512]{2,1,0:T(8,128)(2,1)} async-done(((bf16[2,32,512]{2,1,0:T(8,128)(2,1)}), bf16[2,2048,512]{2,1,0:T(8,128)(2,1)}) %all-gather.5.cloned.1.call-update) | async-done | bytes 4194320 | tf_op jit(solution)/shard_map/all_gather | solution.py:65
  1016.2 6.8 convolution_convert_fusion
  (4 shorter events, 0.0 us)
Async XLA Ops:
  7.2 2.5 copy-start
  7.2 309.7 %all-gather.3.cloned.1.call-start = ((), (), s32[]{:S(2)}) async-start(), calls=%async_computation.1 | async-start | bytes 4259840 | tf_op jit(solution)/shard_map/all_gather | solution.py:37
  8.9 659.4 %reduce-scatter.2.cloned.1.call-start = ((), (), s32[]{:S(2)}) async-start(), calls=%async_computation.2 | async-start | bytes 8519680 | tf_op jit(solution)/shard_map/reduce_scatter | solution.py:50
  316.8 5.9 copy-start.1
  316.8 5.9 copy-start.6
  322.8 6.0 copy-start.7
  338.0 330.6 %copy-start.4 = (f32[2,32,4]{1,2,0:T(4,128)S(1)}, f32[2,32,4]{1,2,0:T(4,128)}, u32[]{:S(2)}) copy-start(f32[2,32,4]{1,2,0:T(4,128)} %param.15) | copy-start | bytes 3076
  338.0 330.9 %copy-start.5 = (f32[2,32,4]{1,2,0:T(4,128)S(1)}, f32[2,32,4]{1,2,0:T(4,128)}, u32[]{:S(2)}) copy-start(f32[2,32,4]{1,2,0:T(4,128)} %param.13) | copy-start | bytes 3076
  338.0 370.7 %copy-start.2 = (f32[2,32,512]{2,1,0:T(8,128)S(1)}, f32[2,32,512]{2,1,0:T(8,128)}, u32[]{:S(2)}) copy-start(f32[2,32,512]{2,1,0:T(8,128)} %param.11) | copy-start | bytes 393220
  338.0 372.5 %copy-start.3 = (s32[2,512]{1,0:T(2,128)S(1)}, s32[2,512]{1,0:T(2,128)}, u32[]{:S(2)}) copy-start(s32[2,512]{1,0:T(2,128)} %param.9) | copy-start | bytes 12292
  338.1 369.7 %all-reduce.2.cloned.1.call-start = ((), (), s32[]{:S(2)}) async-start(), calls=%async_computation.3 | async-start | bytes 262144 | tf_op jit(solution)/shard_map/psum | solution.py:58
  668.4 347.8 %all-gather.5.cloned.1.call-start = ((), (), s32[]{:S(2)}) async-start(), calls=%async_computation.4 | async-start | bytes 4259840 | tf_op jit(solution)/shard_map/all_gather | solution.py:65
Sparse Core Ops, SparseCore 0:
  10.4 306.4 all-gather.2
  338.2 330.1 reduce-scatter.1
  670.9 36.7 all-reduce.1
  710.6 305.4 all-gather.4
where the time goes:
time: 1030 us
  waiting for transfers between devices  942 us (91%)
  other arithmetic  27.8 us (3%)
  matrix products  27.8 us (3%)
  local copies, waits for them, and re-layouts  17.4 us (2%)
  between operations  13.9 us (1%)
    reduce_scatter x1, waiting for transfers between devices, on_device(): lax.psum_scatter(jnp.einsum('erd,erf->def', columns, dgate, preferred_ele...  330 us
    all_gather x1, waiting for transfers between devices, on_device(): lax.all_gather(weight.astype(jnp.bfloat16), 'ep', axis=1, tiled=True)  301 us
    all_gather x1, waiting for transfers between devices, on_device(): lax.all_gather(new_weight.astype(jnp.bfloat16), 'ep', axis=1, tiled=True)  274 us
    psum x1, waiting for transfers between devices, on_device(): summed = lax.psum(partial_value, 'rep')  37 us
  transfers between devices with their start and end apart: 4, of which 4 were waited for; matrix products, arithmetic and copies ran while one was open for 4% of the time, Pallas kernels for 0%

commit v1 on v0

v1 whole, which is shorter than its diff:
```python
import jax
import jax.numpy as jnp
from jax import lax
from jax.sharding import Mesh
from jax.sharding import PartitionSpec as P

QBLOCK = 128

BETA_ONE = 0.9
BETA_TWO = 0.95
CORR_ONE = 1.0 - 0.9**10
CORR_TWO = 1.0 - 0.95**10
EPSILON = 1e-08
RATE = 0.002

BF = jnp.bfloat16
F32 = jnp.float32
XY = ("yh", "yl", "x")


def dequant(quant, scale):
    shaped = quant.astype(F32).reshape(quant.shape[0], quant.shape[1], -1, QBLOCK)
    return (shaped * scale[..., None]).reshape(quant.shape)


def adam_update(weight, grad, first_q, first_scale, second_q, second_scale):
    first = BETA_ONE * dequant(first_q, first_scale) + (1.0 - BETA_ONE) * grad
    second = BETA_TWO * dequant(second_q, second_scale) + (1.0 - BETA_TWO) * grad * grad
    step = first / CORR_ONE / (jnp.sqrt(second / CORR_TWO) + EPSILON)
    return (step, weight - RATE * step)


def swap(value):
    return lax.ppermute(value, "core", [(0, 1), (1, 0)])


def spread(block, axes, count):
    return lax.all_to_all(
        jnp.broadcast_to(block[None], (count,) + block.shape), axes, 0, 0, tiled=True
    )


def gather_rows(block, n_z, n_xy):
    rows, feature = block.shape
    along_z = spread(block, "z", n_z)
    whole = spread(along_z, XY, n_xy)
    n_x = lax.axis_size("x")
    whole = whole.reshape(2, 2, n_x, n_z, rows, feature).transpose(1, 3, 2, 0, 4, 5)
    return whole.reshape(-1, feature)


def reduce_rows(grad, n_z, n_xy):
    depth, feature = grad.shape
    n_x = lax.axis_size("x")
    rows = depth // (n_z * n_xy)
    blocks = grad.reshape(2, n_z, n_x, 2, rows, feature).transpose(3, 0, 2, 1, 4, 5)
    blocks = blocks.reshape(n_xy, n_z, rows, feature)
    got = lax.all_to_all(blocks.astype(BF), XY, 0, 0, tiled=True)
    part = jnp.sum(got.astype(F32), axis=0).astype(BF)
    got = lax.all_to_all(part, "z", 0, 0, tiled=True)
    return jnp.sum(got.astype(F32), axis=0)


def pair(mine, other, core):
    return jnp.where(core == 0, jnp.stack([mine, other]), jnp.stack([other, mine]))


def on_device(tokens, route, cotangent, weight, first_q, first_scale, second_q, second_scale):
    n_rep = lax.axis_size("yh") * lax.axis_size("core")
    n_z = lax.axis_size("z")
    n_xy = lax.axis_size(XY)
    core = lax.axis_index("core")
    high = lax.axis_index("yh")
    rows_here = route.shape[1]
    total_rows = rows_here * n_rep * lax.axis_size("yl") * n_z * lax.axis_size("x")
    owned = weight.shape[1]
    half = owned // 2

    def mine_of(array):
        return lax.dynamic_index_in_dim(array, core, 0, keepdims=False)

    def other_of(array):
        return lax.dynamic_index_in_dim(array, 1 - core, 0, keepdims=False)

    def part_of(array):
        picked = mine_of(array)
        return lax.dynamic_slice_in_dim(picked, high * half, half, 0)

    weight_part = part_of(weight)
    whole = gather_rows(weight_part.astype(BF), n_z, n_xy)
    route_mine = mine_of(route)
    route_other = other_of(route)
    chosen = jnp.concatenate([tokens[route_mine], swap(tokens[route_other])], axis=0)
    cot = jnp.concatenate([mine_of(cotangent), swap(other_of(cotangent))], axis=0)

    gate = jnp.dot(chosen, whole, preferred_element_type=F32)
    sig = jax.nn.sigmoid(gate)
    dgate = (cot.astype(F32) * sig * (1.0 + gate * (1.0 - sig))).astype(BF)
    grad_all = jnp.einsum("rd,rf->df", chosen, dgate, preferred_element_type=F32)
    grad = reduce_rows(grad_all, n_z, n_xy) / total_rows

    def quarter(array):
        return part_of(array)[None]

    _, new_part = adam_update(
        weight_part[None], grad[None], quarter(first_q), quarter(first_scale), quarter(second_q), quarter(second_scale)
    )
    new_whole = gather_rows(new_part[0].astype(BF), n_z, n_xy)
    nexts = jnp.dot(chosen, new_whole, preferred_element_type=F32).astype(BF)
    next_gate = pair(nexts[:rows_here], swap(nexts[rows_here:]), core)

    both = pair(grad, swap(grad), core)
    far = lax.ppermute(both, "yh", [(0, 1), (1, 0)])
    both = jnp.where(
        high == 0, jnp.concatenate([both, far], axis=1), jnp.concatenate([far, both], axis=1)
    )
    step_dir, new_weight = adam_update(weight, both, first_q, first_scale, second_q, second_scale)

    places = jnp.arange(tokens.shape[0], dtype=jnp.int32)

    def at_tokens(routes, rows):
        hot = (places[:, None] == routes[None, :]).astype(BF)
        return jnp.dot(hot, rows, preferred_element_type=F32).astype(BF)

    other_whole = swap(whole)
    other_rows = swap(dgate[rows_here:])
    token_grad = (
        jnp.einsum("tf,df->td", at_tokens(route_mine, dgate[:rows_here]), whole, preferred_element_type=F32)
        + jnp.einsum("tf,df->td", at_tokens(route_other, other_rows), other_whole, preferred_element_type=F32)
    ).astype(BF)
    return (token_grad, step_dir, new_weight, next_gate)


def solution(mesh):
    split = Mesh(mesh.devices.reshape(2, 2, 2, 8, 4), ("yh", "core", "yl", "z", "x"))
    rep = ("yh", "core")
    ep = ("yl", "z", "x")
    every = rep + ep
    in_specs = (
        P(every, None),
        P(None, every),
        P(None, every, None),
        P(None, ep, None),
        P(None, ep, None),
        P(None, ep, None),
        P(None, ep, None),
        P(None, ep, None),
    )
    out_specs = (
        P(every, None),
        P(None, ep, None),
        P(None, ep, None),
        P(None, every, None),
    )
    return jax.shard_map(
        on_device, mesh=split, in_specs=in_specs, out_specs=out_specs, check_vma=False
    )
```

time: 1030 us -> 192 us (0.19)
  the two profiles are of different devices: /device:TPU:16 before, /device:TPU:1 now
where the time goes in v1:
time: 192 us; the launch traced here: 191 us
  blocking collectives  58.2 us (30%)
  starting transfers between devices  34.6 us (18%)
  local copies, waits for them, and re-layouts  30.7 us (16%)
  matrix products  28.9 us (15%)
  waiting for transfers between devices  27.1 us (14%)
  other arithmetic  10.8 us (6%)
    all_to_all x1, blocking collectives, reduce_rows(): got = lax.all_to_all(blocks.astype(BF), XY, 0, 0, tiled=True)  33 us
    all_to_all x2, blocking collectives, spread(): lax.all_to_all(jnp.broadcast_to(block[None], (count,) + block.shape), axe...  25.2 us
    all_to_all x2, waiting for transfers between devices, spread(): lax.all_to_all(jnp.broadcast_to(block[None], (count,) + block.shape), axe...  19.6 us
    ppermute x6, starting transfers between devices, swap(): return lax.ppermute(value, 'core', [(0, 1), (1, 0)])  17 us
    all_to_all x2, starting transfers between devices, spread(): lax.all_to_all(jnp.broadcast_to(block[None], (count,) + block.shape), axe...  11.2 us
    dot_general x1, matrix products, on_device(): jnp.einsum('tf,df->td', at_tokens(route_other, other_rows), other_whole,...  7.46 us
    all_to_all x1, waiting for transfers between devices, reduce_rows(): got = lax.all_to_all(part, 'z', 0, 0, tiled=True)  7.46 us
    unnamed x19, local copies, waits for them, and re-layouts  6.96 us
  transfers between devices with their start and end apart: 10, of which 3 were waited for; matrix products, arithmetic and copies ran while one was open for 23% of the time, Pallas kernels for 0%

profile of v1, /device:TPU:1, one launch (start us, length us, event | category | flops | bytes accessed | tf_op | source)
XLA Modules:
  0.0 191.0 jit_solution(1792224069830748383)
XLA Ops:
  0.7 0.9 compare_select_fusion
  1.5 1.0 copy-done
  2.6 3.3 %gather_fusion.1 = bf16[512,2048]{1,0:T(8,128)(2,1)} fusion(bf16[768,2048]{1,0:T(8,128)(2,1)S(1)} %copy-done, s32[1024]{0:T(1024)S(1)} %get-tuple-element.20), kind=kCustom, calls=%fused_computation.1 | custom fusion | bytes 4196352 | tf_op jit(solution)/shard_map/gather | solution.py:93
  5.9 3.2 %collective-permute-start.1 = (bf16[512,2048]{1,0:T(8,128)(2,1)}, bf16[512,2048]{1,0:T(8,128)(2,1)}, u32[]{:S(2)}, u32[]{:S(2)}) collective-permute-start(bf16[512,2048]{1,0:T(8,128)(2,1)} %gather_fusion.1), channel_id=1, source_target_pairs={{0,64},{64,0},{1,65},{65,1},{2,66},{66,2},{3,67},{67,3},{4,68},{68... | collective-permute-start | bytes 6291464 | tf_op jit(solution)/shard_map/ppermute | solution.py:34
  9.1 0.8 fusion.25
  9.9 14.8 %all_to_all.30 = bf16[8,16,512]{2,1,0:T(8,128)(2,1)S(1)} all-to-all(bf16[8,16,512]{2,1,0:T(8,128)(2,1)S(1)} %broadcast_in_dim.13), channel_id=1, replica_groups=mesh['yh'=2,'core'=2,'yl'=2,'z'=8,'x'=4] {'z'}, dimensions={0} | all-to-all | bytes 262144 | tf_op jit(solution)/shard_map/all_to_all | solution.py:38
  24.7 1.6 broadcast_in_dim.14
  26.3 6.8 %all-to-all-start.1 = ((bf16[16,8,16,512]{3,2,1,0:T(8,128)(2,1)}), bf16[16,8,16,512]{3,2,1,0:T(8,128)(2,1)}, u32[]{:S(2)}, u32[]{:S(2)}) async-start(bf16[16,8,16,512]{3,2,1,0:T(8,128)(2,1)} %broadcast_in_dim.14), calls=%async_computation.1 | async-start | bytes 4194304 | tf_op jit(solution)/shard_map/all_to_all | solution.py:38
  33.0 2.3 %dynamic-slice_bitcast_fusion.1 = (bf16[512,512]{1,0:T(8,128)(2,1)}, bf16[512,512]{1,0:T(8,128)(2,1)}) fusion(bf16[2,512,512]{2,1,0:T(8,128)(2,1)} %param.10, s32[]{:T(128)S(6)} %select_n.73, s32[]{:T(128)S(6)} %select_n.74), kind=kLoop, calls=%fused_computation.19 | loop fusion | bytes 2097160 | tf_op jit(solution)/shard_map/jit(dynamic_index_in_dim)/squeeze | solution.py:80
  35.3 1.8 collective-permute-start
  37.1 3.3 %gather_fusion = bf16[512,2048]{1,0:T(8,128)(2,1)} fusion(bf16[768,2048]{1,0:T(8,128)(2,1)S(1)} %copy-done, s32[1024]{0:T(1024)S(1)} %get-tuple-element.21), kind=kCustom, calls=%fused_computation | custom fusion | bytes 4196352 | tf_op jit(solution)/shard_map/gather | solution.py:93
  40.4 3.2 %constant_dynamic-update-slice_fusion.1 = bf16[1024,2048]{1,0:T(8,128)(2,1)} fusion(bf16[512,2048]{1,0:T(8,128)(2,1)} %gather_fusion), kind=kLoop, calls=%fused_computation.50 | loop fusion | bytes 4194304
  43.6 3.2 %constant_dynamic-update-slice_fusion = bf16[1024,2048]{1,0:T(8,128)(2,1)} fusion(bf16[1024,2048]{1,0:T(8,128)(2,1)} %constant_dynamic-update-slice_fusion.1, bf16[512,2048]{1,0:T(8,128)(2,1)} %collective-permute-done.1), kind=kLoop, calls=%fused_computation.49 | loop fusion | bytes 4194304 | tf_op jit(solution)/shard_map/concatenate | solution.py:93
  46.9 14.1 %all-to-all-done.1 = bf16[16,8,16,512]{3,2,1,0:T(8,128)(2,1)} async-done(((bf16[16,8,16,512]{3,2,1,0:T(8,128)(2,1)}), bf16[16,8,16,512]{3,2,1,0:T(8,128)(2,1)}, u32[]{:S(2)}, u32[]{:S(2)}) %all-to-all-start.1) | async-done | bytes 2097184 | tf_op jit(solution)/shard_map/all_to_all | solution.py:38
  60.9 1.8 copy.28
  62.8 1.3 copy-done.1
  64.1 5.4 %multiply_convert_fusion = bf16[1024,512]{1,0:T(8,128)(2,1)S(1)} fusion(bf16[512,512]{1,0:T(8,128)(2,1)} %collective-permute-done, bf16[512,512]{1,0:T(8,128)(2,1)S(1)} %copy-done.2, bf16[1024,2048]{1,0:T(8,128)(2,1)} %constant_dynamic-update-slice_fusion, bf16[2048,512]{1,0:T(8,128)(2,1)S(1)} %bitcast.79), kind=kOutput, calls=%fused_computation.4 | convolution fusion | flops 2154299392 | bytes 8388608 | tf_op jit(solution)/shard_map/dot_general | solution.py:96
  69.5 4.9 %convolution_convert_fusion = bf16[2048,512]{1,0:T(8,128)(2,1)S(1)} fusion(bf16[1024,2048]{1,0:T(8,128)(2,1)} %constant_dynamic-update-slice_fusion, bf16[1024,512]{1,0:T(8,128)(2,1)S(1)} %multiply_convert_fusion), kind=kOutput, calls=%fused_computation.3 | convolution fusion | flops 2148532224 | bytes 7340032 | tf_op jit(solution)/shard_map/rd,rf->df/dot_general | solution.py:99
  74.4 0.2 copy.30
  74.7 33.0 %all_to_all.31 = bf16[16,8,16,512]{3,2,1,0:T(8,128)(2,1)} all-to-all(bf16[16,8,16,512]{3,2,1,0:T(8,128)(2,1)S(1)} %bitcast.78), channel_id=1, replica_groups=mesh['yh'=2,'core'=2,'yl'=2,'z'=8,'x'=4] {'yh','yl','x'}, dimensions={0} | all-to-all | bytes 4194304 | tf_op jit(solution)/shard_map/all_to_all | solution.py:58
  107.7 2.7 %reduce_sum.21 = bf16[8,16,512]{2,1,0:T(8,128)(2,1)} reduce(bf16[16,8,16,512]{3,2,1,0:T(8,128)(2,1)} %all_to_all.31, bf16[]{:T(256)} %constant.161.clone.1), dimensions={0}, to_apply=%region_0.1 | reduce | flops 983040 | bytes 2228226 | tf_op jit(solution)/shard_map/reduce_sum | solution.py:59
  110.3 3.4 %all-to-all-start.3 = ((bf16[8,16,512]{2,1,0:T(8,128)(2,1)}), bf16[8,16,512]{2,1,0:T(8,128)(2,1)S(1)}, u32[]{:S(2)}, u32[]{:S(2)}) async-start(bf16[8,16,512]{2,1,0:T(8,128)(2,1)} %reduce_sum.21), calls=%async_computation.3 | async-start | bytes 262144 | tf_op jit(solution)/shard_map/all_to_all | solution.py:60
  114.2 7.5 %all-to-all-done.3 = bf16[8,16,512]{2,1,0:T(8,128)(2,1)S(1)} async-done(((bf16[8,16,512]{2,1,0:T(8,128)(2,1)}), bf16[8,16,512]{2,1,0:T(8,128)(2,1)S(1)}, u32[]{:S(2)}, u32[]{:S(2)}) %all-to-all-start.3) | async-done | bytes 131104 | tf_op jit(solution)/shard_map/all_to_all | solution.py:60
  121.7 0.6 copy-done.3
  122.3 0.9 fusion.26
  123.2 10.4 %all_to_all.32 = bf16[8,16,512]{2,1,0:T(8,128)(2,1)S(1)} all-to-all(bf16[8,16,512]{2,1,0:T(8,128)(2,1)S(1)} %broadcast_in_dim.16), channel_id=1, replica_groups=mesh['yh'=2,'core'=2,'yl'=2,'z'=8,'x'=4] {'z'}, dimensions={0} | all-to-all | bytes 262144 | tf_op jit(solution)/shard_map/all_to_all | solution.py:38
  133.6 1.6 broadcast_in_dim.17
  135.2 4.4 %all-to-all-start.5 = ((bf16[16,8,16,512]{3,2,1,0:T(8,128)(2,1)}), bf16[16,8,16,512]{3,2,1,0:T(8,128)(2,1)}, u32[]{:S(2)}, u32[]{:S(2)}) async-start(bf16[16,8,16,512]{3,2,1,0:T(8,128)(2,1)} %broadcast_in_dim.17), calls=%async_computation.5 | async-start | bytes 4194304 | tf_op jit(solution)/shard_map/all_to_all | solution.py:38
  139.7 4.4 %collective-permute-start.3 = (bf16[2048,512]{1,0:T(8,128)(2,1)}, bf16[2048,512]{1,0:T(8,128)(2,1)}, u32[]{:S(2)}, u32[]{:S(2)}) collective-permute-start(bf16[2048,512]{1,0:T(8,128)(2,1)} %bitcast.80), channel_id=1, source_target_pairs={{0,64},{64,0},{1,65},{65,1},{2,66},{66,2},{3,67},{67,3},{4,68},{68... | collective-permute-start | bytes 6291464 | tf_op jit(solution)/shard_map/ppermute | solution.py:34
  144.1 0.1 copy.29
  144.1 0.1 copy.31
  144.2 0.1 mul.176
  144.4 0.1 mul.183
  144.6 0.8 fusion.29
  145.4 6.6 %fusion.4 = f32[768,2048]{1,0:T(8,128)} fusion(bf16[2048,512]{1,0:T(8,128)(2,1)} %bitcast.81, s32[512]{0:T(512)S(1)} %bitcast.88, bf16[1024,512]{1,0:T(8,128)(2,1)} %copy-done.4), kind=kOutput, calls=%fused_computation.12 | convolution fusion | flops 2014052352 | bytes 8914944 | tf_op jit(solution)/shard_map/tf,df->td/dot_general | solution.py:128
  152.1 1.9 slice.21
  153.9 0.5 collective-permute-start.2
  154.4 0.6 copy-done.5
  155.0 0.8 maximum_select_fusion.2
  155.9 3.0 %collective-permute-start.5 = (f32[2,16,512]{2,1,0:T(8,128)S(1)}, f32[2,16,512]{2,1,0:T(8,128)S(1)}, u32[]{:S(2)}, u32[]{:S(2)}) collective-permute-start(f32[2,16,512]{2,1,0:T(8,128)S(1)} %maximum_select_fusion.2), channel_id=1, source_target_pairs={{0,128},{128,0},{1,129},{129,1},{2,130},{130,2},{3,131},{131,3},{4... | collective-permute-start | bytes 196616 | tf_op jit(solution)/shard_map/ppermute | solution.py:113
  158.9 5.6 %all-to-all-done.5 = bf16[16,8,16,512]{3,2,1,0:T(8,128)(2,1)} async-done(((bf16[16,8,16,512]{3,2,1,0:T(8,128)(2,1)}), bf16[16,8,16,512]{3,2,1,0:T(8,128)(2,1)}, u32[]{:S(2)}, u32[]{:S(2)}) %all-to-all-start.5) | async-done | bytes 2097184 | tf_op jit(solution)/shard_map/all_to_all | solution.py:38
  164.4 1.8 copy.34
  166.2 4.5 %convolution_convert_fusion.1 = bf16[1024,512]{1,0:T(8,128)(2,1)S(1)} fusion(bf16[1024,2048]{1,0:T(8,128)(2,1)} %constant_dynamic-update-slice_fusion, bf16[2048,512]{1,0:T(8,128)(2,1)S(1)} %bitcast.82), kind=kOutput, calls=%fused_computation.9 | convolution fusion | flops 2148007936 | bytes 7340032 | tf_op jit(solution)/shard_map/dot_general | solution.py:109
  170.7 1.0 slice_bitcast_fusion
  171.8 7.1 %collective-permute-start.6 = (bf16[512,512]{1,0:T(8,128)(2,1)}, bf16[512,512]{1,0:T(8,128)(2,1)}, u32[]{:S(2)}, u32[]{:S(2)}) collective-permute-start(bf16[512,512]{1,0:T(8,128)(2,1)} %get-tuple-element.11), channel_id=1, source_target_pairs={{0,64},{64,0},{1,65},{65,1},{2,66},{66,2},{3,67},{67,3},{4,68},{68... | collective-permute-start | bytes 1572872 | tf_op jit(solution)/shard_map/ppermute | solution.py:34
  178.9 7.5 %add_convert_fusion = bf16[768,2048]{1,0:T(8,128)(2,1)} fusion(f32[768,2048]{1,0:T(8,128)} %fusion.4, bf16[2048,512]{1,0:T(8,128)(2,1)} %collective-permute-done.3, bf16[512,512]{1,0:T(8,128)(2,1)} %collective-permute-done.2, s32[512]{0:T(512)S(1)} %bitcast.87), kind=kOutput, calls=%fused_computation.2 | convolution fusion | flops 2017198080 | bytes 12060672 | tf_op jit(solution)/shard_map/tf,df->td/dot_general | solution.py:129
  186.3 1.9 multiply_subtract_fusion
  188.2 2.8 %maximum_select_fusion = bf16[2,512,512]{2,1,0:T(8,128)(2,1)} fusion(bf16[1,512,512]{2,1,0:T(8,128)(2,1)} %bitcast.26, bf16[1,512,512]{2,1,0:T(8,128)(2,1)} %get-tuple-element.10, pred[]{:T(512)S(6)} %eq.46), kind=kLoop, calls=%fused_computation.13 | loop fusion | flops 1572864 | bytes 2097153 | tf_op jit(solution)/shard_map/jit(_where)/select_n | solution.py:65
  (33 shorter events, 0.7 us)
Async XLA Ops:
  0.6 1.9 %copy-start = (bf16[768,2048]{1,0:T(8,128)(2,1)S(1)}, bf16[768,2048]{1,0:T(8,128)(2,1)}, u32[]{:S(2)}) copy-start(bf16[768,2048]{1,0:T(8,128)(2,1)} %param.8) | copy-start | bytes 9437188
  5.9 37.8 %collective-permute-start.1 = (bf16[512,2048]{1,0:T(8,128)(2,1)}, bf16[512,2048]{1,0:T(8,128)(2,1)}, u32[]{:S(2)}, u32[]{:S(2)}) collective-permute-start(bf16[512,2048]{1,0:T(8,128)(2,1)} %gather_fusion.1), channel_id=1, source_target_pairs={{0,64},{64,0},{1,65},{65,1},{2,66},{66,2},{3,67},{67,3},{4,68},{68... | collective-permute-start | bytes 6291464 | tf_op jit(solution)/shard_map/ppermute | solution.py:34
  26.3 34.6 %all-to-all-start.1 = ((bf16[16,8,16,512]{3,2,1,0:T(8,128)(2,1)}), bf16[16,8,16,512]{3,2,1,0:T(8,128)(2,1)}, u32[]{:S(2)}, u32[]{:S(2)}) async-start(bf16[16,8,16,512]{3,2,1,0:T(8,128)(2,1)} %broadcast_in_dim.14), calls=%async_computation.1 | async-start | bytes 4194304 | tf_op jit(solution)/shard_map/all_to_all | solution.py:38
  35.3 27.4 %collective-permute-start = (bf16[512,512]{1,0:T(8,128)(2,1)}, bf16[512,512]{1,0:T(8,128)(2,1)}, u32[]{:S(2)}, u32[]{:S(2)}) collective-permute-start(bf16[512,512]{1,0:T(8,128)(2,1)} %get-tuple-element.13), channel_id=1, source_target_pairs={{0,64},{64,0},{1,65},{65,1},{2,66},{66,2},{3,67},{67,3},{4,68},{68... | collective-permute-start | bytes 1572872 | tf_op jit(solution)/shard_map/ppermute | solution.py:34
  60.9 3.2 %copy-start.2 = (bf16[512,512]{1,0:T(8,128)(2,1)S(1)}, bf16[512,512]{1,0:T(8,128)(2,1)}, u32[]{:S(2)}) copy-start(bf16[512,512]{1,0:T(8,128)(2,1)} %get-tuple-element.12) | copy-start | bytes 1572868
  62.8 1.3 copy-start.1
  69.5 5.0 %copy-start.4 = (bf16[1024,512]{1,0:T(8,128)(2,1)}, bf16[1024,512]{1,0:T(8,128)(2,1)S(1)}, u32[]{:S(2)}) copy-start(bf16[1024,512]{1,0:T(8,128)(2,1)S(1)} %multiply_convert_fusion) | copy-start | bytes 3145732
  107.7 6.1 %copy-start.6 = (f32[2,32,4]{1,2,0:T(4,128)S(1)}, f32[2,32,4]{1,2,0:T(4,128)}, u32[]{:S(2)}) copy-start(f32[2,32,4]{1,2,0:T(4,128)} %param.13) | copy-start | bytes 3076
  107.7 6.1 %copy-start.7 = (f32[2,32,4]{1,2,0:T(4,128)S(1)}, f32[2,32,4]{1,2,0:T(4,128)}, u32[]{:S(2)}) copy-start(f32[2,32,4]{1,2,0:T(4,128)} %param.15) | copy-start | bytes 3076
  110.3 11.3 %all-to-all-start.3 = ((bf16[8,16,512]{2,1,0:T(8,128)(2,1)}), bf16[8,16,512]{2,1,0:T(8,128)(2,1)S(1)}, u32[]{:S(2)}, u32[]{:S(2)}) async-start(bf16[8,16,512]{2,1,0:T(8,128)(2,1)} %reduce_sum.21), calls=%async_computation.3 | async-start | bytes 262144 | tf_op jit(solution)/shard_map/all_to_all | solution.py:60
  121.7 0.6 copy-start.3
  135.2 29.2 %all-to-all-start.5 = ((bf16[16,8,16,512]{3,2,1,0:T(8,128)(2,1)}), bf16[16,8,16,512]{3,2,1,0:T(8,128)(2,1)}, u32[]{:S(2)}, u32[]{:S(2)}) async-start(bf16[16,8,16,512]{3,2,1,0:T(8,128)(2,1)} %broadcast_in_dim.17), calls=%async_computation.5 | async-start | bytes 4194304 | tf_op jit(solution)/shard_map/all_to_all | solution.py:38
  139.7 39.2 %collective-permute-start.3 = (bf16[2048,512]{1,0:T(8,128)(2,1)}, bf16[2048,512]{1,0:T(8,128)(2,1)}, u32[]{:S(2)}, u32[]{:S(2)}) collective-permute-start(bf16[2048,512]{1,0:T(8,128)(2,1)} %bitcast.80), channel_id=1, source_target_pairs={{0,64},{64,0},{1,65},{65,1},{2,66},{66,2},{3,67},{67,3},{4,68},{68... | collective-permute-start | bytes 6291464 | tf_op jit(solution)/shard_map/ppermute | solution.py:34
  145.4 9.0 %collective-permute-start.4 = (f32[16,512]{1,0:T(8,128)S(1)}, f32[16,512]{1,0:T(8,128)S(1)}, u32[]{:S(2)}, u32[]{:S(2)}) collective-permute-start(f32[16,512]{1,0:T(8,128)S(1)} %get-tuple-element.15), channel_id=1, source_target_pairs={{0,64},{64,0},{1,65},{65,1},{2,66},{66,2},{3,67},{67,3},{4,68},{68... | collective-permute-start | bytes 98312 | tf_op jit(solution)/shard_map/ppermute | solution.py:34
  153.9 24.9 %collective-permute-start.2 = (bf16[512,512]{1,0:T(8,128)(2,1)}, bf16[512,512]{1,0:T(8,128)(2,1)}, u32[]{:S(2)}, u32[]{:S(2)}) collective-permute-start(bf16[512,512]{1,0:T(8,128)(2,1)} %slice.21), channel_id=1, source_target_pairs={{0,64},{64,0},{1,65},{65,1},{2,66},{66,2},{3,67},{67,3},{4,68},{68... | collective-permute-start | bytes 1572872 | tf_op jit(solution)/shard_map/ppermute | solution.py:34
  154.4 0.6 copy-start.5
  155.9 30.4 %collective-permute-start.5 = (f32[2,16,512]{2,1,0:T(8,128)S(1)}, f32[2,16,512]{2,1,0:T(8,128)S(1)}, u32[]{:S(2)}, u32[]{:S(2)}) collective-permute-start(f32[2,16,512]{2,1,0:T(8,128)S(1)} %maximum_select_fusion.2), channel_id=1, source_target_pairs={{0,128},{128,0},{1,129},{129,1},{2,130},{130,2},{3,131},{131,3},{4... | collective-permute-start | bytes 196616 | tf_op jit(solution)/shard_map/ppermute | solution.py:113
  171.8 16.4 %collective-permute-start.6 = (bf16[512,512]{1,0:T(8,128)(2,1)}, bf16[512,512]{1,0:T(8,128)(2,1)}, u32[]{:S(2)}, u32[]{:S(2)}) collective-permute-start(bf16[512,512]{1,0:T(8,128)(2,1)} %get-tuple-element.11), channel_id=1, source_target_pairs={{0,64},{64,0},{1,65},{65,1},{2,66},{66,2},{3,67},{67,3},{4,68},{68... | collective-permute-start | bytes 1572872 | tf_op jit(solution)/shard_map/ppermute | solution.py:34

commit v2 on v1

v2 whole, which is shorter than its diff:
```python
import functools

import jax
import jax.numpy as jnp
from jax import lax
from jax.experimental import pallas as pl
from jax.experimental.pallas import tpu as pltpu
from jax.sharding import Mesh
from jax.sharding import PartitionSpec as P

QBLOCK = 128

BETA_ONE = 0.9
BETA_TWO = 0.95
CORR_ONE = 1.0 - 0.9**10
CORR_TWO = 1.0 - 0.95**10
EPSILON = 1e-08
RATE = 0.002

BF = jnp.bfloat16
F32 = jnp.float32
XY = ("yh", "yl", "x")


def dequant(quant, scale):
    shaped = quant.astype(F32).reshape(quant.shape[0], quant.shape[1], -1, QBLOCK)
    return (shaped * scale[..., None]).reshape(quant.shape)


def adam_update(weight, grad, first_q, first_scale, second_q, second_scale):
    first = BETA_ONE * dequant(first_q, first_scale) + (1.0 - BETA_ONE) * grad
    second = BETA_TWO * dequant(second_q, second_scale) + (1.0 - BETA_TWO) * grad * grad
    step = first / CORR_ONE / (jnp.sqrt(second / CORR_TWO) + EPSILON)
    return (step, weight - RATE * step)


def swap(value):
    return lax.ppermute(value, "core", [(0, 1), (1, 0)])


def in_hbm(value):
    return pltpu.with_memory_space_constraint(value, pltpu.HBM)


def call(kernel, outs, *args, scratch=(), mib=8, places=None):
    vmem = pl.BlockSpec(memory_space=pltpu.VMEM)
    any_place = pl.BlockSpec(memory_space=pl.ANY)
    return pl.pallas_call(
        kernel,
        out_shape=[
            jax.ShapeDtypeStruct(shape, dtype) if near else pltpu.HBM(shape, dtype)
            for shape, dtype, near in outs
        ],
        in_specs=[
            pl.BlockSpec(memory_space=pltpu.SMEM) if near is None else vmem if near else any_place
            for near in (places or [True] * len(args))
        ],
        out_specs=[vmem if near else any_place for _, _, near in outs],
        scratch_shapes=list(scratch),
        compiler_params=pltpu.CompilerParams(vmem_limit_bytes=mib << 20),
    )(*args)


def repeat_kernel(in_ref, out_ref, sems):
    copies = [pltpu.make_async_copy(in_ref, out_ref.at[k], sems.at[k]) for k in range(out_ref.shape[0])]
    for copy in copies:
        copy.start()
    for copy in copies:
        copy.wait()


def repeat(block, count):
    return call(
        repeat_kernel,
        [((count,) + block.shape, BF, False)],
        block,
        scratch=[pltpu.SemaphoreType.DMA((count,))],
    )[0]


def natural_order(gathered_ref, whole_ref, n_z):
    n_xy, many, _ = gathered_ref.shape
    rows = many // n_z
    n_x = n_xy // 4
    for high in range(2):
        for low in range(2):
            for x in range(n_x):
                for z in range(n_z):
                    at = (((low * n_z + z) * n_x + x) * 2 + high) * rows
                    whole_ref[at : at + rows, :] = gathered_ref[
                        (high * 2 + low) * n_x + x, z * rows : (z + 1) * rows
                    ]


def across_kernel(mine_ref, other_ref, across_ref, buf_ref, sems):
    count, depth = mine_ref.shape
    step = 256
    copies = []
    for d in range(0, depth, step):
        for base, in_ref in ((0, mine_ref), (count, other_ref)):
            buf_ref[d : d + step, base : base + count] = in_ref[:, d : d + step].T
        at = pl.ds(d, step)
        copies.append(pltpu.make_async_copy(buf_ref.at[at], across_ref.at[at], sems.at[d // step]))
        copies[-1].start()
    for copy in copies:
        copy.wait()


def gate_kernel(core_ref, mine_ref, other_ref, cot_mine_ref, cot_other_ref, across_ref, gathered_ref,
                blocks_ref, dmine_ref, dother_ref, whole_out_ref,
                whole_ref, x_ref, cot_ref, turned_ref, d_ref, part_ref, in_sems, w_sems, out_sems):
    low_n, n_z, n_x, high_n, rows, feature = whole_ref.shape
    count, depth = mine_ref.shape
    step = 256
    core = core_ref[0]
    w_copies = []
    for high in range(high_n):
        for low in range(low_n):
            for x in range(n_x):
                k = (high * low_n + low) * n_x + x
                w_copies.append(
                    pltpu.make_async_copy(gathered_ref.at[k], whole_ref.at[low, :, x, high], w_sems.at[k])
                )
    loads = [
        pltpu.make_async_copy(mine_ref, x_ref.at[pl.ds(0, count)], in_sems.at[0]),
        pltpu.make_async_copy(cot_mine_ref.at[core], cot_ref.at[pl.ds(0, count)], in_sems.at[1]),
        pltpu.make_async_copy(other_ref, x_ref.at[pl.ds(count, count)], in_sems.at[2]),
        pltpu.make_async_copy(cot_other_ref.at[core], cot_ref.at[pl.ds(count, count)], in_sems.at[3]),
        pltpu.make_async_copy(across_ref, turned_ref, in_sems.at[4]),
    ]
    for copy in w_copies + loads:
        copy.start()
    for copy in w_copies:
        copy.wait()
    whole_out = pltpu.make_async_copy(whole_ref, whole_out_ref, in_sems.at[5])
    whole_out.start()
    whole = whole_ref[...].reshape(depth, feature)
    d_out = []
    for half in range(2):
        loads[2 * half].wait()
        loads[2 * half + 1].wait()
        for r in range(half * count, (half + 1) * count, step):
            gate = jnp.dot(x_ref[r : r + step, :], whole, preferred_element_type=F32)
            sig = jax.nn.sigmoid(gate)
            d_ref[r : r + step, :] = (cot_ref[r : r + step, :].astype(F32) * sig * (1.0 + gate * (1.0 - sig))).astype(BF)
        d_out.append(
            pltpu.make_async_copy(
                d_ref.at[pl.ds(half * count, count)], (dmine_ref, dother_ref)[half], in_sems.at[6 + half]
            )
        )
        d_out[-1].start()
    loads[4].wait()
    pair_rows = n_x * high_n * rows
    out_copies = []
    for low in range(low_n):
        for z in range(0, n_z, step // pair_rows):
            d = (low * n_z + z) * pair_rows
            part = jnp.dot(turned_ref[d : d + step, :], d_ref[...], preferred_element_type=F32).astype(BF)
            for k in range(step // rows):
                index = d // rows + k
                high = index % high_n
                x = index // high_n % n_x
                part_ref[(high * low_n + low) * n_x + x, index // high_n // n_x % n_z] = part[k * rows : (k + 1) * rows]
        for high in range(high_n):
            at = pl.ds((high * low_n + low) * n_x, n_x)
            out_copies.append(
                pltpu.make_async_copy(part_ref.at[at], blocks_ref.at[at], out_sems.at[high * low_n + low])
            )
            out_copies[-1].start()
    for copy in out_copies + d_out + [whole_out]:
        copy.wait()


def token_kernel(n_z, routes_ref, dmine_ref, dother_ref, whole_ref, other_ref, out_ref, other_whole_ref, placed_ref):
    natural_order(other_ref, other_whole_ref, n_z)
    count = dmine_ref.shape[0]
    step = 256
    turned = (((1,), (1,)), ((), ()))
    for t in range(0, out_ref.shape[0], step):
        places = t + lax.broadcasted_iota(jnp.int32, (step, count), 0)
        for e, d_ref in enumerate((dmine_ref, dother_ref)):
            hot = jnp.where(places == routes_ref[e : e + 1, :], 1.0, 0.0).astype(BF)
            placed_ref[e] = jnp.dot(hot, d_ref[...], preferred_element_type=F32).astype(BF)
        for d in range(0, out_ref.shape[1], 2 * step):
            at = slice(d, d + 2 * step)
            total = lax.dot_general(placed_ref[0], whole_ref[at, :], turned, preferred_element_type=F32)
            total = total + lax.dot_general(placed_ref[1], other_whole_ref[at, :], turned, preferred_element_type=F32)
            out_ref[t : t + step, at] = total.astype(BF)


def sum_kernel(got_ref, out_ref):
    total = got_ref[0].astype(F32)
    for k in range(1, got_ref.shape[0]):
        total = total + got_ref[k].astype(F32)
    out_ref[...] = total.astype(BF)


def sum_blocks(got, step=32):
    count, rows, feature = got.shape
    return pl.pallas_call(
        sum_kernel,
        grid=(rows // step,),
        in_specs=[pl.BlockSpec((count, step, feature), lambda i: (0, i, 0))],
        out_specs=pl.BlockSpec((step, feature), lambda i: (i, 0)),
        out_shape=jax.ShapeDtypeStruct((rows, feature), BF),
    )(got)


def adam_kernel(total_rows):
    def kernel(got_ref, weight_ref, first_ref, second_ref, grad_ref, out_ref):
        total = got_ref[0].astype(F32)
        for k in range(1, got_ref.shape[0]):
            total = total + got_ref[k].astype(F32)
        grad = total / total_rows
        grad_ref[...] = grad
        first = first_ref[...] + (1.0 - BETA_ONE) * grad
        second = second_ref[...] + (1.0 - BETA_TWO) * grad * grad
        step = first / CORR_ONE / (jnp.sqrt(second / CORR_TWO) + EPSILON)
        new = (weight_ref[...] - RATE * step).astype(BF)
        for k in range(out_ref.shape[0]):
            out_ref[k] = new

    return kernel


def next_other_kernel(n_z, x_ref, gathered_ref, out_ref, whole_ref):
    natural_order(gathered_ref, whole_ref, n_z)
    out_ref[...] = jnp.dot(x_ref[...], whole_ref[...], preferred_element_type=F32).astype(BF)


def next_mine_kernel(x_ref, whole_ref, out_ref):
    out_ref[...] = jnp.dot(x_ref[...], whole_ref[...], preferred_element_type=F32).astype(BF)


def pair(mine, other, core):
    return jnp.where(core == 0, jnp.stack([mine, other]), jnp.stack([other, mine]))


def on_device(tokens, route, cotangent, weight, first_q, first_scale, second_q, second_scale):
    n_rep = lax.axis_size("yh") * lax.axis_size("core")
    n_z = lax.axis_size("z")
    n_x = lax.axis_size("x")
    n_xy = lax.axis_size(XY)
    core = lax.axis_index("core")
    high = lax.axis_index("yh")
    rows_here = route.shape[1]
    depth = tokens.shape[1]
    feature = cotangent.shape[2]
    total_rows = rows_here * n_rep * lax.axis_size("yl") * n_z * n_x
    owned = weight.shape[1]
    half = owned // 2

    def mine_of(array):
        return lax.dynamic_index_in_dim(array, core, 0, keepdims=False)

    def other_of(array):
        return lax.dynamic_index_in_dim(array, 1 - core, 0, keepdims=False)

    def part_of(array):
        return lax.dynamic_slice_in_dim(mine_of(array), high * half, half, 0)

    def over_z(blocks):
        return lax.all_to_all(blocks, "z", 0, 0, tiled=True)

    def over_xy(blocks):
        flat = blocks.reshape(n_xy, n_z * half, feature)
        return lax.all_to_all(flat, XY, 0, 0, tiled=True)

    weight_part = part_of(weight)
    start_blocks = jnp.broadcast_to(weight_part.astype(BF)[None], (n_z, half, feature))
    to_send = repeat(over_z(start_blocks).reshape(-1, feature), n_xy)
    tokens_far, route_far, cot_far = swap(tokens), swap(route), swap(cotangent)
    tokens_b, route_b, tokens_far, route_far, to_send = lax.optimization_barrier(
        (tokens, route, tokens_far, route_far, to_send)
    )
    gathered = over_xy(to_send)
    route_mine = mine_of(route_b)
    route_other = other_of(route_b)
    x_other = tokens_far[mine_of(route_far)]
    x_mine = tokens_b[route_mine]
    (across,) = call(
        across_kernel,
        [((depth, 2 * rows_here), BF, False)],
        x_mine,
        x_other,
        scratch=[pltpu.VMEM((depth, 2 * rows_here), BF), pltpu.SemaphoreType.DMA((depth // 256,))],
        mib=16,
    )
    first_part = BETA_ONE * dequant(part_of(first_q)[None], part_of(first_scale)[None])[0]
    second_part = BETA_TWO * dequant(part_of(second_q)[None], part_of(second_scale)[None])[0]
    gathered, x_mine, x_other, across, cot_far, first_part, second_part = lax.optimization_barrier(
        (gathered, x_mine, x_other, across, cot_far, first_part, second_part)
    )

    other_gathered = swap(gathered)
    blocks, dmine, dother, whole = call(
        gate_kernel,
        [
            ((n_xy, n_z, half, feature), BF, False),
            ((rows_here, feature), BF, False),
            ((rows_here, feature), BF, False),
            ((2, n_z, n_x, 2, half, feature), BF, False),
        ],
        core.reshape(1),
        in_hbm(x_mine),
        in_hbm(x_other),
        in_hbm(cotangent),
        in_hbm(cot_far),
        in_hbm(across),
        in_hbm(gathered.reshape(n_xy, n_z, half, feature)),
        scratch=[
            pltpu.VMEM((2, n_z, n_x, 2, half, feature), BF),
            pltpu.VMEM((2 * rows_here, depth), BF),
            pltpu.VMEM((2 * rows_here, feature), BF),
            pltpu.VMEM((depth, 2 * rows_here), BF),
            pltpu.VMEM((2 * rows_here, feature), BF),
            pltpu.VMEM((n_xy, n_z, half, feature), BF),
            pltpu.SemaphoreType.DMA((8,)),
            pltpu.SemaphoreType.DMA((n_xy,)),
            pltpu.SemaphoreType.DMA((4,)),
        ],
        mib=24,
        places=[None] + [False] * 6,
    )
    whole = whole.reshape(depth, feature)
    got = over_xy(blocks)
    other_rows = swap(dother)
    (token_grad,) = call(
        functools.partial(token_kernel, n_z),
        [(tokens.shape, BF, True)],
        jnp.stack([route_mine, route_other]),
        dmine,
        other_rows,
        whole,
        other_gathered,
        scratch=[pltpu.VMEM((depth, feature), BF), pltpu.VMEM((2, 256, feature), BF)],
        mib=14,
    )
    got, token_grad = lax.optimization_barrier((got, token_grad))
    part = sum_blocks(got)
    got_z = over_z(part.reshape(n_z, half, feature))
    grad, new_blocks = call(
        adam_kernel(total_rows),
        [((half, feature), F32, True), ((n_z, half, feature), BF, True)],
        (got_z),
        weight_part,
        first_part,
        second_part,
    )
    new_send = repeat(over_z(new_blocks).reshape(-1, feature), n_xy)
    new_send, grad = lax.optimization_barrier((new_send, grad))
    new_gathered = over_xy(new_send)
    both = pair(grad, swap(grad), core)
    far = lax.ppermute(both, "yh", [(0, 1), (1, 0)])
    both = jnp.where(
        high == 0, jnp.concatenate([both, far], axis=1), jnp.concatenate([far, both], axis=1)
    )
    step_dir, new_weight = adam_update(weight, both, first_q, first_scale, second_q, second_scale)
    new_gathered, step_dir, new_weight = lax.optimization_barrier((new_gathered, step_dir, new_weight))

    next_other, new_whole = call(
        functools.partial(next_other_kernel, n_z),
        [((rows_here, feature), BF, True), ((depth, feature), BF, True)],
        x_other,
        (new_gathered),
    )
    next_other = swap(next_other)
    (next_mine,) = call(
        next_mine_kernel, [((rows_here, feature), BF, True)], x_mine, new_whole
    )
    next_gate = pair(next_mine, next_other, core)
    return (token_grad, step_dir, new_weight, next_gate)


def solution(mesh):
    split = Mesh(mesh.devices.reshape(2, 2, 2, 8, 4), ("yh", "core", "yl", "z", "x"))
    rep = ("yh", "core")
    ep = ("yl", "z", "x")
    every = rep + ep
    in_specs = (
        P(every, None),
        P(None, every),
        P(None, every, None),
        P(None, ep, None),
        P(None, ep, None),
        P(None, ep, None),
        P(None, ep, None),
        P(None, ep, None),
    )
    out_specs = (
        P(every, None),
        P(None, ep, None),
        P(None, ep, None),
        P(None, every, None),
    )
    return jax.shard_map(
        on_device, mesh=split, in_specs=in_specs, out_specs=out_specs, check_vma=False
    )
```

time: 192 us -> 177 us (0.922)
  blocking collectives: 58.2 us -> 10.4 us
  waiting for transfers between devices: 27.1 us -> 70 us
  Pallas kernels: 0 us -> 29.1 us
  matrix products: 28.9 us -> 0 us
  local copies, waits for them, and re-layouts: 30.7 us -> 15.8 us
  starting transfers between devices: 34.6 us -> 47.9 us
  other arithmetic: 10.8 us -> 2.02 us
    all_to_all x3 -> x1, blocking collectives: 58.2 us -> 10.4 us  [over_z(): return lax.all_to_all(blocks, 'z', 0, 0, tiled=True)]
    pallas_call x0 -> x9, Pallas kernels: none -> 29.1 us  [the longest x8 25.6 us: call(): pl.pallas_call(kernel, out_shape=[jax.ShapeDtypeStruct(shape, dtype) if n...]
    dot_general x5 -> x0, matrix products: 28.9 us -> none  [the longest x1 7.46 us: on_device(): jnp.einsum('tf,df->td', at_tokens(route_other, other_rows), other_whole,...]
    all_to_all x3 -> x5, waiting for transfers between devices: 27.1 us -> 51.4 us  [the longest x3 35.6 us: over_xy(): return lax.all_to_all(flat, XY, 0, 0, tiled=True)]
    ppermute x1, waiting for transfers between devices: 0.01 us -> 15.4 us  [on_device(): far = lax.ppermute(both, 'yh', [(0, 1), (1, 0)])]
    all_to_all x3 -> x5, starting transfers between devices: 14.6 us -> 25.7 us  [the longest x3 15.9 us: over_xy(): return lax.all_to_all(flat, XY, 0, 0, tiled=True)]
    transpose x2 -> x0, local copies, waits for them, and re-layouts: 3.63 us -> none  [gather_rows(): whole.reshape(2, 2, n_x, n_z, rows, feature).transpose(1, 3, 2, 0, 4, 5)]
    unnamed x19 -> x26, local copies, waits for them, and re-layouts: 6.96 us -> 3.42 us
  transfers between devices with their start and end apart: 10 -> 13, of which waited for: 3 -> 9; matrix products, arithmetic and copies ran while one was open for 23% -> 8% of each run, Pallas kernels for 0% -> 12%
where the time goes in v2:
time: 177 us; the launch traced here: 176 us
  waiting for transfers between devices  70 us (40%)
  starting transfers between devices  47.9 us (27%)
  Pallas kernels  29.1 us (16%)
  local copies, waits for them, and re-layouts  15.8 us (9%)
  blocking collectives  10.4 us (6%)
  other arithmetic  2.02 us (1%)
    all_to_all x3, waiting for transfers between devices, over_xy(): return lax.all_to_all(flat, XY, 0, 0, tiled=True)  35.6 us
    pallas_call x8, Pallas kernels, call(): pl.pallas_call(kernel, out_shape=[jax.ShapeDtypeStruct(shape, dtype) if n...  25.6 us
    ppermute x7, starting transfers between devices, swap(): return lax.ppermute(value, 'core', [(0, 1), (1, 0)])  19.1 us
    all_to_all x3, starting transfers between devices, over_xy(): return lax.all_to_all(flat, XY, 0, 0, tiled=True)  15.9 us
    all_to_all x2, waiting for transfers between devices, over_z(): return lax.all_to_all(blocks, 'z', 0, 0, tiled=True)  15.8 us
    ppermute x1, waiting for transfers between devices, on_device(): far = lax.ppermute(both, 'yh', [(0, 1), (1, 0)])  15.4 us
    all_to_all x1, blocking collectives, over_z(): return lax.all_to_all(blocks, 'z', 0, 0, tiled=True)  10.4 us
    all_to_all x2, starting transfers between devices, over_z(): return lax.all_to_all(blocks, 'z', 0, 0, tiled=True)  9.82 us
  transfers between devices with their start and end apart: 13, of which 9 were waited for; matrix products, arithmetic and copies ran while one was open for 8% of the time, Pallas kernels for 12%

profile of v2, /device:TPU:1, one launch (start us, length us, event | category | flops | bytes accessed | tf_op | source)
XLA Modules:
  0.0 176.2 jit_solution(15000653211457324422)
XLA Ops:
  0.6 3.3 %collective-permute-start = (bf16[768,2048]{1,0:T(8,128)(2,1)}, bf16[768,2048]{1,0:T(8,128)(2,1)S(1)}, u32[]{:S(2)}, u32[]{:S(2)}) collective-permute-start(bf16[768,2048]{1,0:T(8,128)(2,1)} %param.8), channel_id=1, source_target_pairs={{0,64},{64,0},{1,65},{65,1},{2,66},{66,2},{3,67},{67,3},{4,68},{68... | collective-permute-start | bytes 9437192 | tf_op jit(solution)/shard_map/ppermute | solution.py:38
  4.0 0.8 fusion.7
  4.8 0.7 broadcast_in_dim.5
  5.4 6.5 %all-to-all-start = ((bf16[8,16,512]{2,1,0:T(8,128)(2,1)}), bf16[8,16,512]{2,1,0:T(8,128)(2,1)S(1)}, u32[]{:S(2)}, u32[]{:S(2)}) async-start(bf16[8,16,512]{2,1,0:T(8,128)(2,1)} %broadcast_in_dim.5), calls=%async_computation | async-start | bytes 262144 | tf_op jit(solution)/shard_map/all_to_all | solution.py:263
  11.9 0.3 collective-permute-start.1
  12.2 8.2 %all-to-all-done = bf16[8,16,512]{2,1,0:T(8,128)(2,1)S(1)} async-done(((bf16[8,16,512]{2,1,0:T(8,128)(2,1)}), bf16[8,16,512]{2,1,0:T(8,128)(2,1)S(1)}, u32[]{:S(2)}, u32[]{:S(2)}) %all-to-all-start) | async-done | bytes 131104 | tf_op jit(solution)/shard_map/all_to_all | solution.py:263
  20.4 1.4 shard_map.111
  21.9 6.9 %all-to-all-start.1 = ((bf16[16,128,512]{2,1,0:T(8,128)(2,1)}), bf16[16,128,512]{2,1,0:T(8,128)(2,1)}, u32[]{:S(2)}, u32[]{:S(2)}) async-start(bf16[16,128,512]{2,1,0:T(8,128)(2,1)} %shard_map.111), calls=%async_computation.1 | async-start | bytes 4194304 | tf_op jit(solution)/shard_map/all_to_all | solution.py:267
  28.8 1.9 %collective-permute-start.2 = (bf16[2,512,512]{2,1,0:T(8,128)(2,1)}, bf16[2,512,512]{2,1,0:T(8,128)(2,1)}, u32[]{:S(2)}, u32[]{:S(2)}) collective-permute-start(bf16[2,512,512]{2,1,0:T(8,128)(2,1)} %cot_mine_ref.1), channel_id=1, source_target_pairs={{0,64},{64,0},{1,65},{65,1},{2,66},{66,2},{3,67},{67,3},{4,68},{68... | collective-permute-start | bytes 3145736 | tf_op jit(solution)/shard_map/ppermute | solution.py:38
  30.7 0.1 dynamic-slice_bitcast_fusion.2
  30.8 0.1 copy.16
  31.0 0.1 copy.17
  31.0 0.1 mul.106
  31.1 0.1 mul.112
  31.3 3.4 %gather_fusion.1 = bf16[512,2048]{1,0:T(8,128)(2,1)} fusion(bf16[768,2048]{1,0:T(8,128)(2,1)S(1)} %collective-permute-done, s32[1024]{0:T(1024)S(1)} %pad_clamp_fusion), kind=kCustom, calls=%fused_computation.1 | custom fusion | bytes 4196352 | tf_op jit(solution)/shard_map/gather | solution.py:279
  34.7 6.7 %gather_fusion = bf16[512,2048]{1,0:T(8,128)(2,1)S(1)} fusion(bf16[768,2048]{1,0:T(8,128)(2,1)} %param.8, s32[1024]{0:T(1024)S(1)} %pad_clamp_fusion.1), kind=kCustom, calls=%fused_computation | custom fusion | bytes 4196352 | tf_op jit(solution)/shard_map/gather | solution.py:280
  41.4 1.6 copy-done.2
  43.0 2.6 %shard_map.112.across_ref = bf16[2048,1024]{1,0:T(8,128)(2,1)} custom-call(bf16[512,2048]{1,0:T(8,128)(2,1)S(1)} %gather_fusion, bf16[512,2048]{1,0:T(8,128)(2,1)S(1)} %copy-done.2), custom_call_target="tpu_custom_call" | custom-call | tf_op jit(solution)/shard_map/pallas_call | solution.py:48
  45.6 11.0 %all-to-all-done.1 = bf16[16,128,512]{2,1,0:T(8,128)(2,1)} async-done(((bf16[16,128,512]{2,1,0:T(8,128)(2,1)}), bf16[16,128,512]{2,1,0:T(8,128)(2,1)}, u32[]{:S(2)}, u32[]{:S(2)}) %all-to-all-start.1) | async-done | bytes 2097184 | tf_op jit(solution)/shard_map/all_to_all | solution.py:267
  56.6 3.9 %collective-permute-start.4 = (bf16[16,128,512]{2,1,0:T(8,128)(2,1)}, bf16[16,128,512]{2,1,0:T(8,128)(2,1)S(1)}, u32[]{:S(2)}, u32[]{:S(2)}) collective-permute-start(bf16[16,128,512]{2,1,0:T(8,128)(2,1)} %all-to-all-done.1), channel_id=1, source_target_pairs={{0,64},{64,0},{1,65},{65,1},{2,66},{66,2},{3,67},{67,3},{4,68},{68... | collective-permute-start | bytes 6291464 | tf_op jit(solution)/shard_map/ppermute | solution.py:38
  60.5 9.6 %shard_map.113 = (bf16[16,8,16,512]{3,2,1,0:T(8,128)(2,1)}, bf16[512,512]{1,0:T(8,128)(2,1)}, bf16[512,512]{1,0:T(8,128)(2,1)}, bf16[2,8,4,2,16,512]{5,4,3,2,1,0:T(8,128)(2,1)}) custom-call(s32[1]{0:T(128)} %bitcast.core_ref, bf16[512,2048]{1,0:T(8,128)(2,1)} %copy-done, bf16[512,2048]{1,0:T(8,128)(2,1)} %gather_fusion.1, bf16[2,512,512]{2,1,0:T(8,128)(2,1)} %cot_mine_ref.1, ...), custom_call_target="tpu_custom_call" | custom-call | tf_op jit(solution)/shard_map/pallas_call | solution.py:48
  70.2 4.6 %all-to-all-start.2 = ((bf16[16,128,512]{2,1,0:T(8,128)(2,1)}), bf16[16,128,512]{2,1,0:T(8,128)(2,1)}, u32[]{:S(2)}, u32[]{:S(2)}) async-start(bf16[16,128,512]{2,1,0:T(8,128)(2,1)} %bitcast.44), calls=%async_computation.2 | async-start | bytes 4194304 | tf_op jit(solution)/shard_map/all_to_all | solution.py:267
  74.7 0.3 collective-permute-start.3
  75.0 2.1 %collective-permute-done.3.dother_ref = bf16[512,512]{1,0:T(8,128)(2,1)S(1)} collective-permute-done((bf16[512,512]{1,0:T(8,128)(2,1)}, bf16[512,512]{1,0:T(8,128)(2,1)S(1)}, u32[]{:S(2)}, u32[]{:S(2)}) %collective-permute-start.3) | collective-permute-done | bytes 524320 | tf_op jit(solution)/shard_map/ppermute | solution.py:38
  77.1 1.6 copy-done.4
  78.7 6.2 %shard_map.114 = bf16[768,2048]{1,0:T(8,128)(2,1)} custom-call(s32[2,512]{1,0:T(2,128)S(1)} %pad_add_fusion.routes_ref, bf16[512,512]{1,0:T(8,128)(2,1)S(1)} %copy-done.5, bf16[512,512]{1,0:T(8,128)(2,1)S(1)} %collective-permute-done.3.dother_ref, bf16[2048,512]{1,0:T(8,128)(2,1)S(1)} %bitcast.40, bf16[16,128,512]{2,1,0:T(8,128)(2,1)S(1)} %collective-permute-done.4.other_ref), custom_call_target="tpu_custom_call" | custom-call | tf_op jit(solution)/shard_map/pallas_call | solution.py:48
  84.9 23.8 %all-to-all-done.2.got_ref = bf16[16,128,512]{2,1,0:T(8,128)(2,1)} async-done(((bf16[16,128,512]{2,1,0:T(8,128)(2,1)}), bf16[16,128,512]{2,1,0:T(8,128)(2,1)}, u32[]{:S(2)}, u32[]{:S(2)}) %all-to-all-start.2) | async-done | bytes 2097184 | tf_op jit(solution)/shard_map/all_to_all | solution.py:267
  108.7 3.5 %shard_map.115 = bf16[128,512]{1,0:T(8,128)(2,1)} custom-call(bf16[16,128,512]{2,1,0:T(8,128)(2,1)} %all-to-all-done.2.got_ref), custom_call_target="tpu_custom_call" | custom-call | tf_op jit(solution)/shard_map/pallas_call | solution.py:200
  112.2 3.4 %all-to-all-start.3 = ((bf16[8,16,512]{2,1,0:T(8,128)(2,1)}), bf16[8,16,512]{2,1,0:T(8,128)(2,1)S(1)}, u32[]{:S(2)}, u32[]{:S(2)}) async-start(bf16[8,16,512]{2,1,0:T(8,128)(2,1)} %bitcast.46), calls=%async_computation.3 | async-start | bytes 262144 | tf_op jit(solution)/shard_map/all_to_all | solution.py:263
  115.6 7.6 %all-to-all-done.3.got_ref = bf16[8,16,512]{2,1,0:T(8,128)(2,1)S(1)} async-done(((bf16[8,16,512]{2,1,0:T(8,128)(2,1)}), bf16[8,16,512]{2,1,0:T(8,128)(2,1)S(1)}, u32[]{:S(2)}, u32[]{:S(2)}) %all-to-all-start.3) | async-done | bytes 131104 | tf_op jit(solution)/shard_map/all_to_all | solution.py:263
  123.3 10.4 %all_to_all.30 = bf16[8,16,512]{2,1,0:T(8,128)(2,1)S(1)} all-to-all(bf16[8,16,512]{2,1,0:T(8,128)(2,1)S(1)} %get-tuple-element.49), channel_id=1, replica_groups=mesh['yh'=2,'core'=2,'yl'=2,'z'=8,'x'=4] {'z'}, dimensions={0} | all-to-all | bytes 262144 | tf_op jit(solution)/shard_map/all_to_all | solution.py:263
  133.7 1.5 shard_map.117
  135.2 4.4 %all-to-all-start.5 = ((bf16[16,128,512]{2,1,0:T(8,128)(2,1)}), bf16[16,128,512]{2,1,0:T(8,128)(2,1)}, u32[]{:S(2)}, u32[]{:S(2)}) async-start(bf16[16,128,512]{2,1,0:T(8,128)(2,1)} %shard_map.117), calls=%async_computation.5 | async-start | bytes 4194304 | tf_op jit(solution)/shard_map/all_to_all | solution.py:267
  139.7 3.4 %collective-permute-start.5 = (f32[16,512]{1,0:T(8,128)S(1)}, f32[16,512]{1,0:T(8,128)S(1)}, u32[]{:S(2)}, u32[]{:S(2)}) collective-permute-start(f32[16,512]{1,0:T(8,128)S(1)} %get-tuple-element.52), channel_id=1, source_target_pairs={{0,64},{64,0},{1,65},{65,1},{2,66},{66,2},{3,67},{67,3},{4,68},{68... | collective-permute-start | bytes 98312 | tf_op jit(solution)/shard_map/ppermute | solution.py:38
  143.1 0.9 collective-permute-done.5
  143.9 3.1 %collective-permute-start.6 = (f32[2,16,512]{2,1,0:T(8,128)S(1)}, f32[2,16,512]{2,1,0:T(8,128)S(1)}, u32[]{:S(2)}, u32[]{:S(2)}) collective-permute-start(f32[2,16,512]{2,1,0:T(8,128)S(1)} %maximum_select_fusion.2), channel_id=1, source_target_pairs={{0,128},{128,0},{1,129},{129,1},{2,130},{130,2},{3,131},{131,3},{4... | collective-permute-start | bytes 196616 | tf_op jit(solution)/shard_map/ppermute | solution.py:354
  147.0 0.1 copy.18
  147.1 0.1 copy.19
  147.2 0.1 mul.117
  147.4 0.1 mul.124
  147.6 15.4 %collective-permute-done.6 = f32[2,16,512]{2,1,0:T(8,128)S(1)} collective-permute-done((f32[2,16,512]{2,1,0:T(8,128)S(1)}, f32[2,16,512]{2,1,0:T(8,128)S(1)}, u32[]{:S(2)}, u32[]{:S(2)}) %collective-permute-start.6) | collective-permute-done | bytes 65568 | tf_op jit(solution)/shard_map/ppermute | solution.py:354
  163.0 0.8 multiply_subtract_fusion
  163.8 0.8 all-to-all-done.5.gathered_ref
  164.6 3.0 %shard_map.118 = (bf16[512,512]{1,0:T(8,128)(2,1)S(1)}, bf16[2048,512]{1,0:T(8,128)(2,1)S(1)}) custom-call(bf16[512,2048]{1,0:T(8,128)(2,1)S(1)} %copy-done.3, bf16[16,128,512]{2,1,0:T(8,128)(2,1)} %all-to-all-done.5.gathered_ref), custom_call_target="tpu_custom_call" | custom-call | tf_op jit(solution)/shard_map/pallas_call | solution.py:48
  167.6 6.0 %collective-permute-start.7 = (bf16[512,512]{1,0:T(8,128)(2,1)S(1)}, bf16[512,512]{1,0:T(8,128)(2,1)S(1)}, u32[]{:S(2)}, u32[]{:S(2)}) collective-permute-start(bf16[512,512]{1,0:T(8,128)(2,1)S(1)} %get-tuple-element.57), channel_id=1, source_target_pairs={{0,64},{64,0},{1,65},{65,1},{2,66},{66,2},{3,67},{67,3},{4,68},{68... | collective-permute-start | bytes 1572872 | tf_op jit(solution)/shard_map/ppermute | solution.py:38
  173.6 1.2 shard_map.119
  174.8 0.3 collective-permute-done.7
  175.1 1.1 maximum_select_fusion
  (38 shorter events, 0.4 us)
Async XLA Ops:
  0.6 21.3 %collective-permute-start = (bf16[768,2048]{1,0:T(8,128)(2,1)}, bf16[768,2048]{1,0:T(8,128)(2,1)S(1)}, u32[]{:S(2)}, u32[]{:S(2)}) collective-permute-start(bf16[768,2048]{1,0:T(8,128)(2,1)} %param.8), channel_id=1, source_target_pairs={{0,64},{64,0},{1,65},{65,1},{2,66},{66,2},{3,67},{67,3},{4,68},{68... | collective-permute-start | bytes 9437192 | tf_op jit(solution)/shard_map/ppermute | solution.py:38
  5.4 14.9 %all-to-all-start = ((bf16[8,16,512]{2,1,0:T(8,128)(2,1)}), bf16[8,16,512]{2,1,0:T(8,128)(2,1)S(1)}, u32[]{:S(2)}, u32[]{:S(2)}) async-start(bf16[8,16,512]{2,1,0:T(8,128)(2,1)} %broadcast_in_dim.5), calls=%async_computation | async-start | bytes 262144 | tf_op jit(solution)/shard_map/all_to_all | solution.py:263
  11.9 10.0 %collective-permute-start.1 = (s32[2,512]{1,0:T(2,128)}, s32[2,512]{1,0:T(2,128)S(1)}, u32[]{:S(2)}, u32[]{:S(2)}) collective-permute-start(s32[2,512]{1,0:T(2,128)} %param.9), channel_id=1, source_target_pairs={{0,64},{64,0},{1,65},{65,1},{2,66},{66,2},{3,67},{67,3},{4,68},{68... | collective-permute-start | bytes 12296 | tf_op jit(solution)/shard_map/ppermute | solution.py:38
  21.8 8.9 %copy-start.9 = (f32[2,32,4]{1,2,0:T(4,128)S(1)}, f32[2,32,4]{1,2,0:T(4,128)}, u32[]{:S(2)}) copy-start(f32[2,32,4]{1,2,0:T(4,128)} %param.13) | copy-start | bytes 3076
  21.8 9.1 %copy-start.10 = (f32[2,32,4]{1,2,0:T(4,128)S(1)}, f32[2,32,4]{1,2,0:T(4,128)}, u32[]{:S(2)}) copy-start(f32[2,32,4]{1,2,0:T(4,128)} %param.15) | copy-start | bytes 3076
  21.8 9.4 %copy-start.7 = (s32[2,32,512]{2,1,0:T(8,128)S(1)}, s32[2,32,512]{2,1,0:T(8,128)}, u32[]{:S(2)}) copy-start(s32[2,32,512]{2,1,0:T(8,128)} %param.14) | copy-start | bytes 393220
  21.8 9.4 %copy-start.8 = (s32[2,32,512]{2,1,0:T(8,128)S(1)}, s32[2,32,512]{2,1,0:T(8,128)}, u32[]{:S(2)}) copy-start(s32[2,32,512]{2,1,0:T(8,128)} %param.12) | copy-start | bytes 393220
  21.9 9.4 %copy-start.11 = (s32[2,512]{1,0:T(2,128)S(1)}, s32[2,512]{1,0:T(2,128)}, u32[]{:S(2)}) copy-start(s32[2,512]{1,0:T(2,128)} %param.9) | copy-start | bytes 12292
  21.9 34.7 %all-to-all-start.1 = ((bf16[16,128,512]{2,1,0:T(8,128)(2,1)}), bf16[16,128,512]{2,1,0:T(8,128)(2,1)}, u32[]{:S(2)}, u32[]{:S(2)}) async-start(bf16[16,128,512]{2,1,0:T(8,128)(2,1)} %shard_map.111), calls=%async_computation.1 | async-start | bytes 4194304 | tf_op jit(solution)/shard_map/all_to_all | solution.py:267
  28.8 16.8 %collective-permute-start.2 = (bf16[2,512,512]{2,1,0:T(8,128)(2,1)}, bf16[2,512,512]{2,1,0:T(8,128)(2,1)}, u32[]{:S(2)}, u32[]{:S(2)}) collective-permute-start(bf16[2,512,512]{2,1,0:T(8,128)(2,1)} %cot_mine_ref.1), channel_id=1, source_target_pairs={{0,64},{64,0},{1,65},{65,1},{2,66},{66,2},{3,67},{67,3},{4,68},{68... | collective-permute-start | bytes 3145736 | tf_op jit(solution)/shard_map/ppermute | solution.py:38
  41.4 1.6 copy-start.2
  43.0 2.6 %copy-start = (bf16[512,2048]{1,0:T(8,128)(2,1)}, bf16[512,2048]{1,0:T(8,128)(2,1)S(1)}, u32[]{:S(2)}) copy-start(bf16[512,2048]{1,0:T(8,128)(2,1)S(1)} %gather_fusion) | copy-start | bytes 6291460
  56.6 20.5 %collective-permute-start.4 = (bf16[16,128,512]{2,1,0:T(8,128)(2,1)}, bf16[16,128,512]{2,1,0:T(8,128)(2,1)S(1)}, u32[]{:S(2)}, u32[]{:S(2)}) collective-permute-start(bf16[16,128,512]{2,1,0:T(8,128)(2,1)} %all-to-all-done.1), channel_id=1, source_target_pairs={{0,64},{64,0},{1,65},{65,1},{2,66},{66,2},{3,67},{67,3},{4,68},{68... | collective-permute-start | bytes 6291464 | tf_op jit(solution)/shard_map/ppermute | solution.py:38
  70.1 7.0 %copy-start.5 = (bf16[512,512]{1,0:T(8,128)(2,1)S(1)}, bf16[512,512]{1,0:T(8,128)(2,1)}, u32[]{:S(2)}) copy-start(bf16[512,512]{1,0:T(8,128)(2,1)} %get-tuple-element.42.dmine_ref) | copy-start | bytes 1572868
  70.2 38.6 %all-to-all-start.2 = ((bf16[16,128,512]{2,1,0:T(8,128)(2,1)}), bf16[16,128,512]{2,1,0:T(8,128)(2,1)}, u32[]{:S(2)}, u32[]{:S(2)}) async-start(bf16[16,128,512]{2,1,0:T(8,128)(2,1)} %bitcast.44), calls=%async_computation.2 | async-start | bytes 4194304 | tf_op jit(solution)/shard_map/all_to_all | solution.py:267
  74.7 2.4 %collective-permute-start.3 = (bf16[512,512]{1,0:T(8,128)(2,1)}, bf16[512,512]{1,0:T(8,128)(2,1)S(1)}, u32[]{:S(2)}, u32[]{:S(2)}) collective-permute-start(bf16[512,512]{1,0:T(8,128)(2,1)} %get-tuple-element.43), channel_id=1, source_target_pairs={{0,64},{64,0},{1,65},{65,1},{2,66},{66,2},{3,67},{67,3},{4,68},{68... | collective-permute-start | bytes 1572872 | tf_op jit(solution)/shard_map/ppermute | solution.py:38
  77.1 1.6 copy-start.4
  84.9 30.7 %copy-start.6 = (f32[2,32,512]{2,1,0:T(8,128)S(1)}, f32[2,32,512]{2,1,0:T(8,128)}, u32[]{:S(2)}) copy-start(f32[2,32,512]{2,1,0:T(8,128)} %param.11) | copy-start | bytes 393220
  112.2 11.1 %all-to-all-start.3 = ((bf16[8,16,512]{2,1,0:T(8,128)(2,1)}), bf16[8,16,512]{2,1,0:T(8,128)(2,1)S(1)}, u32[]{:S(2)}, u32[]{:S(2)}) async-start(bf16[8,16,512]{2,1,0:T(8,128)(2,1)} %bitcast.46), calls=%async_computation.3 | async-start | bytes 262144 | tf_op jit(solution)/shard_map/all_to_all | solution.py:263
  135.2 29.4 %all-to-all-start.5 = ((bf16[16,128,512]{2,1,0:T(8,128)(2,1)}), bf16[16,128,512]{2,1,0:T(8,128)(2,1)}, u32[]{:S(2)}, u32[]{:S(2)}) async-start(bf16[16,128,512]{2,1,0:T(8,128)(2,1)} %shard_map.117), calls=%async_computation.5 | async-start | bytes 4194304 | tf_op jit(solution)/shard_map/all_to_all | solution.py:267
  139.7 24.9 %copy-start.3 = (bf16[512,2048]{1,0:T(8,128)(2,1)S(1)}, bf16[512,2048]{1,0:T(8,128)(2,1)}, u32[]{:S(2)}) copy-start(bf16[512,2048]{1,0:T(8,128)(2,1)} %gather_fusion.1) | copy-start | bytes 6291460
  139.7 4.3 %collective-permute-start.5 = (f32[16,512]{1,0:T(8,128)S(1)}, f32[16,512]{1,0:T(8,128)S(1)}, u32[]{:S(2)}, u32[]{:S(2)}) collective-permute-start(f32[16,512]{1,0:T(8,128)S(1)} %get-tuple-element.52), channel_id=1, source_target_pairs={{0,64},{64,0},{1,65},{65,1},{2,66},{66,2},{3,67},{67,3},{4,68},{68... | collective-permute-start | bytes 98312 | tf_op jit(solution)/shard_map/ppermute | solution.py:38
  143.9 19.0 %collective-permute-start.6 = (f32[2,16,512]{2,1,0:T(8,128)S(1)}, f32[2,16,512]{2,1,0:T(8,128)S(1)}, u32[]{:S(2)}, u32[]{:S(2)}) collective-permute-start(f32[2,16,512]{2,1,0:T(8,128)S(1)} %maximum_select_fusion.2), channel_id=1, source_target_pairs={{0,128},{128,0},{1,129},{129,1},{2,130},{130,2},{3,131},{131,3},{4... | collective-permute-start | bytes 196616 | tf_op jit(solution)/shard_map/ppermute | solution.py:354
  164.6 9.0 %copy-start.1 = (bf16[512,2048]{1,0:T(8,128)(2,1)S(1)}, bf16[512,2048]{1,0:T(8,128)(2,1)}, u32[]{:S(2)}) copy-start(bf16[512,2048]{1,0:T(8,128)(2,1)} %copy-done) | copy-start | bytes 6291460
  167.6 7.5 %collective-permute-start.7 = (bf16[512,512]{1,0:T(8,128)(2,1)S(1)}, bf16[512,512]{1,0:T(8,128)(2,1)S(1)}, u32[]{:S(2)}, u32[]{:S(2)}) collective-permute-start(bf16[512,512]{1,0:T(8,128)(2,1)S(1)} %get-tuple-element.57), channel_id=1, source_target_pairs={{0,64},{64,0},{1,65},{65,1},{2,66},{66,2},{3,67},{67,3},{4,68},{68... | collective-permute-start | bytes 1572872 | tf_op jit(solution)/shard_map/ppermute | solution.py:38

commit v3 on v1

v3 whole, which is shorter than its diff:
```python
import jax
import jax.numpy as jnp
from jax import lax
from jax.experimental import pallas as pl
from jax.experimental.pallas import tpu as pltpu
from jax.sharding import Mesh
from jax.sharding import PartitionSpec as P

QBLOCK = 128

BETA_ONE = 0.9
BETA_TWO = 0.95
CORR_ONE = 1.0 - 0.9**10
CORR_TWO = 1.0 - 0.95**10
EPSILON = 1e-08
RATE = 0.002

BF = jnp.bfloat16
F32 = jnp.float32
AXES = ("yh", "core", "yl", "z", "x")
N_Y = 4
N_X = 4


def dequant(quant, scale):
    shaped = quant.astype(F32).reshape(quant.shape[0], quant.shape[1], -1, QBLOCK)
    return (shaped * scale[..., None]).reshape(quant.shape)


def adam_update(weight, grad, first_q, first_scale, second_q, second_scale):
    first = BETA_ONE * dequant(first_q, first_scale) + (1.0 - BETA_ONE) * grad
    second = BETA_TWO * dequant(second_q, second_scale) + (1.0 - BETA_TWO) * grad * grad
    step = first / CORR_ONE / (jnp.sqrt(second / CORR_TWO) + EPSILON)
    return (step, weight - RATE * step)


def swap(value):
    return lax.ppermute(value, "core", [(0, 1), (1, 0)])


def cross(value, other_core):
    flip = 3 if other_core else 2
    return lax.ppermute(value, ("yh", "core"), [(i, i ^ flip) for i in range(4)])


def shift(value, k, inner):
    n_z = lax.axis_size("z")

    def number(y, core, z, x):
        return (((y // 2 * 2 + core) * 2 + y % 2) * n_z + z) * N_X + x

    pairs = []
    for core in range(2):
        for y in range(N_Y):
            for z in range(n_z):
                for x in range(N_X):
                    if (core == 0) == inner:
                        target = number(y, core, z, (x + k) % N_X)
                    else:
                        target = number((y + k) % N_Y, core, z, x)
                    pairs.append((number(y, core, z, x), target))
    return lax.ppermute(value, AXES, pairs)


def place(spot_ref, j, k, away):
    core = spot_ref[0]
    outer = (spot_ref[2] + (j if away else N_Y - j)) % N_Y
    inner = (spot_ref[1] + (k if away else N_X - k)) % N_X
    y = jnp.where(core == 0, outer, inner)
    x = jnp.where(core == 0, inner, outer)
    return y % 2, x, y // 2


def in_hbm(value):
    return pltpu.with_memory_space_constraint(value, pltpu.HBM)


ANY = "any"
SMEM = "smem"
VMEM = "vmem"


def call(kernel, outs, *args, scratch=(), mib=8, places=None):
    spec = {
        ANY: pl.BlockSpec(memory_space=pl.ANY),
        SMEM: pl.BlockSpec(memory_space=pltpu.SMEM),
        VMEM: pl.BlockSpec(memory_space=pltpu.VMEM),
    }
    return pl.pallas_call(
        kernel,
        out_shape=[
            pltpu.HBM(shape, dtype) if where == ANY else jax.ShapeDtypeStruct(shape, dtype)
            for shape, dtype, where in outs
        ],
        in_specs=[spec[where] for where in (places or [VMEM] * len(args))],
        out_specs=[spec[where] for _, _, where in outs],
        scratch_shapes=list(scratch),
        compiler_params=pltpu.CompilerParams(vmem_limit_bytes=mib << 20),
    )(*args)


def pack_kernel(*refs):
    *in_refs, out_ref = refs
    for k, in_ref in enumerate(in_refs):
        out_ref[k] = in_ref[...]


def gather_blocks(block):
    parts = [block] + [shift(block, k, True) for k in (1, 3, 2)]
    parts = [parts[0], parts[1], parts[3], parts[2]]
    (packed,) = call(pack_kernel, [((N_X,) + block.shape, BF, VMEM)], *parts)
    far = [shift(packed, k, False) for k in (1, 3, 2)]
    return [packed, far[0], far[2], far[1]]


def load_whole(spot_ref, block_refs, whole_ref, sems):
    copies = []
    for j in range(N_Y):
        for k in range(N_X):
            low, x, high = place(spot_ref, j, k, False)
            copies.append(
                pltpu.make_async_copy(
                    block_refs[j].at[k], whole_ref.at[low, :, x, high], sems.at[j * N_X + k]
                )
            )
    return copies


def rows_kernel(spot_ref, route_ref, tokens_ref, x_ref, across_ref, buf_ref, sems):
    count, depth = x_ref.shape
    low_n, n_z, n_x, high_n, rows, _ = buf_ref.shape
    step = 256
    core = spot_ref[0]
    places = lax.broadcasted_iota(jnp.int32, (tokens_ref.shape[0], count), 0)
    hot = jnp.where(places == route_ref[...], 1.0, 0.0).astype(BF).T
    copies = []
    for low in range(low_n):
        for d in range(low * depth // low_n, (low + 1) * depth // low_n, step):
            picked = jnp.dot(hot, tokens_ref[:, d : d + step], preferred_element_type=F32).astype(BF)
            x_ref[:, d : d + step] = picked
            turned = picked.T
            for g in range(step // rows):
                index = d // rows + g
                high = index % high_n
                x = index // high_n % n_x
                z = index // high_n // n_x % n_z
                buf_ref[low, z, x, high] = turned[g * rows : (g + 1) * rows]
        for high in range(high_n):
            for x in range(n_x):
                y = 2 * high + low
                j = (jnp.where(core == 0, y, x) - spot_ref[2] + N_Y) % N_Y
                k = (jnp.where(core == 0, x, y) - spot_ref[1] + N_X) % N_X
                copies.append(
                    pltpu.make_async_copy(buf_ref.at[low, :, x, high], across_ref.at[j, k], sems.at[len(copies)])
                )
                copies[-1].start()
    for copy in copies:
        copy.wait()


def gate_kernel(spot_ref, mine_ref, other_ref, cot_mine_ref, cot_other_ref,
                across_mine_ref, across_other_ref, g0, g1, g2, g3, o0, o1, o2, o3, dmine_ref, dother_ref, whole_out_ref,
                whole_ref, x_ref, cot_ref, turned_ref, d_ref, part_ref, in_sems, w_sems, t_sems, out_sems):
    low_n, n_z, n_x, high_n, rows, feature = whole_ref.shape
    count, depth = mine_ref.shape
    step = 256
    core = spot_ref[0]
    w_copies = load_whole(spot_ref, (g0, g1, g2, g3), whole_ref, w_sems)
    loads = [
        pltpu.make_async_copy(mine_ref, x_ref.at[pl.ds(0, count)], in_sems.at[0]),
        pltpu.make_async_copy(cot_mine_ref.at[core], cot_ref.at[pl.ds(0, count)], in_sems.at[1]),
        pltpu.make_async_copy(other_ref, x_ref.at[pl.ds(count, count)], in_sems.at[2]),
        pltpu.make_async_copy(cot_other_ref.at[core], cot_ref.at[pl.ds(count, count)], in_sems.at[3]),
    ]
    order = (1, 3, 2, 0)
    t_loads = [
        [
            pltpu.make_async_copy(ref.at[j], turned_ref.at[half, j], t_sems.at[half, j])
            for half, ref in enumerate((across_mine_ref, across_other_ref))
        ]
        for j in order
    ]
    for copy in w_copies + loads[:2]:
        copy.start()
    for copy in w_copies:
        copy.wait()
    for copy in loads[2:] + [copy for pair in t_loads for copy in pair]:
        copy.start()
    whole_out = pltpu.make_async_copy(whole_ref, whole_out_ref, in_sems.at[4])
    whole_out.start()
    whole = whole_ref[...].reshape(depth, feature)
    outs = [whole_out]
    for half in range(2):
        loads[2 * half].wait()
        loads[2 * half + 1].wait()
        for r in range(half * count, (half + 1) * count, step):
            gate = jnp.dot(x_ref[r : r + step, :], whole, preferred_element_type=F32)
            sig = jax.nn.sigmoid(gate)
            cot = cot_ref[r : r + step, :].astype(F32)
            d_ref[r : r + step, :] = (cot * sig * (1.0 + gate * (1.0 - sig))).astype(BF)
        outs.append(
            pltpu.make_async_copy(
                d_ref.at[pl.ds(half * count, count)], (dmine_ref, dother_ref)[half], in_sems.at[5 + half]
            )
        )
        outs[-1].start()
    for i, j in enumerate(order):
        for copy in t_loads[i]:
            copy.wait()
        for k in range(0, N_X, 2):
            part = None
            for half in range(2):
                turned = turned_ref[half, j, k : k + 2].reshape(2 * n_z * rows, count)
                product = jnp.dot(turned, d_ref[half * count : (half + 1) * count, :], preferred_element_type=F32)
                part = product if part is None else part + product
            part_ref[j, k : k + 2] = part.astype(BF).reshape(2, n_z, rows, feature)
        outs.append(pltpu.make_async_copy(part_ref.at[j], (o0, o1, o2, o3)[j], out_sems.at[j]))
        outs[-1].start()
    for copy in outs:
        copy.wait()


def token_kernel(routes_ref, dmine_ref, dother_ref, whole_ref, other_ref, out_ref, placed_ref):
    count = dmine_ref.shape[0]
    step = 256
    turned = (((1,), (1,)), ((), ()))
    for t in range(0, out_ref.shape[0], step):
        places = t + lax.broadcasted_iota(jnp.int32, (step, count), 0)
        for e, d_ref in enumerate((dmine_ref, dother_ref)):
            hot = jnp.where(places == routes_ref[e : e + 1, :], 1.0, 0.0).astype(BF)
            placed_ref[e] = jnp.dot(hot, d_ref[...], preferred_element_type=F32).astype(BF)
        for d in range(0, out_ref.shape[1], 2 * step):
            at = slice(d, d + 2 * step)
            total = lax.dot_general(placed_ref[0], whole_ref[at, :], turned, preferred_element_type=F32)
            total = total + lax.dot_general(placed_ref[1], other_ref[at, :], turned, preferred_element_type=F32)
            out_ref[t : t + step, at] = total.astype(BF)


def sum_outer_kernel(a, b, c, d, o0, o1, o2, o3):
    for k, out_ref in enumerate((o0, o1, o2, o3)):
        total = a[k].astype(F32) + b[k].astype(F32) + c[k].astype(F32) + d[k].astype(F32)
        out_ref[...] = total.astype(BF)


def sum_inner_kernel(a, b, c, d, out_ref):
    total = a[...].astype(F32) + b[...].astype(F32) + c[...].astype(F32) + d[...].astype(F32)
    out_ref[...] = total.astype(BF)


def adam_kernel(total_rows):
    def kernel(got_ref, weight_ref, first_ref, second_ref, grad_ref, out_ref):
        total = got_ref[0].astype(F32)
        for k in range(1, got_ref.shape[0]):
            total = total + got_ref[k].astype(F32)
        grad = total / total_rows
        grad_ref[...] = grad
        first = first_ref[...] + (1.0 - BETA_ONE) * grad
        second = second_ref[...] + (1.0 - BETA_TWO) * grad * grad
        step = first / CORR_ONE / (jnp.sqrt(second / CORR_TWO) + EPSILON)
        new = (weight_ref[...] - RATE * step).astype(BF)
        for k in range(out_ref.shape[0]):
            out_ref[k] = new

    return kernel


def next_other_kernel(spot_ref, x_ref, g0, g1, g2, g3, out_ref, whole_ref, sems):
    copies = load_whole(spot_ref, (g0, g1, g2, g3), whole_ref, sems)
    for copy in copies:
        copy.start()
    for copy in copies:
        copy.wait()
    whole = whole_ref[...].reshape(x_ref.shape[1], out_ref.shape[1])
    out_ref[...] = jnp.dot(x_ref[...], whole, preferred_element_type=F32).astype(BF)


def next_mine_kernel(x_ref, whole_ref, out_ref):
    out_ref[...] = jnp.dot(x_ref[...], whole_ref[...], preferred_element_type=F32).astype(BF)


def pair(mine, other, core):
    return jnp.where(core == 0, jnp.stack([mine, other]), jnp.stack([other, mine]))


def on_device(tokens, route, cotangent, weight, first_q, first_scale, second_q, second_scale):
    n_z = lax.axis_size("z")
    core = lax.axis_index("core")
    high = lax.axis_index("yh")
    y = high * 2 + lax.axis_index("yl")
    x = lax.axis_index("x")
    spot = jnp.stack([core, jnp.where(core == 0, x, y), jnp.where(core == 0, y, x)]).astype(jnp.int32)
    rows_here = route.shape[1]
    depth = tokens.shape[1]
    feature = cotangent.shape[2]
    total_rows = rows_here * 2 * N_Y * n_z * N_X
    owned = weight.shape[1]
    half = owned // 2
    block_shape = (n_z, half, feature)
    natural = (2, n_z, N_X, 2, half)

    def mine_of(array):
        return lax.dynamic_index_in_dim(array, core, 0, keepdims=False)

    def other_of(array):
        return lax.dynamic_index_in_dim(array, 1 - core, 0, keepdims=False)

    def part_of(array):
        return lax.dynamic_slice_in_dim(mine_of(array), high * half, half, 0)

    def over_z(blocks):
        return lax.all_to_all(blocks, "z", 0, 0, tiled=True)

    weight_part = part_of(weight)
    along_z = over_z(jnp.broadcast_to(weight_part.astype(BF)[None], block_shape))
    tokens_far, route_far, cot_far = swap(tokens), swap(route), swap(cotangent)
    tokens_b, route_b, route_far = lax.optimization_barrier((tokens, route, route_far))
    gathered = gather_blocks(along_z)
    route_mine = mine_of(route_b)
    route_other = other_of(route_b)

    def rows_of(routes, from_tokens):
        return call(
            rows_kernel,
            [((rows_here, depth), BF, VMEM), ((N_Y, N_X, n_z, half, rows_here), BF, ANY)],
            spot,
            routes[None],
            from_tokens,
            scratch=[pltpu.VMEM(natural + (rows_here,), BF), pltpu.SemaphoreType.DMA((N_Y * N_X,))],
            mib=16,
            places=[SMEM, VMEM, VMEM],
        )

    x_mine, across_mine = rows_of(route_mine, tokens_b)
    x_other, across_other = rows_of(mine_of(route_far), tokens_far)
    first_part = BETA_ONE * dequant(part_of(first_q)[None], part_of(first_scale)[None])[0]
    second_part = BETA_TWO * dequant(part_of(second_q)[None], part_of(second_scale)[None])[0]
    *gathered, x_mine, x_other, cot_far, first_part, second_part = lax.optimization_barrier(
        (*gathered, x_mine, x_other, cot_far, first_part, second_part)
    )

    b0, b1, b2, b3, dmine, dother, whole = call(
        gate_kernel,
        [((N_X,) + block_shape, BF, ANY)] * 4
        + [((rows_here, feature), BF, ANY)] * 2
        + [(natural + (feature,), BF, ANY)],
        spot,
        in_hbm(x_mine),
        in_hbm(x_other),
        in_hbm(cotangent),
        in_hbm(cot_far),
        in_hbm(across_mine),
        in_hbm(across_other),
        *gathered,
        scratch=[
            pltpu.VMEM(natural + (feature,), BF),
            pltpu.VMEM((2 * rows_here, depth), BF),
            pltpu.VMEM((2 * rows_here, feature), BF),
            pltpu.VMEM((2, N_Y, N_X, n_z, half, rows_here), BF),
            pltpu.VMEM((2 * rows_here, feature), BF),
            pltpu.VMEM((N_Y, N_X) + block_shape, BF),
            pltpu.SemaphoreType.DMA((7,)),
            pltpu.SemaphoreType.DMA((N_Y * N_X,)),
            pltpu.SemaphoreType.DMA((2, N_Y)),
            pltpu.SemaphoreType.DMA((N_Y,)),
        ],
        mib=24,
        places=[SMEM] + [ANY] * 10,
    )
    whole = whole.reshape(depth, feature)
    got = [shift(block, k, False) for block, k in ((b1, 1), (b3, 3), (b2, 2))]
    p0, p1, p2, p3 = call(sum_outer_kernel, [(block_shape, BF, VMEM)] * 4, b0, *got)
    got = [shift(block, k, True) for block, k in ((p1, 1), (p3, 3), (p2, 2))]
    (part,) = call(sum_inner_kernel, [(block_shape, BF, VMEM)], p0, *got)
    got_z = over_z(part)
    grad, new_blocks = call(
        adam_kernel(total_rows),
        [((half, feature), F32, VMEM), (block_shape, BF, VMEM)],
        got_z,
        weight_part,
        first_part,
        second_part,
    )
    new_along_z = over_z(new_blocks)
    new_along_z, grad, whole, dother = lax.optimization_barrier((new_along_z, grad, whole, dother))
    new_gathered = gather_blocks(new_along_z)

    mine_half = pair(grad, swap(grad), core)
    far_half = pair(cross(grad, False), cross(grad, True), core)
    both = jnp.where(
        high == 0,
        jnp.concatenate([mine_half, far_half], axis=1),
        jnp.concatenate([far_half, mine_half], axis=1),
    )
    step_dir, new_weight = adam_update(weight, both, first_q, first_scale, second_q, second_scale)
    other_whole = swap(whole)
    other_rows = swap(dother)
    (token_grad,) = call(
        token_kernel,
        [(tokens.shape, BF, VMEM)],
        jnp.stack([route_mine, route_other]),
        dmine,
        other_rows,
        whole,
        other_whole,
        scratch=[pltpu.VMEM((2, 256, feature), BF)],
        mib=14,
    )
    *new_gathered, step_dir, new_weight, token_grad = lax.optimization_barrier(
        (*new_gathered, step_dir, new_weight, token_grad)
    )

    next_other, new_whole = call(
        next_other_kernel,
        [((rows_here, feature), BF, VMEM), (natural + (feature,), BF, VMEM)],
        spot,
        x_other,
        *new_gathered,
        scratch=[pltpu.SemaphoreType.DMA((N_Y * N_X,))],
        places=[SMEM, VMEM] + [ANY] * 4,
    )
    next_other = swap(next_other)
    (next_mine,) = call(
        next_mine_kernel,
        [((rows_here, feature), BF, VMEM)],
        x_mine,
        new_whole.reshape(depth, feature),
    )
    next_gate = pair(next_mine, next_other, core)
    return (token_grad, step_dir, new_weight, next_gate)


def solution(mesh):
    split = Mesh(mesh.devices.reshape(2, 2, 2, 8, 4), ("yh", "core", "yl", "z", "x"))
    rep = ("yh", "core")
    ep = ("yl", "z", "x")
    every = rep + ep
    in_specs = (
        P(every, None),
        P(None, every),
        P(None, every, None),
        P(None, ep, None),
        P(None, ep, None),
        P(None, ep, None),
        P(None, ep, None),
        P(None, ep, None),
    )
    out_specs = (
        P(every, None),
        P(None, ep, None),
        P(None, ep, None),
        P(None, every, None),
    )
    return jax.shard_map(
        on_device, mesh=split, in_specs=in_specs, out_specs=out_specs, check_vma=False
    )
```

time: 192 us -> 149 us (0.78)
  blocking collectives: 58.2 us -> 24.4 us
  Pallas kernels: 0 us -> 31.6 us
  matrix products: 28.9 us -> 0 us
  local copies, waits for them, and re-layouts: 30.7 us -> 13 us
  starting transfers between devices: 34.6 us -> 46.2 us
  other arithmetic: 10.8 us -> 4.83 us
    all_to_all x3 -> x2, blocking collectives: 58.2 us -> 24.4 us  [over_z(): return lax.all_to_all(blocks, 'z', 0, 0, tiled=True)]
    pallas_call x0 -> x11, Pallas kernels: none -> 31.6 us  [call(): pl.pallas_call(kernel, out_shape=[pltpu.HBM(shape, dtype) if where == ANY...]
    dot_general x5 -> x0, matrix products: 28.9 us -> none  [the longest x1 7.46 us: on_device(): jnp.einsum('tf,df->td', at_tokens(route_other, other_rows), other_whole,...]
    ppermute x1 -> x20, starting transfers between devices: 2.99 us -> 25.6 us  [the longest x18 21.9 us: shift(): return lax.ppermute(value, AXES, pairs)]
    ppermute x1 -> x20, waiting for transfers between devices: 0.01 us -> 20.1 us  [the longest x18 19.6 us: shift(): return lax.ppermute(value, AXES, pairs)]
    all_to_all x3 -> x1, waiting for transfers between devices: 27.1 us -> 7.02 us  [over_z(): return lax.all_to_all(blocks, 'z', 0, 0, tiled=True)]
    all_to_all x3 -> x1, starting transfers between devices: 14.6 us -> 3.5 us  [over_z(): return lax.all_to_all(blocks, 'z', 0, 0, tiled=True)]
    gather x2 -> x0, local copies, waits for them, and re-layouts: 6.6 us -> none  [the longest x1 3.3 us: on_device(): tokens[route_other]]
  transfers between devices with their start and end apart: 10 -> 28, of which waited for: 3 -> 11; matrix products, arithmetic and copies ran while one was open for 23% -> 8% of each run, Pallas kernels for 0% -> 12%
where the time goes in v3:
time: 149 us; the launch traced here: 148 us
  starting transfers between devices  46.2 us (31%)
  Pallas kernels  31.6 us (21%)
  waiting for transfers between devices  27.4 us (18%)
  blocking collectives  24.4 us (16%)
  local copies, waits for them, and re-layouts  13 us (9%)
  other arithmetic  4.83 us (3%)
    pallas_call x11, Pallas kernels, call(): pl.pallas_call(kernel, out_shape=[pltpu.HBM(shape, dtype) if where == ANY...  31.6 us
    all_to_all x2, blocking collectives, over_z(): return lax.all_to_all(blocks, 'z', 0, 0, tiled=True)  24.4 us
    ppermute x18, starting transfers between devices, shift(): return lax.ppermute(value, AXES, pairs)  21.9 us
    ppermute x18, waiting for transfers between devices, shift(): return lax.ppermute(value, AXES, pairs)  19.6 us
    ppermute x7, starting transfers between devices, swap(): return lax.ppermute(value, 'core', [(0, 1), (1, 0)])  17.1 us
    all_to_all x1, waiting for transfers between devices, over_z(): return lax.all_to_all(blocks, 'z', 0, 0, tiled=True)  7.02 us
    unnamed x22, local copies, waits for them, and re-layouts  5.81 us
    mul x10, local copies, waits for them, and re-layouts, dequant(): return (shaped * scale[..., None]).reshape(quant.shape)  4.15 us
  transfers between devices with their start and end apart: 28, of which 11 were waited for; matrix products, arithmetic and copies ran while one was open for 8% of the time, Pallas kernels for 12%

profile of v3, /device:TPU:1, one launch (start us, length us, event | category | flops | bytes accessed | tf_op | source)
XLA Modules:
  0.0 148.3 jit_solution(6998035697502293822)
XLA Ops:
  0.6 3.3 %collective-permute-start.7 = (bf16[768,2048]{1,0:T(8,128)(2,1)}, bf16[768,2048]{1,0:T(8,128)(2,1)S(1)}, u32[]{:S(2)}, u32[]{:S(2)}) collective-permute-start(bf16[768,2048]{1,0:T(8,128)(2,1)} %tokens_ref), channel_id=1, source_target_pairs={{0,64},{64,0},{1,65},{65,1},{2,66},{66,2},{3,67},{67,3},{4,68},{68... | collective-permute-start | bytes 9437192 | tf_op jit(solution)/shard_map/ppermute | solution.py:38
  4.1 0.8 fusion.7
  4.9 14.1 %all_to_all.15.refs_0_ = bf16[8,16,512]{2,1,0:T(8,128)(2,1)S(1)} all-to-all(bf16[8,16,512]{2,1,0:T(8,128)(2,1)S(1)} %broadcast_in_dim.5), channel_id=1, replica_groups=mesh['yh'=2,'core'=2,'yl'=2,'z'=8,'x'=4] {'z'}, dimensions={0} | all-to-all | bytes 262144 | tf_op jit(solution)/shard_map/all_to_all | solution.py:311
  19.0 1.3 collective-permute-start
  20.3 2.6 %collective-permute-start.1 = (bf16[8,16,512]{2,1,0:T(8,128)(2,1)S(1)}, bf16[8,16,512]{2,1,0:T(8,128)(2,1)S(1)}, u32[]{:S(2)}, u32[]{:S(2)}) collective-permute-start(bf16[8,16,512]{2,1,0:T(8,128)(2,1)S(1)} %all_to_all.15.refs_0_), channel_id=1, source_target_pairs={{0,2},{1,3},{2,0},{3,1},{4,6},{5,7},{6,4},{7,5},{8,10},{9,11},{10,... | collective-permute-start | bytes 393224 | tf_op jit(solution)/shard_map/ppermute | solution.py:62
  22.8 1.1 collective-permute-start.2
  24.7 2.9 %collective-permute-start.6 = (s32[2,512]{1,0:T(2,128)}, s32[2,512]{1,0:T(2,128)}, u32[]{:S(2)}, u32[]{:S(2)}) collective-permute-start(s32[2,512]{1,0:T(2,128)} %param.9), channel_id=1, source_target_pairs={{0,64},{64,0},{1,65},{65,1},{2,66},{66,2},{3,67},{67,3},{4,68},{68... | collective-permute-start | bytes 12296 | tf_op jit(solution)/shard_map/ppermute | solution.py:38
  29.1 0.9 shard_map.111.g0
  30.4 1.9 %collective-permute-start.4 = (bf16[4,8,16,512]{3,2,1,0:T(8,128)(2,1)S(1)}, bf16[4,8,16,512]{3,2,1,0:T(8,128)(2,1)S(1)}, u32[]{:S(2)}, u32[]{:S(2)}) collective-permute-start(bf16[4,8,16,512]{3,2,1,0:T(8,128)(2,1)S(1)} %shard_map.111.g0), channel_id=1, source_target_pairs={{0,128},{1,129},{2,130},{3,131},{4,132},{5,133},{6,134},{7,135},{8... | collective-permute-start | bytes 1572872 | tf_op jit(solution)/shard_map/ppermute | solution.py:62
  32.3 1.2 collective-permute-start.5
  33.6 0.8 mul.116
  34.4 0.8 fusion.5
  35.3 0.8 constant_dynamic-slice_fusion
  36.0 1.9 %copy-done.4 = bf16[768,2048]{1,0:T(8,128)(2,1)S(1)} copy-done((bf16[768,2048]{1,0:T(8,128)(2,1)S(1)}, bf16[768,2048]{1,0:T(8,128)(2,1)}, u32[]{:S(2)}) %copy-start.4) | copy-done | bytes 3145752
  37.9 3.5 %shard_map.112 = (bf16[512,2048]{1,0:T(8,128)(2,1)S(1)}, bf16[4,4,8,16,512]{4,3,2,1,0:T(8,128)(2,1)}) custom-call(s32[3]{0:T(128)S(1)} %pad_add_fusion.1.spot_ref, s32[1,512]{1,0:T(1,128)S(1)} %get-tuple-element.91.route_ref, bf16[768,2048]{1,0:T(8,128)(2,1)S(1)} %copy-done.4), custom_call_target="tpu_custom_call" | custom-call | tf_op jit(solution)/shard_map/pallas_call | solution.py:89
  41.5 1.3 copy-done
  43.5 3.6 %shard_map.113 = (bf16[512,2048]{1,0:T(8,128)(2,1)S(1)}, bf16[4,4,8,16,512]{4,3,2,1,0:T(8,128)(2,1)}) custom-call(s32[3]{0:T(128)S(1)} %pad_add_fusion.1.spot_ref, s32[1,512]{1,0:T(1,128)S(1)} %constant_dynamic-slice_fusion.1.route_ref, bf16[768,2048]{1,0:T(8,128)(2,1)S(1)} %collective-permute-done.7.tokens_ref), custom_call_target="tpu_custom_call" | custom-call | tf_op jit(solution)/shard_map/pallas_call | solution.py:89
  47.2 1.3 copy-done.2
  48.5 10.8 %shard_map.114 = (bf16[4,8,16,512]{3,2,1,0:T(8,128)(2,1)}, bf16[4,8,16,512]{3,2,1,0:T(8,128)(2,1)}, bf16[4,8,16,512]{3,2,1,0:T(8,128)(2,1)}, bf16[4,8,16,512]{3,...) custom-call(s32[3]{0:T(128)S(1)} %pad_add_fusion.1.spot_ref, ...), custom_call_target="tpu_custom_call" | custom-call | tf_op jit(solution)/shard_map/pallas_call | solution.py:89
  59.6 1.9 %collective-permute-start.11 = (bf16[4,8,16,512]{3,2,1,0:T(8,128)(2,1)}, bf16[4,8,16,512]{3,2,1,0:T(8,128)(2,1)S(1)}, u32[]{:S(2)}, u32[]{:S(2)}) collective-permute-start(bf16[4,8,16,512]{3,2,1,0:T(8,128)(2,1)} %get-tuple-element.63), channel_id=1, source_target_pairs={{0,128},{1,129},{2,130},{3,131},{4,132},{5,133},{6,134},{7,135},{8... | collective-permute-start | bytes 1572872 | tf_op jit(solution)/shard_map/ppermute | solution.py:62
  61.9 6.0 %collective-permute-done.10.c = bf16[4,8,16,512]{3,2,1,0:T(8,128)(2,1)S(1)} collective-permute-done((bf16[4,8,16,512]{3,2,1,0:T(8,128)(2,1)}, bf16[4,8,16,512]{3,2,1,0:T(8,128)(2,1)S(1)}, u32[]{:S(2)}, u32[]{:S(2)}) %collective-permute-start.10) | collective-permute-done | bytes 524320 | tf_op jit(solution)/shard_map/ppermute | solution.py:62
  67.9 1.7 %collective-permute-done.11.d = bf16[4,8,16,512]{3,2,1,0:T(8,128)(2,1)S(1)} collective-permute-done((bf16[4,8,16,512]{3,2,1,0:T(8,128)(2,1)}, bf16[4,8,16,512]{3,2,1,0:T(8,128)(2,1)S(1)}, u32[]{:S(2)}, u32[]{:S(2)}) %collective-permute-start.11) | collective-permute-done | bytes 524320 | tf_op jit(solution)/shard_map/ppermute | solution.py:62
  69.7 5.6 %collective-permute-done.9.b = bf16[4,8,16,512]{3,2,1,0:T(8,128)(2,1)S(1)} collective-permute-done((bf16[4,8,16,512]{3,2,1,0:T(8,128)(2,1)}, bf16[4,8,16,512]{3,2,1,0:T(8,128)(2,1)S(1)}, u32[]{:S(2)}, u32[]{:S(2)}) %collective-permute-start.9) | collective-permute-done | bytes 524320 | tf_op jit(solution)/shard_map/ppermute | solution.py:62
  75.2 1.0 copy-done.6
  76.5 1.2 collective-permute-start.12
  77.7 1.6 %collective-permute-start.13 = (bf16[8,16,512]{2,1,0:T(8,128)(2,1)S(1)}, bf16[8,16,512]{2,1,0:T(8,128)(2,1)S(1)}, u32[]{:S(2)}, u32[]{:S(2)}) collective-permute-start(bf16[8,16,512]{2,1,0:T(8,128)(2,1)S(1)} %get-tuple-element.66), channel_id=1, source_target_pairs={{0,3},{1,0},{2,1},{3,2},{4,7},{5,4},{6,5},{7,6},{8,11},{9,8},{10,9... | collective-permute-start | bytes 393224 | tf_op jit(solution)/shard_map/ppermute | solution.py:62
  79.3 1.3 collective-permute-start.14
  80.6 1.0 collective-permute-done.12.b
  81.7 3.0 %collective-permute-done.14.d = bf16[8,16,512]{2,1,0:T(8,128)(2,1)S(1)} collective-permute-done((bf16[8,16,512]{2,1,0:T(8,128)(2,1)S(1)}, bf16[8,16,512]{2,1,0:T(8,128)(2,1)S(1)}, u32[]{:S(2)}, u32[]{:S(2)}) %collective-permute-start.14) | collective-permute-done | bytes 131104 | tf_op jit(solution)/shard_map/ppermute | solution.py:62
  85.3 3.5 %all-to-all-start.1 = ((bf16[8,16,512]{2,1,0:T(8,128)(2,1)}), bf16[8,16,512]{2,1,0:T(8,128)(2,1)S(1)}, u32[]{:S(2)}, u32[]{:S(2)}) async-start(bf16[8,16,512]{2,1,0:T(8,128)(2,1)} %shard_map.116), calls=%async_computation.1 | async-start | bytes 262144 | tf_op jit(solution)/shard_map/all_to_all | solution.py:311
  88.9 0.8 dynamic-slice_bitcast_fusion.weight_ref
  89.7 7.0 %all-to-all-done.1.got_ref = bf16[8,16,512]{2,1,0:T(8,128)(2,1)S(1)} async-done(((bf16[8,16,512]{2,1,0:T(8,128)(2,1)}), bf16[8,16,512]{2,1,0:T(8,128)(2,1)S(1)}, u32[]{:S(2)}, u32[]{:S(2)}) %all-to-all-start.1) | async-done | bytes 131104 | tf_op jit(solution)/shard_map/all_to_all | solution.py:311
  96.8 10.3 %all_to_all.16.refs_0_ = bf16[8,16,512]{2,1,0:T(8,128)(2,1)S(1)} all-to-all(bf16[8,16,512]{2,1,0:T(8,128)(2,1)S(1)} %get-tuple-element.70), channel_id=1, replica_groups=mesh['yh'=2,'core'=2,'yl'=2,'z'=8,'x'=4] {'z'}, dimensions={0} | all-to-all | bytes 262144 | tf_op jit(solution)/shard_map/all_to_all | solution.py:311
  107.1 8.6 %collective-permute-start.25 = (bf16[2048,512]{1,0:T(8,128)(2,1)S(1)}, bf16[2048,512]{1,0:T(8,128)(2,1)}, u32[]{:S(2)}, u32[]{:S(2)}) collective-permute-start(bf16[2048,512]{1,0:T(8,128)(2,1)S(1)} %bitcast.35), channel_id=1, source_target_pairs={{0,64},{64,0},{1,65},{65,1},{2,66},{66,2},{3,67},{67,3},{4,68},{68... | collective-permute-start | bytes 6291464 | tf_op jit(solution)/shard_map/ppermute | solution.py:38
  115.7 1.7 %collective-permute-start.15 = (bf16[8,16,512]{2,1,0:T(8,128)(2,1)S(1)}, bf16[8,16,512]{2,1,0:T(8,128)(2,1)S(1)}, u32[]{:S(2)}, u32[]{:S(2)}) collective-permute-start(bf16[8,16,512]{2,1,0:T(8,128)(2,1)S(1)} %all_to_all.16.refs_0_), channel_id=1, source_target_pairs={{0,1},{1,2},{2,3},{3,0},{4,5},{5,6},{6,7},{7,4},{8,9},{9,10},{10,1... | collective-permute-start | bytes 393224 | tf_op jit(solution)/shard_map/ppermute | solution.py:62
  117.7 2.1 %collective-permute-start.17 = (bf16[8,16,512]{2,1,0:T(8,128)(2,1)S(1)}, bf16[8,16,512]{2,1,0:T(8,128)(2,1)S(1)}, u32[]{:S(2)}, u32[]{:S(2)}) collective-permute-start(bf16[8,16,512]{2,1,0:T(8,128)(2,1)S(1)} %all_to_all.16.refs_0_), channel_id=1, source_target_pairs={{0,3},{1,0},{2,1},{3,2},{4,7},{5,4},{6,5},{7,6},{8,11},{9,8},{10,9... | collective-permute-start | bytes 393224 | tf_op jit(solution)/shard_map/ppermute | solution.py:62
  119.8 0.9 collective-permute-start.22
  121.0 2.8 %collective-permute-start.23 = (f32[16,512]{1,0:T(8,128)S(1)}, f32[16,512]{1,0:T(8,128)S(1)}, u32[]{:S(2)}, u32[]{:S(2)}) collective-permute-start(f32[16,512]{1,0:T(8,128)S(1)} %get-tuple-element.75), channel_id=1, source_target_pairs={{0,192},{64,128},{128,64},{192,0},{1,193},{65,129},{129,65},{193,1... | collective-permute-start | bytes 98312 | tf_op jit(solution)/shard_map/ppermute | solution.py:43
  126.2 1.7 %collective-permute-start.19 = (bf16[4,8,16,512]{3,2,1,0:T(8,128)(2,1)S(1)}, bf16[4,8,16,512]{3,2,1,0:T(8,128)(2,1)S(1)}, u32[]{:S(2)}, u32[]{:S(2)}) collective-permute-start(bf16[4,8,16,512]{3,2,1,0:T(8,128)(2,1)S(1)} %shard_map.118.g0), channel_id=1, source_target_pairs={{0,128},{1,129},{2,130},{3,131},{4,132},{5,133},{6,134},{7,135},{8... | collective-permute-start | bytes 1572872 | tf_op jit(solution)/shard_map/ppermute | solution.py:62
  127.8 0.9 collective-permute-start.20
  128.7 0.8 maximum_select_fusion.2
  129.6 1.9 %multiply_subtract_fusion = (f32[2,32,512]{2,1,0:T(8,128)}, f32[2,32,512]{2,1,0:T(8,128)}) fusion(f32[2,32,512]{2,1,0:T(8,128)} %param.11, f32[2,32,512]{2,1,0:T(8,128)} %mul.129, s32[2,32,512]{2,1,0:T(8,128)} %param.14, f32[2,16,512]{2,1,0:T(8,128)S(1)} %maximum_select_fusion.2, f32[2,16,512]{2,1,0:T(8,128)S(1)} %maximum_select_fusion.3, pred[]{:T(512)S(6)} %eq.5, ...), kind=kLoop, calls=%fused_computation.8 | loop fusion | flops 655360 | bytes 1048577 | tf_op jit(solution)/shard_map/sub | solution.py:34
  131.5 7.9 %shard_map.119 = bf16[768,2048]{1,0:T(8,128)(2,1)} custom-call(s32[2,512]{1,0:T(2,128)S(1)} %pad_add_fusion.routes_ref, bf16[512,512]{1,0:T(8,128)(2,1)S(1)} %copy-done.7, bf16[512,512]{1,0:T(8,128)(2,1)S(1)} %collective-permute-done.24.dother_ref, bf16[2048,512]{1,0:T(8,128)(2,1)S(1)} %bitcast.36, bf16[2048,512]{1,0:T(8,128)(2,1)} %collective-permute-done.25.other_ref), custom_call_target="tpu_custom_call" | custom-call | tf_op jit(solution)/shard_map/pallas_call | solution.py:89
  139.4 1.4 collective-permute-done.18.g1
  141.5 2.6 %shard_map.120 = (bf16[512,512]{1,0:T(8,128)(2,1)S(1)}, bf16[2,8,4,2,16,512]{5,4,3,2,1,0:T(8,128)(2,1)S(1)}) custom-call(s32[3]{0:T(128)S(1)} %pad_add_fusion.1.spot_ref, bf16[512,2048]{1,0:T(8,128)(2,1)S(1)} %copy-done.3, bf16[4,8,16,512]{3,2,1,0:T(8,128)(2,1)S(1)} %shard_map.118.g0, bf16[4,8,16,512]{3,2,1,0:T(8,128)(2,1)S(1)} %collective-permute-done.18.g1, ...), custom_call_target="tpu_custom_call" | custom-call | tf_op jit(solution)/shard_map/pallas_call | solution.py:89
  144.0 1.6 %collective-permute-start.26 = (bf16[512,512]{1,0:T(8,128)(2,1)S(1)}, bf16[512,512]{1,0:T(8,128)(2,1)S(1)}, u32[]{:S(2)}, u32[]{:S(2)}) collective-permute-start(bf16[512,512]{1,0:T(8,128)(2,1)S(1)} %get-tuple-element.87), channel_id=1, source_target_pairs={{0,64},{64,0},{1,65},{65,1},{2,66},{66,2},{3,67},{67,3},{4,68},{68... | collective-permute-start | bytes 1572872 | tf_op jit(solution)/shard_map/ppermute | solution.py:38
  145.6 1.2 shard_map.121
  147.2 1.1 maximum_select_fusion
  (65 shorter events, 9.3 us)
Async XLA Ops:
  0.6 42.9 %collective-permute-start.7 = (bf16[768,2048]{1,0:T(8,128)(2,1)}, bf16[768,2048]{1,0:T(8,128)(2,1)S(1)}, u32[]{:S(2)}, u32[]{:S(2)}) collective-permute-start(bf16[768,2048]{1,0:T(8,128)(2,1)} %tokens_ref), channel_id=1, source_target_pairs={{0,64},{64,0},{1,65},{65,1},{2,66},{66,2},{3,67},{67,3},{4,68},{68... | collective-permute-start | bytes 9437192 | tf_op jit(solution)/shard_map/ppermute | solution.py:38
  4.0 44.5 %collective-permute-start.8 = (bf16[2,512,512]{2,1,0:T(8,128)(2,1)}, bf16[2,512,512]{2,1,0:T(8,128)(2,1)}, u32[]{:S(2)}, u32[]{:S(2)}) collective-permute-start(bf16[2,512,512]{2,1,0:T(8,128)(2,1)} %cot_mine_ref.1), channel_id=1, source_target_pairs={{0,64},{64,0},{1,65},{65,1},{2,66},{66,2},{3,67},{67,3},{4,68},{68... | collective-permute-start | bytes 3145736 | tf_op jit(solution)/shard_map/ppermute | solution.py:38
  19.0 5.7 %collective-permute-start = (bf16[8,16,512]{2,1,0:T(8,128)(2,1)S(1)}, bf16[8,16,512]{2,1,0:T(8,128)(2,1)S(1)}, u32[]{:S(2)}, u32[]{:S(2)}) collective-permute-start(bf16[8,16,512]{2,1,0:T(8,128)(2,1)S(1)} %all_to_all.15.refs_0_), channel_id=1, source_target_pairs={{0,1},{1,2},{2,3},{3,0},{4,5},{5,6},{6,7},{7,4},{8,9},{9,10},{10,1... | collective-permute-start | bytes 393224 | tf_op jit(solution)/shard_map/ppermute | solution.py:62
  20.3 8.8 %collective-permute-start.1 = (bf16[8,16,512]{2,1,0:T(8,128)(2,1)S(1)}, bf16[8,16,512]{2,1,0:T(8,128)(2,1)S(1)}, u32[]{:S(2)}, u32[]{:S(2)}) collective-permute-start(bf16[8,16,512]{2,1,0:T(8,128)(2,1)S(1)} %all_to_all.15.refs_0_), channel_id=1, source_target_pairs={{0,2},{1,3},{2,0},{3,1},{4,6},{5,7},{6,4},{7,5},{8,10},{9,11},{10,... | collective-permute-start | bytes 393224 | tf_op jit(solution)/shard_map/ppermute | solution.py:62
  22.8 6.2 %collective-permute-start.2 = (bf16[8,16,512]{2,1,0:T(8,128)(2,1)S(1)}, bf16[8,16,512]{2,1,0:T(8,128)(2,1)}, u32[]{:S(2)}, u32[]{:S(2)}) collective-permute-start(bf16[8,16,512]{2,1,0:T(8,128)(2,1)S(1)} %all_to_all.15.refs_0_), channel_id=1, source_target_pairs={{0,3},{1,0},{2,1},{3,2},{4,7},{5,4},{6,5},{7,6},{8,11},{9,8},{10,9... | collective-permute-start | bytes 393224 | tf_op jit(solution)/shard_map/ppermute | solution.py:62
  24.7 7.7 %collective-permute-start.6 = (s32[2,512]{1,0:T(2,128)}, s32[2,512]{1,0:T(2,128)}, u32[]{:S(2)}, u32[]{:S(2)}) collective-permute-start(s32[2,512]{1,0:T(2,128)} %param.9), channel_id=1, source_target_pairs={{0,64},{64,0},{1,65},{65,1},{2,66},{66,2},{3,67},{67,3},{4,68},{68... | collective-permute-start | bytes 12296 | tf_op jit(solution)/shard_map/ppermute | solution.py:38
  30.0 18.5 %collective-permute-start.3 = (bf16[4,8,16,512]{3,2,1,0:T(8,128)(2,1)S(1)}, bf16[4,8,16,512]{3,2,1,0:T(8,128)(2,1)S(1)}, u32[]{:S(2)}, u32[]{:S(2)}) collective-permute-start(bf16[4,8,16,512]{3,2,1,0:T(8,128)(2,1)S(1)} %shard_map.111.g0), channel_id=1, source_target_pairs={{0,32},{1,33},{2,34},{3,35},{4,36},{5,37},{6,38},{7,39},{8,40},{9,... | collective-permute-start | bytes 1572872 | tf_op jit(solution)/shard_map/ppermute | solution.py:62
  30.4 18.1 %collective-permute-start.4 = (bf16[4,8,16,512]{3,2,1,0:T(8,128)(2,1)S(1)}, bf16[4,8,16,512]{3,2,1,0:T(8,128)(2,1)S(1)}, u32[]{:S(2)}, u32[]{:S(2)}) collective-permute-start(bf16[4,8,16,512]{3,2,1,0:T(8,128)(2,1)S(1)} %shard_map.111.g0), channel_id=1, source_target_pairs={{0,128},{1,129},{2,130},{3,131},{4,132},{5,133},{6,134},{7,135},{8... | collective-permute-start | bytes 1572872 | tf_op jit(solution)/shard_map/ppermute | solution.py:62
  32.3 16.2 %collective-permute-start.5 = (bf16[4,8,16,512]{3,2,1,0:T(8,128)(2,1)S(1)}, bf16[4,8,16,512]{3,2,1,0:T(8,128)(2,1)S(1)}, u32[]{:S(2)}, u32[]{:S(2)}) collective-permute-start(bf16[4,8,16,512]{3,2,1,0:T(8,128)(2,1)S(1)} %shard_map.111.g0), channel_id=1, source_target_pairs={{0,160},{1,161},{2,162},{3,163},{4,164},{5,165},{6,166},{7,167},{8... | collective-permute-start | bytes 1572872 | tf_op jit(solution)/shard_map/ppermute | solution.py:62
  36.0 1.9 %copy-start.4 = (bf16[768,2048]{1,0:T(8,128)(2,1)S(1)}, bf16[768,2048]{1,0:T(8,128)(2,1)}, u32[]{:S(2)}) copy-start(bf16[768,2048]{1,0:T(8,128)(2,1)} %tokens_ref) | copy-start | bytes 9437188
  41.5 1.3 copy-start
  47.1 1.3 copy-start.2
  48.5 75.3 %copy-start.8 = (f32[2,32,4]{1,2,0:T(4,128)S(1)}, f32[2,32,4]{1,2,0:T(4,128)}, u32[]{:S(2)}) copy-start(f32[2,32,4]{1,2,0:T(4,128)} %param.13) | copy-start | bytes 3076
  48.5 75.4 %copy-start.9 = (f32[2,32,4]{1,2,0:T(4,128)S(1)}, f32[2,32,4]{1,2,0:T(4,128)}, u32[]{:S(2)}) copy-start(f32[2,32,4]{1,2,0:T(4,128)} %param.15) | copy-start | bytes 3076
  59.3 47.8 %copy-start.5 = (bf16[2,8,4,2,16,512]{5,4,3,2,1,0:T(8,128)(2,1)S(1)}, bf16[2,8,4,2,16,512]{5,4,3,2,1,0:T(8,128)(2,1)}, u32[]{:S(2)}) copy-start(bf16[2,8,4,2,16,512]{5,4,3,2,1,0:T(8,128)(2,1)} %get-tuple-element.72) | copy-start | bytes 6291460
  59.3 8.6 %collective-permute-start.10 = (bf16[4,8,16,512]{3,2,1,0:T(8,128)(2,1)}, bf16[4,8,16,512]{3,2,1,0:T(8,128)(2,1)S(1)}, u32[]{:S(2)}, u32[]{:S(2)}) collective-permute-start(bf16[4,8,16,512]{3,2,1,0:T(8,128)(2,1)} %get-tuple-element.62), channel_id=1, source_target_pairs={{0,160},{1,161},{2,162},{3,163},{4,164},{5,165},{6,166},{7,167},{8... | collective-permute-start | bytes 1572872 | tf_op jit(solution)/shard_map/ppermute | solution.py:62
  59.6 10.1 %collective-permute-start.11 = (bf16[4,8,16,512]{3,2,1,0:T(8,128)(2,1)}, bf16[4,8,16,512]{3,2,1,0:T(8,128)(2,1)S(1)}, u32[]{:S(2)}, u32[]{:S(2)}) collective-permute-start(bf16[4,8,16,512]{3,2,1,0:T(8,128)(2,1)} %get-tuple-element.63), channel_id=1, source_target_pairs={{0,128},{1,129},{2,130},{3,131},{4,132},{5,133},{6,134},{7,135},{8... | collective-permute-start | bytes 1572872 | tf_op jit(solution)/shard_map/ppermute | solution.py:62
  61.5 13.8 %collective-permute-start.9 = (bf16[4,8,16,512]{3,2,1,0:T(8,128)(2,1)}, bf16[4,8,16,512]{3,2,1,0:T(8,128)(2,1)S(1)}, u32[]{:S(2)}, u32[]{:S(2)}) collective-permute-start(bf16[4,8,16,512]{3,2,1,0:T(8,128)(2,1)} %get-tuple-element.61), channel_id=1, source_target_pairs={{0,32},{1,33},{2,34},{3,35},{4,36},{5,37},{6,38},{7,39},{8,40},{9,... | collective-permute-start | bytes 1572872 | tf_op jit(solution)/shard_map/ppermute | solution.py:62
  75.2 1.0 copy-start.6
  76.5 5.1 %collective-permute-start.12 = (bf16[8,16,512]{2,1,0:T(8,128)(2,1)S(1)}, bf16[8,16,512]{2,1,0:T(8,128)(2,1)S(1)}, u32[]{:S(2)}, u32[]{:S(2)}) collective-permute-start(bf16[8,16,512]{2,1,0:T(8,128)(2,1)S(1)} %get-tuple-element.65), channel_id=1, source_target_pairs={{0,1},{1,2},{2,3},{3,0},{4,5},{5,6},{6,7},{7,4},{8,9},{9,10},{10,1... | collective-permute-start | bytes 393224 | tf_op jit(solution)/shard_map/ppermute | solution.py:62
  77.7 3.9 %collective-permute-start.13 = (bf16[8,16,512]{2,1,0:T(8,128)(2,1)S(1)}, bf16[8,16,512]{2,1,0:T(8,128)(2,1)S(1)}, u32[]{:S(2)}, u32[]{:S(2)}) collective-permute-start(bf16[8,16,512]{2,1,0:T(8,128)(2,1)S(1)} %get-tuple-element.66), channel_id=1, source_target_pairs={{0,3},{1,0},{2,1},{3,2},{4,7},{5,4},{6,5},{7,6},{8,11},{9,8},{10,9... | collective-permute-start | bytes 393224 | tf_op jit(solution)/shard_map/ppermute | solution.py:62
  79.3 5.3 %collective-permute-start.14 = (bf16[8,16,512]{2,1,0:T(8,128)(2,1)S(1)}, bf16[8,16,512]{2,1,0:T(8,128)(2,1)S(1)}, u32[]{:S(2)}, u32[]{:S(2)}) collective-permute-start(bf16[8,16,512]{2,1,0:T(8,128)(2,1)S(1)} %get-tuple-element.67), channel_id=1, source_target_pairs={{0,2},{1,3},{2,0},{3,1},{4,6},{5,7},{6,4},{7,5},{8,10},{9,11},{10,... | collective-permute-start | bytes 393224 | tf_op jit(solution)/shard_map/ppermute | solution.py:62
  85.3 46.2 %copy-start.7 = (bf16[512,512]{1,0:T(8,128)(2,1)S(1)}, bf16[512,512]{1,0:T(8,128)(2,1)}, u32[]{:S(2)}) copy-start(bf16[512,512]{1,0:T(8,128)(2,1)} %get-tuple-element.76.dmine_ref) | copy-start | bytes 1572868
  85.3 11.3 %all-to-all-start.1 = ((bf16[8,16,512]{2,1,0:T(8,128)(2,1)}), bf16[8,16,512]{2,1,0:T(8,128)(2,1)S(1)}, u32[]{:S(2)}, u32[]{:S(2)}) async-start(bf16[8,16,512]{2,1,0:T(8,128)(2,1)} %shard_map.116), calls=%async_computation.1 | async-start | bytes 262144 | tf_op jit(solution)/shard_map/all_to_all | solution.py:311
  107.1 24.4 %collective-permute-start.25 = (bf16[2048,512]{1,0:T(8,128)(2,1)S(1)}, bf16[2048,512]{1,0:T(8,128)(2,1)}, u32[]{:S(2)}, u32[]{:S(2)}) collective-permute-start(bf16[2048,512]{1,0:T(8,128)(2,1)S(1)} %bitcast.35), channel_id=1, source_target_pairs={{0,64},{64,0},{1,65},{65,1},{2,66},{66,2},{3,67},{67,3},{4,68},{68... | collective-permute-start | bytes 6291464 | tf_op jit(solution)/shard_map/ppermute | solution.py:38
  115.7 5.3 %collective-permute-start.15 = (bf16[8,16,512]{2,1,0:T(8,128)(2,1)S(1)}, bf16[8,16,512]{2,1,0:T(8,128)(2,1)S(1)}, u32[]{:S(2)}, u32[]{:S(2)}) collective-permute-start(bf16[8,16,512]{2,1,0:T(8,128)(2,1)S(1)} %all_to_all.16.refs_0_), channel_id=1, source_target_pairs={{0,1},{1,2},{2,3},{3,0},{4,5},{5,6},{6,7},{7,4},{8,9},{9,10},{10,1... | collective-permute-start | bytes 393224 | tf_op jit(solution)/shard_map/ppermute | solution.py:62
  117.4 6.4 %collective-permute-start.16 = (bf16[8,16,512]{2,1,0:T(8,128)(2,1)S(1)}, bf16[8,16,512]{2,1,0:T(8,128)(2,1)S(1)}, u32[]{:S(2)}, u32[]{:S(2)}) collective-permute-start(bf16[8,16,512]{2,1,0:T(8,128)(2,1)S(1)} %all_to_all.16.refs_0_), channel_id=1, source_target_pairs={{0,2},{1,3},{2,0},{3,1},{4,6},{5,7},{6,4},{7,5},{8,10},{9,11},{10,... | collective-permute-start | bytes 393224 | tf_op jit(solution)/shard_map/ppermute | solution.py:62
  117.7 7.3 %collective-permute-start.17 = (bf16[8,16,512]{2,1,0:T(8,128)(2,1)S(1)}, bf16[8,16,512]{2,1,0:T(8,128)(2,1)S(1)}, u32[]{:S(2)}, u32[]{:S(2)}) collective-permute-start(bf16[8,16,512]{2,1,0:T(8,128)(2,1)S(1)} %all_to_all.16.refs_0_), channel_id=1, source_target_pairs={{0,3},{1,0},{2,1},{3,2},{4,7},{5,4},{6,5},{7,6},{8,11},{9,8},{10,9... | collective-permute-start | bytes 393224 | tf_op jit(solution)/shard_map/ppermute | solution.py:62
  119.8 5.8 %collective-permute-start.22 = (f32[16,512]{1,0:T(8,128)S(1)}, f32[16,512]{1,0:T(8,128)S(1)}, u32[]{:S(2)}, u32[]{:S(2)}) collective-permute-start(f32[16,512]{1,0:T(8,128)S(1)} %get-tuple-element.75), channel_id=1, source_target_pairs={{0,128},{64,192},{128,0},{192,64},{1,129},{65,193},{129,1},{193,65... | collective-permute-start | bytes 98312 | tf_op jit(solution)/shard_map/ppermute | solution.py:43
  121.0 5.2 %collective-permute-start.23 = (f32[16,512]{1,0:T(8,128)S(1)}, f32[16,512]{1,0:T(8,128)S(1)}, u32[]{:S(2)}, u32[]{:S(2)}) collective-permute-start(f32[16,512]{1,0:T(8,128)S(1)} %get-tuple-element.75), channel_id=1, source_target_pairs={{0,192},{64,128},{128,64},{192,0},{1,193},{65,129},{129,65},{193,1... | collective-permute-start | bytes 98312 | tf_op jit(solution)/shard_map/ppermute | solution.py:43
  123.8 4.0 %collective-permute-start.21 = (f32[16,512]{1,0:T(8,128)S(1)}, f32[16,512]{1,0:T(8,128)}, u32[]{:S(2)}, u32[]{:S(2)}) collective-permute-start(f32[16,512]{1,0:T(8,128)S(1)} %get-tuple-element.75), channel_id=1, source_target_pairs={{0,64},{64,0},{1,65},{65,1},{2,66},{66,2},{3,67},{67,3},{4,68},{68... | collective-permute-start | bytes 98312 | tf_op jit(solution)/shard_map/ppermute | solution.py:38
  125.1 6.4 %collective-permute-start.24 = (bf16[512,512]{1,0:T(8,128)(2,1)}, bf16[512,512]{1,0:T(8,128)(2,1)S(1)}, u32[]{:S(2)}, u32[]{:S(2)}) collective-permute-start(bf16[512,512]{1,0:T(8,128)(2,1)} %get-tuple-element.77), channel_id=1, source_target_pairs={{0,64},{64,0},{1,65},{65,1},{2,66},{66,2},{3,67},{67,3},{4,68},{68... | collective-permute-start | bytes 1572872 | tf_op jit(solution)/shard_map/ppermute | solution.py:38
  125.6 15.2 %collective-permute-start.18 = (bf16[4,8,16,512]{3,2,1,0:T(8,128)(2,1)S(1)}, bf16[4,8,16,512]{3,2,1,0:T(8,128)(2,1)S(1)}, u32[]{:S(2)}, u32[]{:S(2)}) collective-permute-start(bf16[4,8,16,512]{3,2,1,0:T(8,128)(2,1)S(1)} %shard_map.118.g0), channel_id=1, source_target_pairs={{0,32},{1,33},{2,34},{3,35},{4,36},{5,37},{6,38},{7,39},{8,40},{9,... | collective-permute-start | bytes 1572872 | tf_op jit(solution)/shard_map/ppermute | solution.py:62
  126.2 14.7 %collective-permute-start.19 = (bf16[4,8,16,512]{3,2,1,0:T(8,128)(2,1)S(1)}, bf16[4,8,16,512]{3,2,1,0:T(8,128)(2,1)S(1)}, u32[]{:S(2)}, u32[]{:S(2)}) collective-permute-start(bf16[4,8,16,512]{3,2,1,0:T(8,128)(2,1)S(1)} %shard_map.118.g0), channel_id=1, source_target_pairs={{0,128},{1,129},{2,130},{3,131},{4,132},{5,133},{6,134},{7,135},{8... | collective-permute-start | bytes 1572872 | tf_op jit(solution)/shard_map/ppermute | solution.py:62
  127.8 13.6 %collective-permute-start.20 = (bf16[4,8,16,512]{3,2,1,0:T(8,128)(2,1)S(1)}, bf16[4,8,16,512]{3,2,1,0:T(8,128)(2,1)S(1)}, u32[]{:S(2)}, u32[]{:S(2)}) collective-permute-start(bf16[4,8,16,512]{3,2,1,0:T(8,128)(2,1)S(1)} %shard_map.118.g0), channel_id=1, source_target_pairs={{0,160},{1,161},{2,162},{3,163},{4,164},{5,165},{6,166},{7,167},{8... | collective-permute-start | bytes 1572872 | tf_op jit(solution)/shard_map/ppermute | solution.py:62
  131.5 10.0 %copy-start.3 = (bf16[512,2048]{1,0:T(8,128)(2,1)S(1)}, bf16[512,2048]{1,0:T(8,128)(2,1)}, u32[]{:S(2)}) copy-start(bf16[512,2048]{1,0:T(8,128)(2,1)} %copy-done.2) | copy-start | bytes 6291460
  141.5 4.2 %copy-start.1 = (bf16[512,2048]{1,0:T(8,128)(2,1)S(1)}, bf16[512,2048]{1,0:T(8,128)(2,1)}, u32[]{:S(2)}) copy-start(bf16[512,2048]{1,0:T(8,128)(2,1)} %copy-done) | copy-start | bytes 6291460
  144.0 3.1 %collective-permute-start.26 = (bf16[512,512]{1,0:T(8,128)(2,1)S(1)}, bf16[512,512]{1,0:T(8,128)(2,1)S(1)}, u32[]{:S(2)}, u32[]{:S(2)}) collective-permute-start(bf16[512,512]{1,0:T(8,128)(2,1)S(1)} %get-tuple-element.87), channel_id=1, source_target_pairs={{0,64},{64,0},{1,65},{65,1},{2,66},{66,2},{3,67},{67,3},{4,68},{68... | collective-permute-start | bytes 1572872 | tf_op jit(solution)/shard_map/ppermute | solution.py:38

commit v4 on v3

--- a/solution.py
+++ b/solution.py
@@ -38,9 +38,8 @@
     return lax.ppermute(value, "core", [(0, 1), (1, 0)])
 
 
-def cross(value, other_core):
-    flip = 3 if other_core else 2
-    return lax.ppermute(value, ("yh", "core"), [(i, i ^ flip) for i in range(4)])
+def cross(value):
+    return lax.ppermute(value, "yh", [(0, 1), (1, 0)])
 
 
 def shift(value, k, inner):
@@ -105,12 +104,14 @@
         out_ref[k] = in_ref[...]
 
 
-def gather_blocks(block):
+def gather_blocks(block, beside=None):
     parts = [block] + [shift(block, k, True) for k in (1, 3, 2)]
     parts = [parts[0], parts[1], parts[3], parts[2]]
+    if beside is not None:
+        parts, beside = lax.optimization_barrier((parts, beside))
     (packed,) = call(pack_kernel, [((N_X,) + block.shape, BF, VMEM)], *parts)
     far = [shift(packed, k, False) for k in (1, 3, 2)]
-    return [packed, far[0], far[2], far[1]]
+    return [packed, far[0], far[2], far[1]], beside
 
 
 def load_whole(spot_ref, block_refs, whole_ref, sems):
@@ -126,18 +127,21 @@
     return copies
 
 
-def rows_kernel(spot_ref, route_ref, tokens_ref, x_ref, across_ref, buf_ref, sems):
+def rows_kernel(spot_ref, route_ref, tokens_ref, x_ref, across_ref, from_ref, rows_ref, buf_ref, in_sems, sems):
     count, depth = x_ref.shape
     low_n, n_z, n_x, high_n, rows, _ = buf_ref.shape
     step = 256
     core = spot_ref[0]
+    load = pltpu.make_async_copy(tokens_ref, from_ref, in_sems.at[0])
+    load.start()
     places = lax.broadcasted_iota(jnp.int32, (tokens_ref.shape[0], count), 0)
     hot = jnp.where(places == route_ref[...], 1.0, 0.0).astype(BF).T
     copies = []
+    load.wait()
     for low in range(low_n):
         for d in range(low * depth // low_n, (low + 1) * depth // low_n, step):
-            picked = jnp.dot(hot, tokens_ref[:, d : d + step], preferred_element_type=F32).astype(BF)
-            x_ref[:, d : d + step] = picked
+            picked = jnp.dot(hot, from_ref[:, d : d + step], preferred_element_type=F32).astype(BF)
+            rows_ref[:, d : d + step] = picked
             turned = picked.T
             for g in range(step // rows):
                 index = d // rows + g
@@ -154,6 +158,8 @@
                     pltpu.make_async_copy(buf_ref.at[low, :, x, high], across_ref.at[j, k], sems.at[len(copies)])
                 )
                 copies[-1].start()
+    copies.append(pltpu.make_async_copy(rows_ref, x_ref, in_sems.at[1]))
+    copies[-1].start()
     for copy in copies:
         copy.wait()
 
@@ -213,9 +219,14 @@
                 turned = turned_ref[half, j, k : k + 2].reshape(2 * n_z * rows, count)
                 product = jnp.dot(turned, d_ref[half * count : (half + 1) * count, :], preferred_element_type=F32)
                 part = product if part is None else part + product
-            part_ref[j, k : k + 2] = part.astype(BF).reshape(2, n_z, rows, feature)
-        outs.append(pltpu.make_async_copy(part_ref.at[j], (o0, o1, o2, o3)[j], out_sems.at[j]))
-        outs[-1].start()
+            part = part.astype(BF).reshape(2, n_z, rows, feature)
+            if j:
+                part_ref[j - 1, k : k + 2] = part
+            else:
+                o0[k : k + 2] = part
+        if j:
+            outs.append(pltpu.make_async_copy(part_ref.at[j - 1], (o1, o2, o3)[j - 1], out_sems.at[j - 1]))
+            outs[-1].start()
     for copy in outs:
         copy.wait()
 
@@ -313,24 +324,29 @@
     weight_part = part_of(weight)
     along_z = over_z(jnp.broadcast_to(weight_part.astype(BF)[None], block_shape))
     tokens_far, route_far, cot_far = swap(tokens), swap(route), swap(cotangent)
-    tokens_b, route_b, route_far = lax.optimization_barrier((tokens, route, route_far))
-    gathered = gather_blocks(along_z)
-    route_mine = mine_of(route_b)
-    route_other = other_of(route_b)
+    gathered, _ = gather_blocks(along_z)
+    route_mine = mine_of(route)
+    route_other = other_of(route)
 
     def rows_of(routes, from_tokens):
         return call(
             rows_kernel,
-            [((rows_here, depth), BF, VMEM), ((N_Y, N_X, n_z, half, rows_here), BF, ANY)],
+            [((rows_here, depth), BF, ANY), ((N_Y, N_X, n_z, half, rows_here), BF, ANY)],
             spot,
             routes[None],
-            from_tokens,
-            scratch=[pltpu.VMEM(natural + (rows_here,), BF), pltpu.SemaphoreType.DMA((N_Y * N_X,))],
+            in_hbm(from_tokens),
+            scratch=[
+                pltpu.VMEM(tokens.shape, BF),
+                pltpu.VMEM((rows_here, depth), BF),
+                pltpu.VMEM(natural + (rows_here,), BF),
+                pltpu.SemaphoreType.DMA((2,)),
+                pltpu.SemaphoreType.DMA((N_Y * N_X,)),
+            ],
             mib=16,
-            places=[SMEM, VMEM, VMEM],
+            places=[SMEM, VMEM, ANY],
         )
 
-    x_mine, across_mine = rows_of(route_mine, tokens_b)
+    x_mine, across_mine = rows_of(route_mine, tokens)
     x_other, across_other = rows_of(mine_of(route_far), tokens_far)
     first_part = BETA_ONE * dequant(part_of(first_q)[None], part_of(first_scale)[None])[0]
     second_part = BETA_TWO * dequant(part_of(second_q)[None], part_of(second_scale)[None])[0]
@@ -340,14 +356,15 @@
 
     b0, b1, b2, b3, dmine, dother, whole = call(
         gate_kernel,
-        [((N_X,) + block_shape, BF, ANY)] * 4
+        [((N_X,) + block_shape, BF, VMEM)]
+        + [((N_X,) + block_shape, BF, ANY)] * 3
         + [((rows_here, feature), BF, ANY)] * 2
         + [(natural + (feature,), BF, ANY)],
         spot,
         in_hbm(x_mine),
         in_hbm(x_other),
         in_hbm(cotangent),
-        in_hbm(cot_far),
+        cot_far,
         in_hbm(across_mine),
         in_hbm(across_other),
         *gathered,
@@ -357,41 +374,17 @@
             pltpu.VMEM((2 * rows_here, feature), BF),
             pltpu.VMEM((2, N_Y, N_X, n_z, half, rows_here), BF),
             pltpu.VMEM((2 * rows_here, feature), BF),
-            pltpu.VMEM((N_Y, N_X) + block_shape, BF),
+            pltpu.VMEM((N_Y - 1, N_X) + block_shape, BF),
             pltpu.SemaphoreType.DMA((7,)),
             pltpu.SemaphoreType.DMA((N_Y * N_X,)),
             pltpu.SemaphoreType.DMA((2, N_Y)),
-            pltpu.SemaphoreType.DMA((N_Y,)),
+            pltpu.SemaphoreType.DMA((N_Y - 1,)),
         ],
         mib=24,
         places=[SMEM] + [ANY] * 10,
     )
     whole = whole.reshape(depth, feature)
     got = [shift(block, k, False) for block, k in ((b1, 1), (b3, 3), (b2, 2))]
-    p0, p1, p2, p3 = call(sum_outer_kernel, [(block_shape, BF, VMEM)] * 4, b0, *got)
-    got = [shift(block, k, True) for block, k in ((p1, 1), (p3, 3), (p2, 2))]
-    (part,) = call(sum_inner_kernel, [(block_shape, BF, VMEM)], p0, *got)
-    got_z = over_z(part)
-    grad, new_blocks = call(
-        adam_kernel(total_rows),
-        [((half, feature), F32, VMEM), (block_shape, BF, VMEM)],
-        got_z,
-        weight_part,
-        first_part,
-        second_part,
-    )
-    new_along_z = over_z(new_blocks)
-    new_along_z, grad, whole, dother = lax.optimization_barrier((new_along_z, grad, whole, dother))
-    new_gathered = gather_blocks(new_along_z)
-
-    mine_half = pair(grad, swap(grad), core)
-    far_half = pair(cross(grad, False), cross(grad, True), core)
-    both = jnp.where(
-        high == 0,
-        jnp.concatenate([mine_half, far_half], axis=1),
-        jnp.concatenate([far_half, mine_half], axis=1),
-    )
-    step_dir, new_weight = adam_update(weight, both, first_q, first_scale, second_q, second_scale)
     other_whole = swap(whole)
     other_rows = swap(dother)
     (token_grad,) = call(
@@ -405,9 +398,29 @@
         scratch=[pltpu.VMEM((2, 256, feature), BF)],
         mib=14,
     )
-    *new_gathered, step_dir, new_weight, token_grad = lax.optimization_barrier(
-        (*new_gathered, step_dir, new_weight, token_grad)
-    )
+    *got, token_grad = lax.optimization_barrier((*got, token_grad))
+    p0, p1, p2, p3 = call(sum_outer_kernel, [(block_shape, BF, VMEM)] * 4, b0, *got)
+    got = [shift(block, k, True) for block, k in ((p1, 1), (p3, 3), (p2, 2))]
+    (part,) = call(sum_inner_kernel, [(block_shape, BF, VMEM)], p0, *got)
+    got_z = over_z(part)
+    grad, new_blocks = call(
+        adam_kernel(total_rows),
+        [((half, feature), F32, VMEM), (block_shape, BF, VMEM)],
+        got_z,
+        weight_part,
+        first_part,
+        second_part,
+    )
+    new_along_z = over_z(new_blocks)
+
+    new_along_z, grad = lax.optimization_barrier((new_along_z, grad))
+    new_gathered, far_grad = gather_blocks(new_along_z, cross(grad))
+    owned_grad = jnp.where(
+        high == 0, jnp.concatenate([grad, far_grad], axis=0), jnp.concatenate([far_grad, grad], axis=0)
+    )
+    both = pair(owned_grad, swap(owned_grad), core)
+    step_dir, new_weight = adam_update(weight, both, first_q, first_scale, second_q, second_scale)
+    *new_gathered, step_dir, new_weight = lax.optimization_barrier((*new_gathered, step_dir, new_weight))
 
     next_other, new_whole = call(
         next_other_kernel,

time: 149 us -> 146 us (0.980)
  local copies, waits for them, and re-layouts: 13 us -> 8.09 us
  waiting for transfers between devices: 27.4 us -> 23.6 us
  starting transfers between devices: 46.2 us -> 49.7 us
  Pallas kernels: 31.6 us -> 34.2 us
    ppermute x18, waiting for transfers between devices: 19.6 us -> 11.8 us  [shift(): return lax.ppermute(value, AXES, pairs)]
    ppermute x7, starting transfers between devices: 17.1 us -> 24.3 us  [swap(): return lax.ppermute(value, 'core', [(0, 1), (1, 0)])]
    unnamed x22 -> x14, local copies, waits for them, and re-layouts: 5.81 us -> 2.83 us
    ppermute x7, waiting for transfers between devices: 0.3 us -> 2.89 us  [swap(): return lax.ppermute(value, 'core', [(0, 1), (1, 0)])]
    pallas_call x11, Pallas kernels: 31.6 us -> 34.2 us  [call(): pl.pallas_call(kernel, out_shape=[pltpu.HBM(shape, dtype) if where == ANY...]
    ppermute x18, starting transfers between devices: 21.9 us -> 19.5 us  [shift(): return lax.ppermute(value, AXES, pairs)]
    ppermute x2 -> x1, starting transfers between devices: 3.71 us -> 2.36 us  [cross(): return lax.ppermute(value, 'yh', [(0, 1), (1, 0)])]
  transfers between devices with their start and end apart: 28 -> 27, of which waited for: 11 -> 13; matrix products, arithmetic and copies ran while one was open for 8% -> 6% of each run, Pallas kernels for 12% -> 14%
where the time goes in v4:
time: 146 us; the launch traced here: 145 us
  starting transfers between devices  49.7 us (34%)
  Pallas kernels  34.2 us (23%)
  blocking collectives  24.5 us (17%)
  waiting for transfers between devices  23.6 us (16%)
  local copies, waits for them, and re-layouts  8.09 us (6%)
  other arithmetic  4 us (3%)
    pallas_call x11, Pallas kernels, call(): pl.pallas_call(kernel, out_shape=[pltpu.HBM(shape, dtype) if where == ANY...  34.2 us
    all_to_all x2, blocking collectives, over_z(): return lax.all_to_all(blocks, 'z', 0, 0, tiled=True)  24.5 us
    ppermute x7, starting transfers between devices, swap(): return lax.ppermute(value, 'core', [(0, 1), (1, 0)])  24.3 us
    ppermute x18, starting transfers between devices, shift(): return lax.ppermute(value, AXES, pairs)  19.5 us
    ppermute x18, waiting for transfers between devices, shift(): return lax.ppermute(value, AXES, pairs)  11.8 us
    all_to_all x1, waiting for transfers between devices, over_z(): return lax.all_to_all(blocks, 'z', 0, 0, tiled=True)  7.01 us
    all_to_all x1, starting transfers between devices, over_z(): return lax.all_to_all(blocks, 'z', 0, 0, tiled=True)  3.5 us
  transfers between devices with their start and end apart: 27, of which 13 were waited for; matrix products, arithmetic and copies ran while one was open for 6% of the time, Pallas kernels for 14%

profile of v4, /device:TPU:1, one launch (start us, length us, event | category | flops | bytes accessed | tf_op | source)
XLA Modules:
  0.0 144.9 jit_solution(1737496106376433704)
XLA Ops:
  0.6 3.3 %collective-permute-start.7 = (bf16[768,2048]{1,0:T(8,128)(2,1)}, bf16[768,2048]{1,0:T(8,128)(2,1)}, u32[]{:S(2)}, u32[]{:S(2)}) collective-permute-start(bf16[768,2048]{1,0:T(8,128)(2,1)} %tokens_ref.1), channel_id=1, source_target_pairs={{0,64},{64,0},{1,65},{65,1},{2,66},{66,2},{3,67},{67,3},{4,68},{68... | collective-permute-start | bytes 9437192 | tf_op jit(solution)/shard_map/ppermute | solution.py:38
  4.1 0.8 fusion.7
  4.9 14.1 %all_to_all.15.refs_0_ = bf16[8,16,512]{2,1,0:T(8,128)(2,1)S(1)} all-to-all(bf16[8,16,512]{2,1,0:T(8,128)(2,1)S(1)} %broadcast_in_dim.5), channel_id=1, replica_groups=mesh['yh'=2,'core'=2,'yl'=2,'z'=8,'x'=4] {'z'}, dimensions={0} | all-to-all | bytes 262144 | tf_op jit(solution)/shard_map/all_to_all | solution.py:322
  19.0 1.3 collective-permute-start
  20.3 2.6 %collective-permute-start.1 = (bf16[8,16,512]{2,1,0:T(8,128)(2,1)S(1)}, bf16[8,16,512]{2,1,0:T(8,128)(2,1)S(1)}, u32[]{:S(2)}, u32[]{:S(2)}) collective-permute-start(bf16[8,16,512]{2,1,0:T(8,128)(2,1)S(1)} %all_to_all.15.refs_0_), channel_id=1, source_target_pairs={{0,2},{1,3},{2,0},{3,1},{4,6},{5,7},{6,4},{7,5},{8,10},{9,11},{10,... | collective-permute-start | bytes 393224 | tf_op jit(solution)/shard_map/ppermute | solution.py:61
  22.8 1.1 collective-permute-start.2
  23.9 0.8 dynamic-slice_bitcast_fusion.2
  24.7 2.9 %collective-permute-start.6 = (s32[2,512]{1,0:T(2,128)}, s32[2,512]{1,0:T(2,128)S(1)}, u32[]{:S(2)}, u32[]{:S(2)}) collective-permute-start(s32[2,512]{1,0:T(2,128)} %param.9), channel_id=1, source_target_pairs={{0,64},{64,0},{1,65},{65,1},{2,66},{66,2},{3,67},{67,3},{4,68},{68... | collective-permute-start | bytes 12296 | tf_op jit(solution)/shard_map/ppermute | solution.py:38
  27.6 0.8 dynamic-slice_bitcast_fusion.1
  28.9 1.9 %collective-permute-start.4 = (bf16[4,8,16,512]{3,2,1,0:T(8,128)(2,1)S(1)}, bf16[4,8,16,512]{3,2,1,0:T(8,128)(2,1)S(1)}, u32[]{:S(2)}, u32[]{:S(2)}) collective-permute-start(bf16[4,8,16,512]{3,2,1,0:T(8,128)(2,1)S(1)} %shard_map.111.g0), channel_id=1, source_target_pairs={{0,128},{1,129},{2,130},{3,131},{4,132},{5,133},{6,134},{7,135},{8... | collective-permute-start | bytes 1572872 | tf_op jit(solution)/shard_map/ppermute | solution.py:61
  30.8 1.2 collective-permute-start.5
  32.1 0.8 constant_dynamic-slice_fusion
  32.8 6.2 %shard_map.112 = (bf16[512,2048]{1,0:T(8,128)(2,1)}, bf16[4,4,8,16,512]{4,3,2,1,0:T(8,128)(2,1)}) custom-call(s32[3]{0:T(128)S(1)} %pad_add_fusion.1.spot_ref, s32[1,512]{1,0:T(1,128)S(1)} %get-tuple-element.97.route_ref, bf16[768,2048]{1,0:T(8,128)(2,1)} %tokens_ref.1), custom_call_target="tpu_custom_call" | custom-call | tf_op jit(solution)/shard_map/pallas_call | solution.py:88
  39.2 0.9 fusion.5
  40.1 6.2 %shard_map.113 = (bf16[512,2048]{1,0:T(8,128)(2,1)}, bf16[4,4,8,16,512]{4,3,2,1,0:T(8,128)(2,1)}) custom-call(s32[3]{0:T(128)S(1)} %pad_add_fusion.1.spot_ref, s32[1,512]{1,0:T(1,128)S(1)} %constant_dynamic-slice_fusion.1.route_ref, bf16[768,2048]{1,0:T(8,128)(2,1)} %collective-permute-done.7.tokens_ref), custom_call_target="tpu_custom_call" | custom-call | tf_op jit(solution)/shard_map/pallas_call | solution.py:88
  46.4 9.6 %shard_map.114 = (bf16[4,8,16,512]{3,2,1,0:T(8,128)(2,1)S(1)}, bf16[4,8,16,512]{3,2,1,0:T(8,128)(2,1)}, bf16[4,8,16,512]{3,2,1,0:T(8,128)(2,1)}, bf16[4,8,16,512...) custom-call(s32[3]{0:T(128)S(1)} %pad_add_fusion.1.spot_ref, ...), custom_call_target="tpu_custom_call" | custom-call | tf_op jit(solution)/shard_map/pallas_call | solution.py:88
  56.0 4.4 %collective-permute-start.13 = (bf16[2048,512]{1,0:T(8,128)(2,1)}, bf16[2048,512]{1,0:T(8,128)(2,1)S(1)}, u32[]{:S(2)}, u32[]{:S(2)}) collective-permute-start(bf16[2048,512]{1,0:T(8,128)(2,1)} %bitcast.34), channel_id=1, source_target_pairs={{0,64},{64,0},{1,65},{65,1},{2,66},{66,2},{3,67},{67,3},{4,68},{68... | collective-permute-start | bytes 6291464 | tf_op jit(solution)/shard_map/ppermute | solution.py:38
  60.5 2.4 %collective-permute-start.10 = (bf16[4,8,16,512]{3,2,1,0:T(8,128)(2,1)}, bf16[4,8,16,512]{3,2,1,0:T(8,128)(2,1)S(1)}, u32[]{:S(2)}, u32[]{:S(2)}) collective-permute-start(bf16[4,8,16,512]{3,2,1,0:T(8,128)(2,1)} %get-tuple-element.61), channel_id=1, source_target_pairs={{0,160},{1,161},{2,162},{3,163},{4,164},{5,165},{6,166},{7,167},{8... | collective-permute-start | bytes 1572872 | tf_op jit(solution)/shard_map/ppermute | solution.py:61
  63.4 1.7 %collective-permute-done.12.dother_ref = bf16[512,512]{1,0:T(8,128)(2,1)S(1)} collective-permute-done((bf16[512,512]{1,0:T(8,128)(2,1)}, bf16[512,512]{1,0:T(8,128)(2,1)S(1)}, u32[]{:S(2)}, u32[]{:S(2)}) %collective-permute-start.12) | collective-permute-done | bytes 524320 | tf_op jit(solution)/shard_map/ppermute | solution.py:38
  65.1 1.6 %copy-done.2 = bf16[2,8,4,2,16,512]{5,4,3,2,1,0:T(8,128)(2,1)S(1)} copy-done((bf16[2,8,4,2,16,512]{5,4,3,2,1,0:T(8,128)(2,1)S(1)}, bf16[2,8,4,2,16,512]{5,4,3,2,1,0:T(8,128)(2,1)}, u32[]{:S(2)}) %copy-start.2) | copy-done | bytes 2097176
  66.7 1.0 copy-done.3
  67.7 6.2 %shard_map.115 = bf16[768,2048]{1,0:T(8,128)(2,1)} custom-call(s32[2,512]{1,0:T(2,128)S(1)} %pad_add_fusion.routes_ref, bf16[512,512]{1,0:T(8,128)(2,1)S(1)} %copy-done.3, bf16[512,512]{1,0:T(8,128)(2,1)S(1)} %collective-permute-done.12.dother_ref, bf16[2048,512]{1,0:T(8,128)(2,1)S(1)} %bitcast.35, bf16[2048,512]{1,0:T(8,128)(2,1)S(1)} %collective-permute-done.13.other_ref), custom_call_target="tpu_custom_call" | custom-call | tf_op jit(solution)/shard_map/pallas_call | solution.py:88
  73.9 1.0 collective-permute-done.10.c
  74.9 3.3 %collective-permute-done.9.b = bf16[4,8,16,512]{3,2,1,0:T(8,128)(2,1)S(1)} collective-permute-done((bf16[4,8,16,512]{3,2,1,0:T(8,128)(2,1)}, bf16[4,8,16,512]{3,2,1,0:T(8,128)(2,1)S(1)}, u32[]{:S(2)}, u32[]{:S(2)}) %collective-permute-start.9) | collective-permute-done | bytes 524320 | tf_op jit(solution)/shard_map/ppermute | solution.py:61
  79.0 2.2 %collective-permute-start.15 = (bf16[8,16,512]{2,1,0:T(8,128)(2,1)S(1)}, bf16[8,16,512]{2,1,0:T(8,128)(2,1)S(1)}, u32[]{:S(2)}, u32[]{:S(2)}) collective-permute-start(bf16[8,16,512]{2,1,0:T(8,128)(2,1)S(1)} %get-tuple-element.73), channel_id=1, source_target_pairs={{0,3},{1,0},{2,1},{3,2},{4,7},{5,4},{6,5},{7,6},{8,11},{9,8},{10,9... | collective-permute-start | bytes 393224 | tf_op jit(solution)/shard_map/ppermute | solution.py:61
  81.2 2.3 %collective-permute-done.14.b = bf16[8,16,512]{2,1,0:T(8,128)(2,1)S(1)} collective-permute-done((bf16[8,16,512]{2,1,0:T(8,128)(2,1)S(1)}, bf16[8,16,512]{2,1,0:T(8,128)(2,1)S(1)}, u32[]{:S(2)}, u32[]{:S(2)}) %collective-permute-start.14) | collective-permute-done | bytes 131104 | tf_op jit(solution)/shard_map/ppermute | solution.py:61
  83.6 1.0 collective-permute-done.15.c
  84.5 2.3 %collective-permute-done.16.d = bf16[8,16,512]{2,1,0:T(8,128)(2,1)S(1)} collective-permute-done((bf16[8,16,512]{2,1,0:T(8,128)(2,1)S(1)}, bf16[8,16,512]{2,1,0:T(8,128)(2,1)S(1)}, u32[]{:S(2)}, u32[]{:S(2)}) %collective-permute-start.16) | collective-permute-done | bytes 131104 | tf_op jit(solution)/shard_map/ppermute | solution.py:61
  86.8 0.7 shard_map.117
  87.6 3.5 %all-to-all-start.1 = ((bf16[8,16,512]{2,1,0:T(8,128)(2,1)}), bf16[8,16,512]{2,1,0:T(8,128)(2,1)S(1)}, u32[]{:S(2)}, u32[]{:S(2)}) async-start(bf16[8,16,512]{2,1,0:T(8,128)(2,1)} %shard_map.117), calls=%async_computation.1 | async-start | bytes 262144 | tf_op jit(solution)/shard_map/all_to_all | solution.py:322
  91.1 0.8 dynamic-slice_bitcast_fusion.weight_ref
  91.9 7.0 %all-to-all-done.1.got_ref = bf16[8,16,512]{2,1,0:T(8,128)(2,1)S(1)} async-done(((bf16[8,16,512]{2,1,0:T(8,128)(2,1)}), bf16[8,16,512]{2,1,0:T(8,128)(2,1)S(1)}, u32[]{:S(2)}, u32[]{:S(2)}) %all-to-all-start.1) | async-done | bytes 131104 | tf_op jit(solution)/shard_map/all_to_all | solution.py:322
  98.9 10.4 %all_to_all.16.refs_0_ = bf16[8,16,512]{2,1,0:T(8,128)(2,1)S(1)} all-to-all(bf16[8,16,512]{2,1,0:T(8,128)(2,1)S(1)} %get-tuple-element.77), channel_id=1, replica_groups=mesh['yh'=2,'core'=2,'yl'=2,'z'=8,'x'=4] {'z'}, dimensions={0} | all-to-all | bytes 262144 | tf_op jit(solution)/shard_map/all_to_all | solution.py:322
  109.4 2.6 %collective-permute-start.18 = (bf16[8,16,512]{2,1,0:T(8,128)(2,1)S(1)}, bf16[8,16,512]{2,1,0:T(8,128)(2,1)S(1)}, u32[]{:S(2)}, u32[]{:S(2)}) collective-permute-start(bf16[8,16,512]{2,1,0:T(8,128)(2,1)S(1)} %all_to_all.16.refs_0_), channel_id=1, source_target_pairs={{0,2},{1,3},{2,0},{3,1},{4,6},{5,7},{6,4},{7,5},{8,10},{9,11},{10,... | collective-permute-start | bytes 393224 | tf_op jit(solution)/shard_map/ppermute | solution.py:61
  112.0 2.4 %collective-permute-start.20 = (f32[16,512]{1,0:T(8,128)S(1)}, f32[16,512]{1,0:T(8,128)S(1)}, u32[]{:S(2)}, u32[]{:S(2)}) collective-permute-start(f32[16,512]{1,0:T(8,128)S(1)} %get-tuple-element.80), channel_id=1, source_target_pairs={{0,128},{128,0},{1,129},{129,1},{2,130},{130,2},{3,131},{131,3},{4... | collective-permute-start | bytes 98312 | tf_op jit(solution)/shard_map/ppermute | solution.py:42
  114.4 1.9 %collective-permute-done.20 = f32[16,512]{1,0:T(8,128)S(1)} collective-permute-done((f32[16,512]{1,0:T(8,128)S(1)}, f32[16,512]{1,0:T(8,128)S(1)}, u32[]{:S(2)}, u32[]{:S(2)}) %collective-permute-start.20) | collective-permute-done | bytes 32800 | tf_op jit(solution)/shard_map/ppermute | solution.py:42
  116.5 2.0 %collective-permute-start.22 = (bf16[4,8,16,512]{3,2,1,0:T(8,128)(2,1)S(1)}, bf16[4,8,16,512]{3,2,1,0:T(8,128)(2,1)}, u32[]{:S(2)}, u32[]{:S(2)}) collective-permute-start(bf16[4,8,16,512]{3,2,1,0:T(8,128)(2,1)S(1)} %shard_map.119.g0), channel_id=1, source_target_pairs={{0,128},{1,129},{2,130},{3,131},{4,132},{5,133},{6,134},{7,135},{8... | collective-permute-start | bytes 1572872 | tf_op jit(solution)/shard_map/ppermute | solution.py:61
  118.5 0.7 collective-permute-start.23
  119.7 0.7 mul.129
  120.5 7.3 %collective-permute-start.24 = (f32[32,512]{1,0:T(8,128)S(1)}, f32[32,512]{1,0:T(8,128)S(1)}, u32[]{:S(2)}, u32[]{:S(2)}) collective-permute-start(f32[32,512]{1,0:T(8,128)S(1)} %maximum_select_fusion.3), channel_id=1, source_target_pairs={{0,64},{64,0},{1,65},{65,1},{2,66},{66,2},{3,67},{67,3},{4,68},{68... | collective-permute-start | bytes 196616 | tf_op jit(solution)/shard_map/ppermute | solution.py:38
  127.8 0.9 collective-permute-done.24
  128.6 1.9 %multiply_subtract_fusion = (f32[2,32,512]{2,1,0:T(8,128)}, f32[2,32,512]{2,1,0:T(8,128)}) fusion(f32[2,32,512]{2,1,0:T(8,128)} %param.11, f32[2,32,512]{2,1,0:T(8,128)} %mul.129, s32[2,32,512]{2,1,0:T(8,128)} %param.14, f32[1,32,512]{2,1,0:T(8,128)S(1)} %maximum_select_fusion.2, f32[1,32,512]{2,1,0:T(8,128)S(1)} %bitcast.41, pred[]{:T(512)S(6)} %eq.4, ...), kind=kLoop, calls=%fused_computation.8 | loop fusion | flops 655360 | bytes 1048577 | tf_op jit(solution)/shard_map/sub | solution.py:34
  130.6 1.2 collective-permute-done.21.g1
  131.8 0.6 collective-permute-done.23.g3
  132.4 3.6 %shard_map.120 = (bf16[512,512]{1,0:T(8,128)(2,1)S(1)}, bf16[2,8,4,2,16,512]{5,4,3,2,1,0:T(8,128)(2,1)S(1)}) custom-call(s32[3]{0:T(128)S(1)} %pad_add_fusion.1.spot_ref, bf16[512,2048]{1,0:T(8,128)(2,1)S(1)} %copy-done.1, bf16[4,8,16,512]{3,2,1,0:T(8,128)(2,1)S(1)} %shard_map.119.g0, bf16[4,8,16,512]{3,2,1,0:T(8,128)(2,1)S(1)} %collective-permute-done.21.g1, ...), custom_call_target="tpu_custom_call" | custom-call | tf_op jit(solution)/shard_map/pallas_call | solution.py:88
  136.0 6.2 %collective-permute-start.25 = (bf16[512,512]{1,0:T(8,128)(2,1)S(1)}, bf16[512,512]{1,0:T(8,128)(2,1)S(1)}, u32[]{:S(2)}, u32[]{:S(2)}) collective-permute-start(bf16[512,512]{1,0:T(8,128)(2,1)S(1)} %get-tuple-element.93), channel_id=1, source_target_pairs={{0,64},{64,0},{1,65},{65,1},{2,66},{66,2},{3,67},{67,3},{4,68},{68... | collective-permute-start | bytes 1572872 | tf_op jit(solution)/shard_map/ppermute | solution.py:38
  142.2 1.2 shard_map.121
  143.7 1.1 maximum_select_fusion
  (55 shorter events, 3.6 us)
Async XLA Ops:
  0.6 39.5 %collective-permute-start.7 = (bf16[768,2048]{1,0:T(8,128)(2,1)}, bf16[768,2048]{1,0:T(8,128)(2,1)}, u32[]{:S(2)}, u32[]{:S(2)}) collective-permute-start(bf16[768,2048]{1,0:T(8,128)(2,1)} %tokens_ref.1), channel_id=1, source_target_pairs={{0,64},{64,0},{1,65},{65,1},{2,66},{66,2},{3,67},{67,3},{4,68},{68... | collective-permute-start | bytes 9437192 | tf_op jit(solution)/shard_map/ppermute | solution.py:38
  4.0 42.4 %collective-permute-start.8 = (bf16[2,512,512]{2,1,0:T(8,128)(2,1)}, bf16[2,512,512]{2,1,0:T(8,128)(2,1)S(1)}, u32[]{:S(2)}, u32[]{:S(2)}) collective-permute-start(bf16[2,512,512]{2,1,0:T(8,128)(2,1)} %cot_mine_ref.1), channel_id=1, source_target_pairs={{0,64},{64,0},{1,65},{65,1},{2,66},{66,2},{3,67},{67,3},{4,68},{68... | collective-permute-start | bytes 3145736 | tf_op jit(solution)/shard_map/ppermute | solution.py:38
  19.0 5.7 %collective-permute-start = (bf16[8,16,512]{2,1,0:T(8,128)(2,1)S(1)}, bf16[8,16,512]{2,1,0:T(8,128)(2,1)S(1)}, u32[]{:S(2)}, u32[]{:S(2)}) collective-permute-start(bf16[8,16,512]{2,1,0:T(8,128)(2,1)S(1)} %all_to_all.15.refs_0_), channel_id=1, source_target_pairs={{0,1},{1,2},{2,3},{3,0},{4,5},{5,6},{6,7},{7,4},{8,9},{9,10},{10,1... | collective-permute-start | bytes 393224 | tf_op jit(solution)/shard_map/ppermute | solution.py:61
  20.3 8.2 %collective-permute-start.1 = (bf16[8,16,512]{2,1,0:T(8,128)(2,1)S(1)}, bf16[8,16,512]{2,1,0:T(8,128)(2,1)S(1)}, u32[]{:S(2)}, u32[]{:S(2)}) collective-permute-start(bf16[8,16,512]{2,1,0:T(8,128)(2,1)S(1)} %all_to_all.15.refs_0_), channel_id=1, source_target_pairs={{0,2},{1,3},{2,0},{3,1},{4,6},{5,7},{6,4},{7,5},{8,10},{9,11},{10,... | collective-permute-start | bytes 393224 | tf_op jit(solution)/shard_map/ppermute | solution.py:61
  22.8 5.6 %collective-permute-start.2 = (bf16[8,16,512]{2,1,0:T(8,128)(2,1)S(1)}, bf16[8,16,512]{2,1,0:T(8,128)(2,1)S(1)}, u32[]{:S(2)}, u32[]{:S(2)}) collective-permute-start(bf16[8,16,512]{2,1,0:T(8,128)(2,1)S(1)} %all_to_all.15.refs_0_), channel_id=1, source_target_pairs={{0,3},{1,0},{2,1},{3,2},{4,7},{5,4},{6,5},{7,6},{8,11},{9,8},{10,9... | collective-permute-start | bytes 393224 | tf_op jit(solution)/shard_map/ppermute | solution.py:61
  24.7 6.2 %collective-permute-start.6 = (s32[2,512]{1,0:T(2,128)}, s32[2,512]{1,0:T(2,128)S(1)}, u32[]{:S(2)}, u32[]{:S(2)}) collective-permute-start(s32[2,512]{1,0:T(2,128)} %param.9), channel_id=1, source_target_pairs={{0,64},{64,0},{1,65},{65,1},{2,66},{66,2},{3,67},{67,3},{4,68},{68... | collective-permute-start | bytes 12296 | tf_op jit(solution)/shard_map/ppermute | solution.py:38
  28.5 17.8 %collective-permute-start.3 = (bf16[4,8,16,512]{3,2,1,0:T(8,128)(2,1)S(1)}, bf16[4,8,16,512]{3,2,1,0:T(8,128)(2,1)S(1)}, u32[]{:S(2)}, u32[]{:S(2)}) collective-permute-start(bf16[4,8,16,512]{3,2,1,0:T(8,128)(2,1)S(1)} %shard_map.111.g0), channel_id=1, source_target_pairs={{0,32},{1,33},{2,34},{3,35},{4,36},{5,37},{6,38},{7,39},{8,40},{9,... | collective-permute-start | bytes 1572872 | tf_op jit(solution)/shard_map/ppermute | solution.py:61
  28.9 17.4 %collective-permute-start.4 = (bf16[4,8,16,512]{3,2,1,0:T(8,128)(2,1)S(1)}, bf16[4,8,16,512]{3,2,1,0:T(8,128)(2,1)S(1)}, u32[]{:S(2)}, u32[]{:S(2)}) collective-permute-start(bf16[4,8,16,512]{3,2,1,0:T(8,128)(2,1)S(1)} %shard_map.111.g0), channel_id=1, source_target_pairs={{0,128},{1,129},{2,130},{3,131},{4,132},{5,133},{6,134},{7,135},{8... | collective-permute-start | bytes 1572872 | tf_op jit(solution)/shard_map/ppermute | solution.py:61
  30.8 15.5 %collective-permute-start.5 = (bf16[4,8,16,512]{3,2,1,0:T(8,128)(2,1)S(1)}, bf16[4,8,16,512]{3,2,1,0:T(8,128)(2,1)S(1)}, u32[]{:S(2)}, u32[]{:S(2)}) collective-permute-start(bf16[4,8,16,512]{3,2,1,0:T(8,128)(2,1)S(1)} %shard_map.111.g0), channel_id=1, source_target_pairs={{0,160},{1,161},{2,162},{3,163},{4,164},{5,165},{6,166},{7,167},{8... | collective-permute-start | bytes 1572872 | tf_op jit(solution)/shard_map/ppermute | solution.py:61
  56.0 9.1 %collective-permute-start.13 = (bf16[2048,512]{1,0:T(8,128)(2,1)}, bf16[2048,512]{1,0:T(8,128)(2,1)S(1)}, u32[]{:S(2)}, u32[]{:S(2)}) collective-permute-start(bf16[2048,512]{1,0:T(8,128)(2,1)} %bitcast.34), channel_id=1, source_target_pairs={{0,64},{64,0},{1,65},{65,1},{2,66},{66,2},{3,67},{67,3},{4,68},{68... | collective-permute-start | bytes 6291464 | tf_op jit(solution)/shard_map/ppermute | solution.py:38
  60.4 4.7 %collective-permute-start.12 = (bf16[512,512]{1,0:T(8,128)(2,1)}, bf16[512,512]{1,0:T(8,128)(2,1)S(1)}, u32[]{:S(2)}, u32[]{:S(2)}) collective-permute-start(bf16[512,512]{1,0:T(8,128)(2,1)} %get-tuple-element.64), channel_id=1, source_target_pairs={{0,64},{64,0},{1,65},{65,1},{2,66},{66,2},{3,67},{67,3},{4,68},{68... | collective-permute-start | bytes 1572872 | tf_op jit(solution)/shard_map/ppermute | solution.py:38
  60.5 14.4 %collective-permute-start.10 = (bf16[4,8,16,512]{3,2,1,0:T(8,128)(2,1)}, bf16[4,8,16,512]{3,2,1,0:T(8,128)(2,1)S(1)}, u32[]{:S(2)}, u32[]{:S(2)}) collective-permute-start(bf16[4,8,16,512]{3,2,1,0:T(8,128)(2,1)} %get-tuple-element.61), channel_id=1, source_target_pairs={{0,160},{1,161},{2,162},{3,163},{4,164},{5,165},{6,166},{7,167},{8... | collective-permute-start | bytes 1572872 | tf_op jit(solution)/shard_map/ppermute | solution.py:61
  62.8 12.1 %collective-permute-start.11 = (bf16[4,8,16,512]{3,2,1,0:T(8,128)(2,1)}, bf16[4,8,16,512]{3,2,1,0:T(8,128)(2,1)S(1)}, u32[]{:S(2)}, u32[]{:S(2)}) collective-permute-start(bf16[4,8,16,512]{3,2,1,0:T(8,128)(2,1)} %get-tuple-element.62), channel_id=1, source_target_pairs={{0,128},{1,129},{2,130},{3,131},{4,132},{5,133},{6,134},{7,135},{8... | collective-permute-start | bytes 1572872 | tf_op jit(solution)/shard_map/ppermute | solution.py:61
  63.2 14.9 %collective-permute-start.9 = (bf16[4,8,16,512]{3,2,1,0:T(8,128)(2,1)}, bf16[4,8,16,512]{3,2,1,0:T(8,128)(2,1)S(1)}, u32[]{:S(2)}, u32[]{:S(2)}) collective-permute-start(bf16[4,8,16,512]{3,2,1,0:T(8,128)(2,1)} %get-tuple-element.60), channel_id=1, source_target_pairs={{0,32},{1,33},{2,34},{3,35},{4,36},{5,37},{6,38},{7,39},{8,40},{9,... | collective-permute-start | bytes 1572872 | tf_op jit(solution)/shard_map/ppermute | solution.py:61
  65.1 1.6 %copy-start.2 = (bf16[2,8,4,2,16,512]{5,4,3,2,1,0:T(8,128)(2,1)S(1)}, bf16[2,8,4,2,16,512]{5,4,3,2,1,0:T(8,128)(2,1)}, u32[]{:S(2)}) copy-start(bf16[2,8,4,2,16,512]{5,4,3,2,1,0:T(8,128)(2,1)} %get-tuple-element.65) | copy-start | bytes 6291460
  66.7 1.0 copy-start.3
  78.2 41.0 %copy-start.4 = (f32[2,32,4]{1,2,0:T(4,128)S(1)}, f32[2,32,4]{1,2,0:T(4,128)}, u32[]{:S(2)}) copy-start(f32[2,32,4]{1,2,0:T(4,128)} %param.13) | copy-start | bytes 3076
  78.2 41.1 %copy-start.5 = (f32[2,32,4]{1,2,0:T(4,128)S(1)}, f32[2,32,4]{1,2,0:T(4,128)}, u32[]{:S(2)}) copy-start(f32[2,32,4]{1,2,0:T(4,128)} %param.15) | copy-start | bytes 3076
  78.4 5.1 %collective-permute-start.14 = (bf16[8,16,512]{2,1,0:T(8,128)(2,1)S(1)}, bf16[8,16,512]{2,1,0:T(8,128)(2,1)S(1)}, u32[]{:S(2)}, u32[]{:S(2)}) collective-permute-start(bf16[8,16,512]{2,1,0:T(8,128)(2,1)S(1)} %get-tuple-element.72), channel_id=1, source_target_pairs={{0,1},{1,2},{2,3},{3,0},{4,5},{5,6},{6,7},{7,4},{8,9},{9,10},{10,1... | collective-permute-start | bytes 393224 | tf_op jit(solution)/shard_map/ppermute | solution.py:61
  79.0 5.6 %collective-permute-start.15 = (bf16[8,16,512]{2,1,0:T(8,128)(2,1)S(1)}, bf16[8,16,512]{2,1,0:T(8,128)(2,1)S(1)}, u32[]{:S(2)}, u32[]{:S(2)}) collective-permute-start(bf16[8,16,512]{2,1,0:T(8,128)(2,1)S(1)} %get-tuple-element.73), channel_id=1, source_target_pairs={{0,3},{1,0},{2,1},{3,2},{4,7},{5,4},{6,5},{7,6},{8,11},{9,8},{10,9... | collective-permute-start | bytes 393224 | tf_op jit(solution)/shard_map/ppermute | solution.py:61
  81.2 5.6 %collective-permute-start.16 = (bf16[8,16,512]{2,1,0:T(8,128)(2,1)S(1)}, bf16[8,16,512]{2,1,0:T(8,128)(2,1)S(1)}, u32[]{:S(2)}, u32[]{:S(2)}) collective-permute-start(bf16[8,16,512]{2,1,0:T(8,128)(2,1)S(1)} %get-tuple-element.74), channel_id=1, source_target_pairs={{0,2},{1,3},{2,0},{3,1},{4,6},{5,7},{6,4},{7,5},{8,10},{9,11},{10,... | collective-permute-start | bytes 393224 | tf_op jit(solution)/shard_map/ppermute | solution.py:61
  87.5 44.9 %copy-start.1 = (bf16[512,2048]{1,0:T(8,128)(2,1)S(1)}, bf16[512,2048]{1,0:T(8,128)(2,1)}, u32[]{:S(2)}) copy-start(bf16[512,2048]{1,0:T(8,128)(2,1)} %get-tuple-element.52.other_ref.x_ref) | copy-start | bytes 6291460
  87.6 11.3 %all-to-all-start.1 = ((bf16[8,16,512]{2,1,0:T(8,128)(2,1)}), bf16[8,16,512]{2,1,0:T(8,128)(2,1)S(1)}, u32[]{:S(2)}, u32[]{:S(2)}) async-start(bf16[8,16,512]{2,1,0:T(8,128)(2,1)} %shard_map.117), calls=%async_computation.1 | async-start | bytes 262144 | tf_op jit(solution)/shard_map/all_to_all | solution.py:322
  109.4 7.0 %collective-permute-start.17 = (bf16[8,16,512]{2,1,0:T(8,128)(2,1)S(1)}, bf16[8,16,512]{2,1,0:T(8,128)(2,1)S(1)}, u32[]{:S(2)}, u32[]{:S(2)}) collective-permute-start(bf16[8,16,512]{2,1,0:T(8,128)(2,1)S(1)} %all_to_all.16.refs_0_), channel_id=1, source_target_pairs={{0,1},{1,2},{2,3},{3,0},{4,5},{5,6},{6,7},{7,4},{8,9},{9,10},{10,1... | collective-permute-start | bytes 393224 | tf_op jit(solution)/shard_map/ppermute | solution.py:61
  109.4 7.0 %collective-permute-start.18 = (bf16[8,16,512]{2,1,0:T(8,128)(2,1)S(1)}, bf16[8,16,512]{2,1,0:T(8,128)(2,1)S(1)}, u32[]{:S(2)}, u32[]{:S(2)}) collective-permute-start(bf16[8,16,512]{2,1,0:T(8,128)(2,1)S(1)} %all_to_all.16.refs_0_), channel_id=1, source_target_pairs={{0,2},{1,3},{2,0},{3,1},{4,6},{5,7},{6,4},{7,5},{8,10},{9,11},{10,... | collective-permute-start | bytes 393224 | tf_op jit(solution)/shard_map/ppermute | solution.py:61
  112.0 4.4 %collective-permute-start.19 = (bf16[8,16,512]{2,1,0:T(8,128)(2,1)S(1)}, bf16[8,16,512]{2,1,0:T(8,128)(2,1)S(1)}, u32[]{:S(2)}, u32[]{:S(2)}) collective-permute-start(bf16[8,16,512]{2,1,0:T(8,128)(2,1)S(1)} %all_to_all.16.refs_0_), channel_id=1, source_target_pairs={{0,3},{1,0},{2,1},{3,2},{4,7},{5,4},{6,5},{7,6},{8,11},{9,8},{10,9... | collective-permute-start | bytes 393224 | tf_op jit(solution)/shard_map/ppermute | solution.py:61
  112.0 4.3 %collective-permute-start.20 = (f32[16,512]{1,0:T(8,128)S(1)}, f32[16,512]{1,0:T(8,128)S(1)}, u32[]{:S(2)}, u32[]{:S(2)}) collective-permute-start(f32[16,512]{1,0:T(8,128)S(1)} %get-tuple-element.80), channel_id=1, source_target_pairs={{0,128},{128,0},{1,129},{129,1},{2,130},{130,2},{3,131},{131,3},{4... | collective-permute-start | bytes 98312 | tf_op jit(solution)/shard_map/ppermute | solution.py:42
  116.4 15.3 %collective-permute-start.21 = (bf16[4,8,16,512]{3,2,1,0:T(8,128)(2,1)S(1)}, bf16[4,8,16,512]{3,2,1,0:T(8,128)(2,1)S(1)}, u32[]{:S(2)}, u32[]{:S(2)}) collective-permute-start(bf16[4,8,16,512]{3,2,1,0:T(8,128)(2,1)S(1)} %shard_map.119.g0), channel_id=1, source_target_pairs={{0,32},{1,33},{2,34},{3,35},{4,36},{5,37},{6,38},{7,39},{8,40},{9,... | collective-permute-start | bytes 1572872 | tf_op jit(solution)/shard_map/ppermute | solution.py:61
  116.5 15.2 %collective-permute-start.22 = (bf16[4,8,16,512]{3,2,1,0:T(8,128)(2,1)S(1)}, bf16[4,8,16,512]{3,2,1,0:T(8,128)(2,1)}, u32[]{:S(2)}, u32[]{:S(2)}) collective-permute-start(bf16[4,8,16,512]{3,2,1,0:T(8,128)(2,1)S(1)} %shard_map.119.g0), channel_id=1, source_target_pairs={{0,128},{1,129},{2,130},{3,131},{4,132},{5,133},{6,134},{7,135},{8... | collective-permute-start | bytes 1572872 | tf_op jit(solution)/shard_map/ppermute | solution.py:61
  118.5 13.9 %collective-permute-start.23 = (bf16[4,8,16,512]{3,2,1,0:T(8,128)(2,1)S(1)}, bf16[4,8,16,512]{3,2,1,0:T(8,128)(2,1)}, u32[]{:S(2)}, u32[]{:S(2)}) collective-permute-start(bf16[4,8,16,512]{3,2,1,0:T(8,128)(2,1)S(1)} %shard_map.119.g0), channel_id=1, source_target_pairs={{0,160},{1,161},{2,162},{3,163},{4,164},{5,165},{6,166},{7,167},{8... | collective-permute-start | bytes 1572872 | tf_op jit(solution)/shard_map/ppermute | solution.py:61
  120.5 8.2 %collective-permute-start.24 = (f32[32,512]{1,0:T(8,128)S(1)}, f32[32,512]{1,0:T(8,128)S(1)}, u32[]{:S(2)}, u32[]{:S(2)}) collective-permute-start(f32[32,512]{1,0:T(8,128)S(1)} %maximum_select_fusion.3), channel_id=1, source_target_pairs={{0,64},{64,0},{1,65},{65,1},{2,66},{66,2},{3,67},{67,3},{4,68},{68... | collective-permute-start | bytes 196616 | tf_op jit(solution)/shard_map/ppermute | solution.py:38
  132.4 9.8 %copy-start = (bf16[512,2048]{1,0:T(8,128)(2,1)S(1)}, bf16[512,2048]{1,0:T(8,128)(2,1)}, u32[]{:S(2)}) copy-start(bf16[512,2048]{1,0:T(8,128)(2,1)} %get-tuple-element.51.mine_ref.x_ref) | copy-start | bytes 6291460
  136.0 7.7 %collective-permute-start.25 = (bf16[512,512]{1,0:T(8,128)(2,1)S(1)}, bf16[512,512]{1,0:T(8,128)(2,1)S(1)}, u32[]{:S(2)}, u32[]{:S(2)}) collective-permute-start(bf16[512,512]{1,0:T(8,128)(2,1)S(1)} %get-tuple-element.93), channel_id=1, source_target_pairs={{0,64},{64,0},{1,65},{65,1},{2,66},{66,2},{3,67},{67,3},{4,68},{68... | collective-permute-start | bytes 1572872 | tf_op jit(solution)/shard_map/ppermute | solution.py:38

commit v5 on v4

--- a/solution.py
+++ b/solution.py
@@ -398,7 +398,7 @@
         scratch=[pltpu.VMEM((2, 256, feature), BF)],
         mib=14,
     )
-    *got, token_grad = lax.optimization_barrier((*got, token_grad))
+    *got, token_grad, owned_part = lax.optimization_barrier((*got, token_grad, part_of(weight)))
     p0, p1, p2, p3 = call(sum_outer_kernel, [(block_shape, BF, VMEM)] * 4, b0, *got)
     got = [shift(block, k, True) for block, k in ((p1, 1), (p3, 3), (p2, 2))]
     (part,) = call(sum_inner_kernel, [(block_shape, BF, VMEM)], p0, *got)
@@ -407,7 +407,7 @@
         adam_kernel(total_rows),
         [((half, feature), F32, VMEM), (block_shape, BF, VMEM)],
         got_z,
-        weight_part,
+        owned_part,
         first_part,
         second_part,
     )

time: 146 us -> 144 us (0.986)
  blocking collectives: 24.5 us -> 34.9 us
  waiting for transfers between devices: 23.6 us -> 15.9 us
  starting transfers between devices: 49.7 us -> 46.1 us
    all_to_all x2 -> x3, blocking collectives: 24.5 us -> 34.9 us  [over_z(): return lax.all_to_all(blocks, 'z', 0, 0, tiled=True)]
    all_to_all x1 -> x0, waiting for transfers between devices: 7.01 us -> none  [over_z(): return lax.all_to_all(blocks, 'z', 0, 0, tiled=True)]
    all_to_all x1 -> x0, starting transfers between devices: 3.5 us -> none  [over_z(): return lax.all_to_all(blocks, 'z', 0, 0, tiled=True)]
  transfers between devices with their start and end apart: 27 -> 26, of which waited for: 13 -> 12; matrix products, arithmetic and copies ran while one was open for 6% -> 6% of each run, Pallas kernels for 14% -> 14%
where the time goes in v5:
time: 144 us; the launch traced here: 143 us
  starting transfers between devices  46.1 us (32%)
  blocking collectives  34.9 us (24%)
  Pallas kernels  33.5 us (23%)
  waiting for transfers between devices  15.9 us (11%)
  local copies, waits for them, and re-layouts  8.08 us (6%)
  other arithmetic  4 us (3%)
    all_to_all x3, blocking collectives, over_z(): return lax.all_to_all(blocks, 'z', 0, 0, tiled=True)  34.9 us
    pallas_call x11, Pallas kernels, call(): pl.pallas_call(kernel, out_shape=[pltpu.HBM(shape, dtype) if where == ANY...  33.5 us
    ppermute x7, starting transfers between devices, swap(): return lax.ppermute(value, 'core', [(0, 1), (1, 0)])  24.2 us
    ppermute x18, starting transfers between devices, shift(): return lax.ppermute(value, AXES, pairs)  19.5 us
    ppermute x18, waiting for transfers between devices, shift(): return lax.ppermute(value, AXES, pairs)  11.9 us
  transfers between devices with their start and end apart: 26, of which 12 were waited for; matrix products, arithmetic and copies ran while one was open for 6% of the time, Pallas kernels for 14%

profile of v5, /device:TPU:1, one launch (start us, length us, event | category | flops | bytes accessed | tf_op | source)
XLA Modules:
  0.0 143.3 jit_solution(3205054377071009584)
XLA Ops:
  0.6 3.3 %collective-permute-start.7 = (bf16[768,2048]{1,0:T(8,128)(2,1)}, bf16[768,2048]{1,0:T(8,128)(2,1)}, u32[]{:S(2)}, u32[]{:S(2)}) collective-permute-start(bf16[768,2048]{1,0:T(8,128)(2,1)} %tokens_ref.1), channel_id=1, source_target_pairs={{0,64},{64,0},{1,65},{65,1},{2,66},{66,2},{3,67},{67,3},{4,68},{68... | collective-permute-start | bytes 9437192 | tf_op jit(solution)/shard_map/ppermute | solution.py:38
  4.1 0.8 fusion.7
  4.9 14.1 %all_to_all.15.refs_0_ = bf16[8,16,512]{2,1,0:T(8,128)(2,1)S(1)} all-to-all(bf16[8,16,512]{2,1,0:T(8,128)(2,1)S(1)} %broadcast_in_dim.5), channel_id=1, replica_groups=mesh['yh'=2,'core'=2,'yl'=2,'z'=8,'x'=4] {'z'}, dimensions={0} | all-to-all | bytes 262144 | tf_op jit(solution)/shard_map/all_to_all | solution.py:322
  19.0 1.3 collective-permute-start
  20.3 2.6 %collective-permute-start.1 = (bf16[8,16,512]{2,1,0:T(8,128)(2,1)S(1)}, bf16[8,16,512]{2,1,0:T(8,128)(2,1)S(1)}, u32[]{:S(2)}, u32[]{:S(2)}) collective-permute-start(bf16[8,16,512]{2,1,0:T(8,128)(2,1)S(1)} %all_to_all.15.refs_0_), channel_id=1, source_target_pairs={{0,2},{1,3},{2,0},{3,1},{4,6},{5,7},{6,4},{7,5},{8,10},{9,11},{10,... | collective-permute-start | bytes 393224 | tf_op jit(solution)/shard_map/ppermute | solution.py:61
  22.8 1.1 collective-permute-start.2
  23.9 0.8 dynamic-slice_bitcast_fusion.2
  24.7 2.9 %collective-permute-start.6 = (s32[2,512]{1,0:T(2,128)}, s32[2,512]{1,0:T(2,128)S(1)}, u32[]{:S(2)}, u32[]{:S(2)}) collective-permute-start(s32[2,512]{1,0:T(2,128)} %param.9), channel_id=1, source_target_pairs={{0,64},{64,0},{1,65},{65,1},{2,66},{66,2},{3,67},{67,3},{4,68},{68... | collective-permute-start | bytes 12296 | tf_op jit(solution)/shard_map/ppermute | solution.py:38
  27.6 0.8 dynamic-slice_bitcast_fusion.1
  28.9 1.9 %collective-permute-start.4 = (bf16[4,8,16,512]{3,2,1,0:T(8,128)(2,1)S(1)}, bf16[4,8,16,512]{3,2,1,0:T(8,128)(2,1)S(1)}, u32[]{:S(2)}, u32[]{:S(2)}) collective-permute-start(bf16[4,8,16,512]{3,2,1,0:T(8,128)(2,1)S(1)} %shard_map.111.g0), channel_id=1, source_target_pairs={{0,128},{1,129},{2,130},{3,131},{4,132},{5,133},{6,134},{7,135},{8... | collective-permute-start | bytes 1572872 | tf_op jit(solution)/shard_map/ppermute | solution.py:61
  30.8 1.2 collective-permute-start.5
  32.1 0.8 constant_dynamic-slice_fusion
  32.8 6.2 %shard_map.112 = (bf16[512,2048]{1,0:T(8,128)(2,1)}, bf16[4,4,8,16,512]{4,3,2,1,0:T(8,128)(2,1)}) custom-call(s32[3]{0:T(128)S(1)} %pad_add_fusion.1.spot_ref, s32[1,512]{1,0:T(1,128)S(1)} %get-tuple-element.99.route_ref, bf16[768,2048]{1,0:T(8,128)(2,1)} %tokens_ref.1), custom_call_target="tpu_custom_call" | custom-call | tf_op jit(solution)/shard_map/pallas_call | solution.py:88
  39.2 0.9 fusion.5
  40.1 6.2 %shard_map.113 = (bf16[512,2048]{1,0:T(8,128)(2,1)}, bf16[4,4,8,16,512]{4,3,2,1,0:T(8,128)(2,1)}) custom-call(s32[3]{0:T(128)S(1)} %pad_add_fusion.1.spot_ref, s32[1,512]{1,0:T(1,128)S(1)} %constant_dynamic-slice_fusion.1.route_ref, bf16[768,2048]{1,0:T(8,128)(2,1)} %collective-permute-done.7.tokens_ref), custom_call_target="tpu_custom_call" | custom-call | tf_op jit(solution)/shard_map/pallas_call | solution.py:88
  46.4 9.6 %shard_map.114 = (bf16[4,8,16,512]{3,2,1,0:T(8,128)(2,1)S(1)}, bf16[4,8,16,512]{3,2,1,0:T(8,128)(2,1)}, bf16[4,8,16,512]{3,2,1,0:T(8,128)(2,1)}, bf16[4,8,16,512...) custom-call(s32[3]{0:T(128)S(1)} %pad_add_fusion.1.spot_ref, ...), custom_call_target="tpu_custom_call" | custom-call | tf_op jit(solution)/shard_map/pallas_call | solution.py:88
  56.0 4.4 %collective-permute-start.13 = (bf16[2048,512]{1,0:T(8,128)(2,1)}, bf16[2048,512]{1,0:T(8,128)(2,1)S(1)}, u32[]{:S(2)}, u32[]{:S(2)}) collective-permute-start(bf16[2048,512]{1,0:T(8,128)(2,1)} %bitcast.34), channel_id=1, source_target_pairs={{0,64},{64,0},{1,65},{65,1},{2,66},{66,2},{3,67},{67,3},{4,68},{68... | collective-permute-start | bytes 6291464 | tf_op jit(solution)/shard_map/ppermute | solution.py:38
  60.4 2.4 %collective-permute-start.10 = (bf16[4,8,16,512]{3,2,1,0:T(8,128)(2,1)}, bf16[4,8,16,512]{3,2,1,0:T(8,128)(2,1)S(1)}, u32[]{:S(2)}, u32[]{:S(2)}) collective-permute-start(bf16[4,8,16,512]{3,2,1,0:T(8,128)(2,1)} %get-tuple-element.62), channel_id=1, source_target_pairs={{0,160},{1,161},{2,162},{3,163},{4,164},{5,165},{6,166},{7,167},{8... | collective-permute-start | bytes 1572872 | tf_op jit(solution)/shard_map/ppermute | solution.py:61
  62.8 0.4 collective-permute-start.11
  63.4 0.8 dynamic-slice_bitcast_fusion.weight_ref
  64.2 0.9 collective-permute-done.12.dother_ref
  65.1 1.6 %copy-done.2 = bf16[2,8,4,2,16,512]{5,4,3,2,1,0:T(8,128)(2,1)S(1)} copy-done((bf16[2,8,4,2,16,512]{5,4,3,2,1,0:T(8,128)(2,1)S(1)}, bf16[2,8,4,2,16,512]{5,4,3,2,1,0:T(8,128)(2,1)}, u32[]{:S(2)}) %copy-start.2) | copy-done | bytes 2097176
  66.7 1.0 copy-done.3
  67.7 6.2 %shard_map.115 = bf16[768,2048]{1,0:T(8,128)(2,1)} custom-call(s32[2,512]{1,0:T(2,128)S(1)} %pad_add_fusion.routes_ref, bf16[512,512]{1,0:T(8,128)(2,1)S(1)} %copy-done.3, bf16[512,512]{1,0:T(8,128)(2,1)S(1)} %collective-permute-done.12.dother_ref, bf16[2048,512]{1,0:T(8,128)(2,1)S(1)} %bitcast.35, bf16[2048,512]{1,0:T(8,128)(2,1)S(1)} %collective-permute-done.13.other_ref), custom_call_target="tpu_custom_call" | custom-call | tf_op jit(solution)/shard_map/pallas_call | solution.py:88
  73.9 1.0 collective-permute-done.10.c
  74.9 3.3 %collective-permute-done.9.b = bf16[4,8,16,512]{3,2,1,0:T(8,128)(2,1)S(1)} collective-permute-done((bf16[4,8,16,512]{3,2,1,0:T(8,128)(2,1)}, bf16[4,8,16,512]{3,2,1,0:T(8,128)(2,1)S(1)}, u32[]{:S(2)}, u32[]{:S(2)}) %collective-permute-start.9) | collective-permute-done | bytes 524320 | tf_op jit(solution)/shard_map/ppermute | solution.py:61
  78.4 0.5 collective-permute-start.14
  78.9 2.3 %collective-permute-start.15 = (bf16[8,16,512]{2,1,0:T(8,128)(2,1)S(1)}, bf16[8,16,512]{2,1,0:T(8,128)(2,1)S(1)}, u32[]{:S(2)}, u32[]{:S(2)}) collective-permute-start(bf16[8,16,512]{2,1,0:T(8,128)(2,1)S(1)} %get-tuple-element.74), channel_id=1, source_target_pairs={{0,3},{1,0},{2,1},{3,2},{4,7},{5,4},{6,5},{7,6},{8,11},{9,8},{10,9... | collective-permute-start | bytes 393224 | tf_op jit(solution)/shard_map/ppermute | solution.py:61
  81.2 2.3 %collective-permute-done.14.b = bf16[8,16,512]{2,1,0:T(8,128)(2,1)S(1)} collective-permute-done((bf16[8,16,512]{2,1,0:T(8,128)(2,1)S(1)}, bf16[8,16,512]{2,1,0:T(8,128)(2,1)S(1)}, u32[]{:S(2)}, u32[]{:S(2)}) %collective-permute-start.14) | collective-permute-done | bytes 131104 | tf_op jit(solution)/shard_map/ppermute | solution.py:61
  83.5 1.0 collective-permute-done.15.c
  84.5 2.3 %collective-permute-done.16.d = bf16[8,16,512]{2,1,0:T(8,128)(2,1)S(1)} collective-permute-done((bf16[8,16,512]{2,1,0:T(8,128)(2,1)S(1)}, bf16[8,16,512]{2,1,0:T(8,128)(2,1)S(1)}, u32[]{:S(2)}, u32[]{:S(2)}) %collective-permute-start.16) | collective-permute-done | bytes 131104 | tf_op jit(solution)/shard_map/ppermute | solution.py:61
  86.9 10.4 %all_to_all.16.got_ref = bf16[8,16,512]{2,1,0:T(8,128)(2,1)S(1)} all-to-all(bf16[8,16,512]{2,1,0:T(8,128)(2,1)S(1)} %shard_map.117), channel_id=1, replica_groups=mesh['yh'=2,'core'=2,'yl'=2,'z'=8,'x'=4] {'z'}, dimensions={0} | all-to-all | bytes 262144 | tf_op jit(solution)/shard_map/all_to_all | solution.py:322
  97.4 10.4 %all_to_all.17.refs_0_ = bf16[8,16,512]{2,1,0:T(8,128)(2,1)S(1)} all-to-all(bf16[8,16,512]{2,1,0:T(8,128)(2,1)S(1)} %get-tuple-element.79), channel_id=1, replica_groups=mesh['yh'=2,'core'=2,'yl'=2,'z'=8,'x'=4] {'z'}, dimensions={0} | all-to-all | bytes 262144 | tf_op jit(solution)/shard_map/all_to_all | solution.py:322
  107.8 2.7 %collective-permute-start.18 = (bf16[8,16,512]{2,1,0:T(8,128)(2,1)S(1)}, bf16[8,16,512]{2,1,0:T(8,128)(2,1)S(1)}, u32[]{:S(2)}, u32[]{:S(2)}) collective-permute-start(bf16[8,16,512]{2,1,0:T(8,128)(2,1)S(1)} %all_to_all.17.refs_0_), channel_id=1, source_target_pairs={{0,2},{1,3},{2,0},{3,1},{4,6},{5,7},{6,4},{7,5},{8,10},{9,11},{10,... | collective-permute-start | bytes 393224 | tf_op jit(solution)/shard_map/ppermute | solution.py:61
  110.5 2.4 %collective-permute-start.20 = (f32[16,512]{1,0:T(8,128)S(1)}, f32[16,512]{1,0:T(8,128)S(1)}, u32[]{:S(2)}, u32[]{:S(2)}) collective-permute-start(f32[16,512]{1,0:T(8,128)S(1)} %get-tuple-element.82), channel_id=1, source_target_pairs={{0,128},{128,0},{1,129},{129,1},{2,130},{130,2},{3,131},{131,3},{4... | collective-permute-start | bytes 98312 | tf_op jit(solution)/shard_map/ppermute | solution.py:42
  112.9 1.9 %collective-permute-done.20 = f32[16,512]{1,0:T(8,128)S(1)} collective-permute-done((f32[16,512]{1,0:T(8,128)S(1)}, f32[16,512]{1,0:T(8,128)S(1)}, u32[]{:S(2)}, u32[]{:S(2)}) %collective-permute-start.20) | collective-permute-done | bytes 32800 | tf_op jit(solution)/shard_map/ppermute | solution.py:42
  115.0 1.9 %collective-permute-start.22 = (bf16[4,8,16,512]{3,2,1,0:T(8,128)(2,1)S(1)}, bf16[4,8,16,512]{3,2,1,0:T(8,128)(2,1)}, u32[]{:S(2)}, u32[]{:S(2)}) collective-permute-start(bf16[4,8,16,512]{3,2,1,0:T(8,128)(2,1)S(1)} %shard_map.119.g0), channel_id=1, source_target_pairs={{0,128},{1,129},{2,130},{3,131},{4,132},{5,133},{6,134},{7,135},{8... | collective-permute-start | bytes 1572872 | tf_op jit(solution)/shard_map/ppermute | solution.py:61
  116.9 0.7 collective-permute-start.23
  118.2 0.7 mul.130
  118.9 7.3 %collective-permute-start.24 = (f32[32,512]{1,0:T(8,128)S(1)}, f32[32,512]{1,0:T(8,128)S(1)}, u32[]{:S(2)}, u32[]{:S(2)}) collective-permute-start(f32[32,512]{1,0:T(8,128)S(1)} %maximum_select_fusion.3), channel_id=1, source_target_pairs={{0,64},{64,0},{1,65},{65,1},{2,66},{66,2},{3,67},{67,3},{4,68},{68... | collective-permute-start | bytes 196616 | tf_op jit(solution)/shard_map/ppermute | solution.py:38
  126.2 0.9 collective-permute-done.24
  127.1 1.9 %multiply_subtract_fusion = (f32[2,32,512]{2,1,0:T(8,128)}, f32[2,32,512]{2,1,0:T(8,128)}) fusion(f32[2,32,512]{2,1,0:T(8,128)} %param.11, f32[2,32,512]{2,1,0:T(8,128)} %mul.130, s32[2,32,512]{2,1,0:T(8,128)} %param.14, f32[1,32,512]{2,1,0:T(8,128)S(1)} %maximum_select_fusion.2, f32[1,32,512]{2,1,0:T(8,128)S(1)} %bitcast.41, pred[]{:T(512)S(6)} %eq.4, ...), kind=kLoop, calls=%fused_computation.8 | loop fusion | flops 655360 | bytes 1048577 | tf_op jit(solution)/shard_map/sub | solution.py:34
  129.0 1.2 collective-permute-done.21.g1
  130.2 0.6 collective-permute-done.23.g3
  130.9 3.6 %shard_map.120 = (bf16[512,512]{1,0:T(8,128)(2,1)S(1)}, bf16[2,8,4,2,16,512]{5,4,3,2,1,0:T(8,128)(2,1)S(1)}) custom-call(s32[3]{0:T(128)S(1)} %pad_add_fusion.1.spot_ref, bf16[512,2048]{1,0:T(8,128)(2,1)S(1)} %copy-done.1, bf16[4,8,16,512]{3,2,1,0:T(8,128)(2,1)S(1)} %shard_map.119.g0, bf16[4,8,16,512]{3,2,1,0:T(8,128)(2,1)S(1)} %collective-permute-done.21.g1, ...), custom_call_target="tpu_custom_call" | custom-call | tf_op jit(solution)/shard_map/pallas_call | solution.py:88
  134.5 6.2 %collective-permute-start.25 = (bf16[512,512]{1,0:T(8,128)(2,1)S(1)}, bf16[512,512]{1,0:T(8,128)(2,1)S(1)}, u32[]{:S(2)}, u32[]{:S(2)}) collective-permute-start(bf16[512,512]{1,0:T(8,128)(2,1)S(1)} %get-tuple-element.95), channel_id=1, source_target_pairs={{0,64},{64,0},{1,65},{65,1},{2,66},{66,2},{3,67},{67,3},{4,68},{68... | collective-permute-start | bytes 1572872 | tf_op jit(solution)/shard_map/ppermute | solution.py:38
  140.6 1.2 shard_map.121
  142.2 1.1 maximum_select_fusion
  (54 shorter events, 2.7 us)
Async XLA Ops:
  0.6 39.5 %collective-permute-start.7 = (bf16[768,2048]{1,0:T(8,128)(2,1)}, bf16[768,2048]{1,0:T(8,128)(2,1)}, u32[]{:S(2)}, u32[]{:S(2)}) collective-permute-start(bf16[768,2048]{1,0:T(8,128)(2,1)} %tokens_ref.1), channel_id=1, source_target_pairs={{0,64},{64,0},{1,65},{65,1},{2,66},{66,2},{3,67},{67,3},{4,68},{68... | collective-permute-start | bytes 9437192 | tf_op jit(solution)/shard_map/ppermute | solution.py:38
  4.0 42.4 %collective-permute-start.8 = (bf16[2,512,512]{2,1,0:T(8,128)(2,1)}, bf16[2,512,512]{2,1,0:T(8,128)(2,1)S(1)}, u32[]{:S(2)}, u32[]{:S(2)}) collective-permute-start(bf16[2,512,512]{2,1,0:T(8,128)(2,1)} %cot_mine_ref.1), channel_id=1, source_target_pairs={{0,64},{64,0},{1,65},{65,1},{2,66},{66,2},{3,67},{67,3},{4,68},{68... | collective-permute-start | bytes 3145736 | tf_op jit(solution)/shard_map/ppermute | solution.py:38
  19.0 5.7 %collective-permute-start = (bf16[8,16,512]{2,1,0:T(8,128)(2,1)S(1)}, bf16[8,16,512]{2,1,0:T(8,128)(2,1)S(1)}, u32[]{:S(2)}, u32[]{:S(2)}) collective-permute-start(bf16[8,16,512]{2,1,0:T(8,128)(2,1)S(1)} %all_to_all.15.refs_0_), channel_id=1, source_target_pairs={{0,1},{1,2},{2,3},{3,0},{4,5},{5,6},{6,7},{7,4},{8,9},{9,10},{10,1... | collective-permute-start | bytes 393224 | tf_op jit(solution)/shard_map/ppermute | solution.py:61
  20.3 8.2 %collective-permute-start.1 = (bf16[8,16,512]{2,1,0:T(8,128)(2,1)S(1)}, bf16[8,16,512]{2,1,0:T(8,128)(2,1)S(1)}, u32[]{:S(2)}, u32[]{:S(2)}) collective-permute-start(bf16[8,16,512]{2,1,0:T(8,128)(2,1)S(1)} %all_to_all.15.refs_0_), channel_id=1, source_target_pairs={{0,2},{1,3},{2,0},{3,1},{4,6},{5,7},{6,4},{7,5},{8,10},{9,11},{10,... | collective-permute-start | bytes 393224 | tf_op jit(solution)/shard_map/ppermute | solution.py:61
  22.8 5.6 %collective-permute-start.2 = (bf16[8,16,512]{2,1,0:T(8,128)(2,1)S(1)}, bf16[8,16,512]{2,1,0:T(8,128)(2,1)S(1)}, u32[]{:S(2)}, u32[]{:S(2)}) collective-permute-start(bf16[8,16,512]{2,1,0:T(8,128)(2,1)S(1)} %all_to_all.15.refs_0_), channel_id=1, source_target_pairs={{0,3},{1,0},{2,1},{3,2},{4,7},{5,4},{6,5},{7,6},{8,11},{9,8},{10,9... | collective-permute-start | bytes 393224 | tf_op jit(solution)/shard_map/ppermute | solution.py:61
  24.7 6.2 %collective-permute-start.6 = (s32[2,512]{1,0:T(2,128)}, s32[2,512]{1,0:T(2,128)S(1)}, u32[]{:S(2)}, u32[]{:S(2)}) collective-permute-start(s32[2,512]{1,0:T(2,128)} %param.9), channel_id=1, source_target_pairs={{0,64},{64,0},{1,65},{65,1},{2,66},{66,2},{3,67},{67,3},{4,68},{68... | collective-permute-start | bytes 12296 | tf_op jit(solution)/shard_map/ppermute | solution.py:38
  28.5 17.8 %collective-permute-start.3 = (bf16[4,8,16,512]{3,2,1,0:T(8,128)(2,1)S(1)}, bf16[4,8,16,512]{3,2,1,0:T(8,128)(2,1)S(1)}, u32[]{:S(2)}, u32[]{:S(2)}) collective-permute-start(bf16[4,8,16,512]{3,2,1,0:T(8,128)(2,1)S(1)} %shard_map.111.g0), channel_id=1, source_target_pairs={{0,32},{1,33},{2,34},{3,35},{4,36},{5,37},{6,38},{7,39},{8,40},{9,... | collective-permute-start | bytes 1572872 | tf_op jit(solution)/shard_map/ppermute | solution.py:61
  28.9 17.4 %collective-permute-start.4 = (bf16[4,8,16,512]{3,2,1,0:T(8,128)(2,1)S(1)}, bf16[4,8,16,512]{3,2,1,0:T(8,128)(2,1)S(1)}, u32[]{:S(2)}, u32[]{:S(2)}) collective-permute-start(bf16[4,8,16,512]{3,2,1,0:T(8,128)(2,1)S(1)} %shard_map.111.g0), channel_id=1, source_target_pairs={{0,128},{1,129},{2,130},{3,131},{4,132},{5,133},{6,134},{7,135},{8... | collective-permute-start | bytes 1572872 | tf_op jit(solution)/shard_map/ppermute | solution.py:61
  30.8 15.5 %collective-permute-start.5 = (bf16[4,8,16,512]{3,2,1,0:T(8,128)(2,1)S(1)}, bf16[4,8,16,512]{3,2,1,0:T(8,128)(2,1)S(1)}, u32[]{:S(2)}, u32[]{:S(2)}) collective-permute-start(bf16[4,8,16,512]{3,2,1,0:T(8,128)(2,1)S(1)} %shard_map.111.g0), channel_id=1, source_target_pairs={{0,160},{1,161},{2,162},{3,163},{4,164},{5,165},{6,166},{7,167},{8... | collective-permute-start | bytes 1572872 | tf_op jit(solution)/shard_map/ppermute | solution.py:61
  56.0 9.1 %collective-permute-start.13 = (bf16[2048,512]{1,0:T(8,128)(2,1)}, bf16[2048,512]{1,0:T(8,128)(2,1)S(1)}, u32[]{:S(2)}, u32[]{:S(2)}) collective-permute-start(bf16[2048,512]{1,0:T(8,128)(2,1)} %bitcast.34), channel_id=1, source_target_pairs={{0,64},{64,0},{1,65},{65,1},{2,66},{66,2},{3,67},{67,3},{4,68},{68... | collective-permute-start | bytes 6291464 | tf_op jit(solution)/shard_map/ppermute | solution.py:38
  60.3 4.7 %collective-permute-start.12 = (bf16[512,512]{1,0:T(8,128)(2,1)}, bf16[512,512]{1,0:T(8,128)(2,1)S(1)}, u32[]{:S(2)}, u32[]{:S(2)}) collective-permute-start(bf16[512,512]{1,0:T(8,128)(2,1)} %get-tuple-element.65), channel_id=1, source_target_pairs={{0,64},{64,0},{1,65},{65,1},{2,66},{66,2},{3,67},{67,3},{4,68},{68... | collective-permute-start | bytes 1572872 | tf_op jit(solution)/shard_map/ppermute | solution.py:38
  60.4 14.5 %collective-permute-start.10 = (bf16[4,8,16,512]{3,2,1,0:T(8,128)(2,1)}, bf16[4,8,16,512]{3,2,1,0:T(8,128)(2,1)S(1)}, u32[]{:S(2)}, u32[]{:S(2)}) collective-permute-start(bf16[4,8,16,512]{3,2,1,0:T(8,128)(2,1)} %get-tuple-element.62), channel_id=1, source_target_pairs={{0,160},{1,161},{2,162},{3,163},{4,164},{5,165},{6,166},{7,167},{8... | collective-permute-start | bytes 1572872 | tf_op jit(solution)/shard_map/ppermute | solution.py:61
  62.8 12.1 %collective-permute-start.11 = (bf16[4,8,16,512]{3,2,1,0:T(8,128)(2,1)}, bf16[4,8,16,512]{3,2,1,0:T(8,128)(2,1)S(1)}, u32[]{:S(2)}, u32[]{:S(2)}) collective-permute-start(bf16[4,8,16,512]{3,2,1,0:T(8,128)(2,1)} %get-tuple-element.63), channel_id=1, source_target_pairs={{0,128},{1,129},{2,130},{3,131},{4,132},{5,133},{6,134},{7,135},{8... | collective-permute-start | bytes 1572872 | tf_op jit(solution)/shard_map/ppermute | solution.py:61
  63.2 14.9 %collective-permute-start.9 = (bf16[4,8,16,512]{3,2,1,0:T(8,128)(2,1)}, bf16[4,8,16,512]{3,2,1,0:T(8,128)(2,1)S(1)}, u32[]{:S(2)}, u32[]{:S(2)}) collective-permute-start(bf16[4,8,16,512]{3,2,1,0:T(8,128)(2,1)} %get-tuple-element.61), channel_id=1, source_target_pairs={{0,32},{1,33},{2,34},{3,35},{4,36},{5,37},{6,38},{7,39},{8,40},{9,... | collective-permute-start | bytes 1572872 | tf_op jit(solution)/shard_map/ppermute | solution.py:61
  65.1 1.6 %copy-start.2 = (bf16[2,8,4,2,16,512]{5,4,3,2,1,0:T(8,128)(2,1)S(1)}, bf16[2,8,4,2,16,512]{5,4,3,2,1,0:T(8,128)(2,1)}, u32[]{:S(2)}) copy-start(bf16[2,8,4,2,16,512]{5,4,3,2,1,0:T(8,128)(2,1)} %get-tuple-element.66) | copy-start | bytes 6291460
  66.7 1.0 copy-start.3
  78.2 39.5 %copy-start.4 = (f32[2,32,4]{1,2,0:T(4,128)S(1)}, f32[2,32,4]{1,2,0:T(4,128)}, u32[]{:S(2)}) copy-start(f32[2,32,4]{1,2,0:T(4,128)} %param.13) | copy-start | bytes 3076
  78.2 39.6 %copy-start.5 = (f32[2,32,4]{1,2,0:T(4,128)S(1)}, f32[2,32,4]{1,2,0:T(4,128)}, u32[]{:S(2)}) copy-start(f32[2,32,4]{1,2,0:T(4,128)} %param.15) | copy-start | bytes 3076
  78.4 5.1 %collective-permute-start.14 = (bf16[8,16,512]{2,1,0:T(8,128)(2,1)S(1)}, bf16[8,16,512]{2,1,0:T(8,128)(2,1)S(1)}, u32[]{:S(2)}, u32[]{:S(2)}) collective-permute-start(bf16[8,16,512]{2,1,0:T(8,128)(2,1)S(1)} %get-tuple-element.73), channel_id=1, source_target_pairs={{0,1},{1,2},{2,3},{3,0},{4,5},{5,6},{6,7},{7,4},{8,9},{9,10},{10,1... | collective-permute-start | bytes 393224 | tf_op jit(solution)/shard_map/ppermute | solution.py:61
  78.9 5.6 %collective-permute-start.15 = (bf16[8,16,512]{2,1,0:T(8,128)(2,1)S(1)}, bf16[8,16,512]{2,1,0:T(8,128)(2,1)S(1)}, u32[]{:S(2)}, u32[]{:S(2)}) collective-permute-start(bf16[8,16,512]{2,1,0:T(8,128)(2,1)S(1)} %get-tuple-element.74), channel_id=1, source_target_pairs={{0,3},{1,0},{2,1},{3,2},{4,7},{5,4},{6,5},{7,6},{8,11},{9,8},{10,9... | collective-permute-start | bytes 393224 | tf_op jit(solution)/shard_map/ppermute | solution.py:61
  81.2 5.6 %collective-permute-start.16 = (bf16[8,16,512]{2,1,0:T(8,128)(2,1)S(1)}, bf16[8,16,512]{2,1,0:T(8,128)(2,1)S(1)}, u32[]{:S(2)}, u32[]{:S(2)}) collective-permute-start(bf16[8,16,512]{2,1,0:T(8,128)(2,1)S(1)} %get-tuple-element.75), channel_id=1, source_target_pairs={{0,2},{1,3},{2,0},{3,1},{4,6},{5,7},{6,4},{7,5},{8,10},{9,11},{10,... | collective-permute-start | bytes 393224 | tf_op jit(solution)/shard_map/ppermute | solution.py:61
  86.9 44.0 %copy-start.1 = (bf16[512,2048]{1,0:T(8,128)(2,1)S(1)}, bf16[512,2048]{1,0:T(8,128)(2,1)}, u32[]{:S(2)}) copy-start(bf16[512,2048]{1,0:T(8,128)(2,1)} %get-tuple-element.53.other_ref.x_ref) | copy-start | bytes 6291460
  107.8 7.0 %collective-permute-start.17 = (bf16[8,16,512]{2,1,0:T(8,128)(2,1)S(1)}, bf16[8,16,512]{2,1,0:T(8,128)(2,1)S(1)}, u32[]{:S(2)}, u32[]{:S(2)}) collective-permute-start(bf16[8,16,512]{2,1,0:T(8,128)(2,1)S(1)} %all_to_all.17.refs_0_), channel_id=1, source_target_pairs={{0,1},{1,2},{2,3},{3,0},{4,5},{5,6},{6,7},{7,4},{8,9},{9,10},{10,1... | collective-permute-start | bytes 393224 | tf_op jit(solution)/shard_map/ppermute | solution.py:61
  107.8 7.0 %collective-permute-start.18 = (bf16[8,16,512]{2,1,0:T(8,128)(2,1)S(1)}, bf16[8,16,512]{2,1,0:T(8,128)(2,1)S(1)}, u32[]{:S(2)}, u32[]{:S(2)}) collective-permute-start(bf16[8,16,512]{2,1,0:T(8,128)(2,1)S(1)} %all_to_all.17.refs_0_), channel_id=1, source_target_pairs={{0,2},{1,3},{2,0},{3,1},{4,6},{5,7},{6,4},{7,5},{8,10},{9,11},{10,... | collective-permute-start | bytes 393224 | tf_op jit(solution)/shard_map/ppermute | solution.py:61
  110.5 4.4 %collective-permute-start.19 = (bf16[8,16,512]{2,1,0:T(8,128)(2,1)S(1)}, bf16[8,16,512]{2,1,0:T(8,128)(2,1)S(1)}, u32[]{:S(2)}, u32[]{:S(2)}) collective-permute-start(bf16[8,16,512]{2,1,0:T(8,128)(2,1)S(1)} %all_to_all.17.refs_0_), channel_id=1, source_target_pairs={{0,3},{1,0},{2,1},{3,2},{4,7},{5,4},{6,5},{7,6},{8,11},{9,8},{10,9... | collective-permute-start | bytes 393224 | tf_op jit(solution)/shard_map/ppermute | solution.py:61
  110.5 4.3 %collective-permute-start.20 = (f32[16,512]{1,0:T(8,128)S(1)}, f32[16,512]{1,0:T(8,128)S(1)}, u32[]{:S(2)}, u32[]{:S(2)}) collective-permute-start(f32[16,512]{1,0:T(8,128)S(1)} %get-tuple-element.82), channel_id=1, source_target_pairs={{0,128},{128,0},{1,129},{129,1},{2,130},{130,2},{3,131},{131,3},{4... | collective-permute-start | bytes 98312 | tf_op jit(solution)/shard_map/ppermute | solution.py:42
  114.9 15.3 %collective-permute-start.21 = (bf16[4,8,16,512]{3,2,1,0:T(8,128)(2,1)S(1)}, bf16[4,8,16,512]{3,2,1,0:T(8,128)(2,1)S(1)}, u32[]{:S(2)}, u32[]{:S(2)}) collective-permute-start(bf16[4,8,16,512]{3,2,1,0:T(8,128)(2,1)S(1)} %shard_map.119.g0), channel_id=1, source_target_pairs={{0,32},{1,33},{2,34},{3,35},{4,36},{5,37},{6,38},{7,39},{8,40},{9,... | collective-permute-start | bytes 1572872 | tf_op jit(solution)/shard_map/ppermute | solution.py:61
  115.0 15.2 %collective-permute-start.22 = (bf16[4,8,16,512]{3,2,1,0:T(8,128)(2,1)S(1)}, bf16[4,8,16,512]{3,2,1,0:T(8,128)(2,1)}, u32[]{:S(2)}, u32[]{:S(2)}) collective-permute-start(bf16[4,8,16,512]{3,2,1,0:T(8,128)(2,1)S(1)} %shard_map.119.g0), channel_id=1, source_target_pairs={{0,128},{1,129},{2,130},{3,131},{4,132},{5,133},{6,134},{7,135},{8... | collective-permute-start | bytes 1572872 | tf_op jit(solution)/shard_map/ppermute | solution.py:61
  116.9 13.9 %collective-permute-start.23 = (bf16[4,8,16,512]{3,2,1,0:T(8,128)(2,1)S(1)}, bf16[4,8,16,512]{3,2,1,0:T(8,128)(2,1)}, u32[]{:S(2)}, u32[]{:S(2)}) collective-permute-start(bf16[4,8,16,512]{3,2,1,0:T(8,128)(2,1)S(1)} %shard_map.119.g0), channel_id=1, source_target_pairs={{0,160},{1,161},{2,162},{3,163},{4,164},{5,165},{6,166},{7,167},{8... | collective-permute-start | bytes 1572872 | tf_op jit(solution)/shard_map/ppermute | solution.py:61
  118.9 8.2 %collective-permute-start.24 = (f32[32,512]{1,0:T(8,128)S(1)}, f32[32,512]{1,0:T(8,128)S(1)}, u32[]{:S(2)}, u32[]{:S(2)}) collective-permute-start(f32[32,512]{1,0:T(8,128)S(1)} %maximum_select_fusion.3), channel_id=1, source_target_pairs={{0,64},{64,0},{1,65},{65,1},{2,66},{66,2},{3,67},{67,3},{4,68},{68... | collective-permute-start | bytes 196616 | tf_op jit(solution)/shard_map/ppermute | solution.py:38
  130.9 9.8 %copy-start = (bf16[512,2048]{1,0:T(8,128)(2,1)S(1)}, bf16[512,2048]{1,0:T(8,128)(2,1)}, u32[]{:S(2)}) copy-start(bf16[512,2048]{1,0:T(8,128)(2,1)} %get-tuple-element.52.mine_ref.x_ref) | copy-start | bytes 6291460
  134.5 7.7 %collective-permute-start.25 = (bf16[512,512]{1,0:T(8,128)(2,1)S(1)}, bf16[512,512]{1,0:T(8,128)(2,1)S(1)}, u32[]{:S(2)}, u32[]{:S(2)}) collective-permute-start(bf16[512,512]{1,0:T(8,128)(2,1)S(1)} %get-tuple-element.95), channel_id=1, source_target_pairs={{0,64},{64,0},{1,65},{65,1},{2,66},{66,2},{3,67},{67,3},{4,68},{68... | collective-permute-start | bytes 1572872 | tf_op jit(solution)/shard_map/ppermute | solution.py:38
